TPU v7x, 32 devices: a whole 2x2x4 slice. The times are simulated.
32 devices in a mesh: gx: 4 (over y, core), gy: 8 (over z, x).
Axes of the slice: x: 2, y: 2, z: 4, core: 2. Of those that a mesh axis runs over, the one named last changes fastest.
Arguments:
- source: float32 [128, 128, 128], P('gx', 'gy'), may hold values from -30 to 30
- permittivity: float32 [128, 128, 128], P('gx', 'gy'), may hold values from 2 to 80
- screening: float32 [128, 128, 128], P('gx', 'gy'), may hold values from 0 to 16
- potential: float32 [128, 128, 128], P('gx', 'gy'), may hold values from -3 to 3
- fixed_cell: int32 [128, 128, 128], P('gx', 'gy'), may hold values 0 or 1
Outputs:
- result: float32 [128, 128, 128], P('gx', 'gy')
All inputs are finite; a program needn't handle non-finite values. No bound on the sum of `fixed_cell` on one device may be relied on, other than what follows from the above.
Results may differ from a plain program's by a relative error of at most 0.0003.
Values sent between devices are 32-bit elements; how exact they have to be, the bound alone decides.
No kernel may reach another device: no remote copies, remote signals or barrier semaphores. Data moves between devices by JAX's collectives and lax.ppermute only.
A program may use at most 128 MiB of HBM per device.

v0:
```python
import jax
import jax.numpy as jnp
from jax import lax
from jax.sharding import PartitionSpec as P


def padded_2(block, sides, width):
    for axis, dim in sides:
        count = lax.axis_size(axis)
        forward = [(i, i + 1) for i in range(count - 1)]
        backward = [(target, source) for source, target in forward]
        low = lax.ppermute(
            lax.slice_in_dim(block, block.shape[dim] - width, None, axis=dim), axis, forward
        )
        high = lax.ppermute(lax.slice_in_dim(block, 0, width, axis=dim), axis, backward)
        block = jnp.concatenate([low, block, high], axis=dim)
    return block


def neighbours(padded):
    inner = padded[1:-1, 1:-1]
    depth = jnp.pad(inner, ((0, 0), (0, 0), (1, 1)))
    return jnp.stack(
        [
            padded[2:, 1:-1],
            padded[:-2, 1:-1],
            padded[1:-1, 2:],
            padded[1:-1, :-2],
            depth[:, :, 2:],
            depth[:, :, :-2],
        ]
    )


def position(shape, start_x, start_y):
    first = lax.broadcasted_iota(jnp.int32, shape, 0) + start_x
    second = lax.broadcasted_iota(jnp.int32, shape, 1) + start_y
    third = lax.broadcasted_iota(jnp.int32, shape, 2)
    return (first, second, third)


def parity_at(shape, start_x, start_y):
    first, second, third = position(shape, start_x, start_y)
    return (first + second + third) % 2


def restrict(field):
    first, second, third = field.shape
    return field.reshape(first // 2, 2, second // 2, 2, third // 2, 2).mean(axis=(1, 3, 5))


def prolong(field):
    return jnp.repeat(jnp.repeat(jnp.repeat(field, 2, axis=0), 2, axis=1), 2, axis=2)


def fine_rim(stack):
    return padded_2(stack, (("gx", 1), ("gy", 2)), 1)


def mid_rim(stack):
    return padded_2(stack, (("gx", 1), ("gy", 2)), 1)


def low_rim(stack):
    return padded_2(stack, (("gx", 1), ("gy", 2)), 1)


def face_stack(padded):
    faces = 0.5 * (padded[1:-1, 1:-1][None] + neighbours(padded))
    return (faces, jnp.sum(faces, axis=0))


def fine_mapped(padded, faces, centre, screening, source):
    field = padded[1:-1, 1:-1]
    beside = jnp.sum(faces * neighbours(padded), axis=0)
    return centre * field - beside + screening * jnp.sinh(field) - source


def fine_half(padded, faces, centre, screening, source, mask):
    field = padded[1:-1, 1:-1]
    update = field - fine_mapped(padded, faces, centre, screening, source) / (
        centre + screening * jnp.cosh(field)
    )
    return jnp.where(mask, update, field)


def coarse_applied(padded, faces, centre, react, factor):
    field = padded[1:-1, 1:-1]
    beside = jnp.sum(faces * neighbours(padded), axis=0)
    return factor * (centre * field - beside) + react * field


def coarse_half(padded, faces, centre, react, rhs, factor, mask):
    field = padded[1:-1, 1:-1]
    applied = coarse_applied(padded, faces, centre, react, factor)
    update = field - (applied - rhs) / (factor * centre + react)
    return jnp.where(mask, update, field)


def coarse_terms(field, faces0, centre0, screening, source, free, permittivity):
    padded = fine_rim(field[None])[0]
    fine_residual = jnp.where(
        free, -fine_mapped(padded, faces0, centre0, screening, source), jnp.float32(0.0)
    )
    react = screening * jnp.cosh(field)
    perm1 = restrict(permittivity)
    react1 = restrict(react)
    rhs1 = restrict(fine_residual)
    return (perm1, react1, rhs1, restrict(perm1), restrict(react1))


def level_residual(err1, level):
    faces, centre, react, rhs, factor, parity = level
    applied = coarse_applied(mid_rim(err1[None])[0], faces, centre, react, factor)
    return restrict(rhs - applied)


def narrow_level(perm, react, rhs, factor, start_x, start_y, extend):
    faces, centre = face_stack(extend(perm[None])[0])
    parity = parity_at(perm.shape, start_x, start_y)
    return (faces, centre, react, rhs, factor, parity)


def narrow_sweeps(field, level, sweeps, from_zero, extend):
    faces, centre, react, rhs, factor, parity = level
    for sweep in range(sweeps):
        for colour in (0, 1):
            if from_zero and sweep == 0 and (colour == 0):
                padded = jnp.pad(field, ((1, 1), (1, 1), (0, 0)))
            else:
                padded = extend(field[None])[0]
            field = coarse_half(padded, faces, centre, react, rhs, factor, parity == colour)
    return field


def body(source, permittivity, screening, potential, fixed_cell):
    rows_x = source.shape[0]
    rows_y = source.shape[1]
    index_x = lax.axis_index("gx")
    index_y = lax.axis_index("gy")
    free = fixed_cell == 0
    start_x = index_x * rows_x
    start_y = index_y * rows_y
    parity0 = parity_at(source.shape, start_x, start_y)
    mask_even = free & (parity0 == 0)
    mask_odd = free & (parity0 == 1)
    half_x = rows_x // 2
    half_y = rows_y // 2
    quarter_x = rows_x // 4
    quarter_y = rows_y // 4
    both = fine_rim(jnp.stack([permittivity, potential]))
    faces0, centre0 = face_stack(both[0])
    field = fine_half(both[1], faces0, centre0, screening, source, mask_even)
    field = fine_half(fine_rim(field[None])[0], faces0, centre0, screening, source, mask_odd)
    perm1, react1, rhs1, perm2, react2 = coarse_terms(
        field, faces0, centre0, screening, source, free, permittivity
    )
    level1 = narrow_level(perm1, react1, rhs1, 0.25, index_x * half_x, index_y * half_y, mid_rim)
    err1 = narrow_sweeps(jnp.zeros_like(rhs1), level1, 2, True, mid_rim)
    rhs2 = level_residual(err1, level1)
    level2 = narrow_level(
        perm2, react2, rhs2, 0.0625, index_x * quarter_x, index_y * quarter_y, low_rim
    )
    err2 = narrow_sweeps(jnp.zeros_like(rhs2), level2, 4, True, low_rim)
    err1 = narrow_sweeps(err1 + prolong(err2), level1, 2, False, mid_rim)
    field = jnp.where(free, field + prolong(err1), field)
    field = fine_half(fine_rim(field[None])[0], faces0, centre0, screening, source, mask_even)
    result = fine_half(fine_rim(field[None])[0], faces0, centre0, screening, source, mask_odd)
    return result


def solution(mesh):
    placed = (
        P("gx", "gy", None),
        P("gx", "gy", None),
        P("gx", "gy", None),
        P("gx", "gy", None),
        P("gx", "gy", None),
    )
    return jax.shard_map(
        body, mesh=mesh, in_specs=placed, out_specs=P("gx", "gy", None), check_vma=False
    )
```

profile of v0, /device:TPU:1, one launch (start us, length us, event | category | flops | bytes accessed | tf_op | source)
XLA Modules:
  0.0 494.2 jit_solution(9816493529234652694)
XLA Ops:
  0.8 4.5 collective-permute-start
  7.2 18.8 %reshape.291 = f32[16,2,8,2,64,2]{5,4,3,2,1,0:T(8,128)} reshape(f32[32,16,128]{2,1,0:T(8,128)} %param.6) | data formatting | bytes 524288 | tf_op jit(solution)/shard_map/reshape | solution.py:49
  26.0 7.0 %reduce_sum.282 = f32[16,8,64]{2,1,0:T(8,128)S(1)} reduce(f32[16,2,8,2,64,2]{5,4,3,2,1,0:T(8,128)} %reshape.291, f32[]{:T(128)} %constant.78.clone.1), dimensions={1,3,5}, to_apply=%region_3.4 | reduce | flops 57344 | bytes 294916 | tf_op jit(solution)/shard_map/reduce_sum | solution.py:49
  33.1 3.6 collective-permute-start.8
  41.1 3.8 collective-permute-start.28
  53.1 4.6 collective-permute-start.30
  59.2 4.2 collective-permute-start.2
  64.7 4.4 collective-permute-done.3
  72.8 5.8 %collective-permute-start.4 = (f32[1,1,16,128]{3,2,1,0:T(8,128)S(1)}, f32[1,1,16,128]{3,2,1,0:T(8,128)S(1)}, u32[]{:S(2)}, u32[]{:S(2)}) collective-permute-start(f32[1,1,16,128]{3,2,1,0:T(8,128)S(1)} %get-tuple-element.60), channel_id=1, source_target_pairs={{0,8},{8,16},{16,24},{1,9},{9,17},{17,25},{2,10},{10,18},{18,26},{... | collective-permute-start | bytes 24584 | tf_op jit(solution)/shard_map/ppermute | solution.py:12
  83.7 4.5 collective-permute-start.6
  108.3 18.8 %reshape.292 = f32[16,2,8,2,64,2]{5,4,3,2,1,0:T(8,128)} reshape(f32[32,16,128]{2,1,0:T(8,128)} %get-tuple-element.11) | data formatting | bytes 524288 | tf_op jit(solution)/shard_map/reshape | solution.py:49
  127.2 7.0 %reduce_sum.285 = f32[16,8,64]{2,1,0:T(8,128)S(1)} reduce(f32[16,2,8,2,64,2]{5,4,3,2,1,0:T(8,128)} %reshape.292, f32[]{:T(128)} %constant.78.clone.1), dimensions={1,3,5}, to_apply=%region_6.7 | reduce | flops 57344 | bytes 294916 | tf_op jit(solution)/shard_map/reduce_sum | solution.py:49
  137.7 18.8 %reshape.293 = f32[16,2,8,2,64,2]{5,4,3,2,1,0:T(8,128)} reshape(f32[32,16,128]{2,1,0:T(8,128)} %negate_select_fusion.2) | data formatting | bytes 524288 | tf_op jit(solution)/shard_map/reshape | solution.py:49
  156.6 7.0 %reduce_sum.287 = f32[16,8,64]{2,1,0:T(8,128)S(1)} reduce(f32[16,2,8,2,64,2]{5,4,3,2,1,0:T(8,128)} %reshape.293, f32[]{:T(128)} %constant.78.clone.1), dimensions={1,3,5}, to_apply=%region_8.9 | reduce | flops 57344 | bytes 294916 | tf_op jit(solution)/shard_map/reduce_sum | solution.py:49
  170.9 4.3 collective-permute-start.18
  176.5 4.3 collective-permute-done.19
  189.5 4.5 collective-permute-start.22
  199.1 3.4 collective-permute-start.24
  223.5 4.5 collective-permute-start.34
  233.7 4.3 div.118
  239.8 4.3 reshape.294
  246.0 3.4 collective-permute-start.36
  266.1 3.4 collective-permute-start.40
  286.3 3.4 collective-permute-start.44
  306.4 3.4 collective-permute-start.48
  326.5 3.4 collective-permute-start.52
  346.6 3.4 collective-permute-start.56
  366.7 3.4 collective-permute-start.60
  389.6 3.4 collective-permute-start.64
  405.6 3.4 collective-permute-start.68
  437.5 3.4 collective-permute-start.76
  458.3 3.4 collective-permute-start.80
  (536 shorter events, 311.6 us)
Async XLA Ops:
  0.8 58.3 %collective-permute-start = (f32[2,1,16,128]{3,2,1,0:T(8,128)S(1)}, f32[2,1,16,128]{3,2,1,0:T(8,128)S(1)}, u32[]{:S(2)}, u32[]{:S(2)}) collective-permute-start(f32[2,1,16,128]{3,2,1,0:T(8,128)S(1)} %get-tuple-element.19), channel_id=1, source_target_pairs={{0,8},{8,16},{16,24},{1,9},{9,17},{17,25},{2,10},{10,18},{18,26},{... | collective-permute-start | bytes 49160 | tf_op jit(solution)/shard_map/ppermute | solution.py:12
  5.3 53.8 %collective-permute-start.1 = (f32[2,1,16,128]{3,2,1,0:T(8,128)S(1)}, f32[2,1,16,128]{3,2,1,0:T(8,128)S(1)}, u32[]{:S(2)}, u32[]{:S(2)}) collective-permute-start(f32[2,1,16,128]{3,2,1,0:T(8,128)S(1)} %get-tuple-element.20), channel_id=1, source_target_pairs={{8,0},{16,8},{24,16},{9,1},{17,9},{25,17},{10,2},{18,10},{26,18},{... | collective-permute-start | bytes 49160 | tf_op jit(solution)/shard_map/ppermute | solution.py:15
  33.1 12.9 %collective-permute-start.8 = (f32[1,1,8,64]{3,2,1,0:T(8,128)S(1)}, f32[1,1,8,64]{3,2,1,0:T(8,128)S(1)}, u32[]{:S(2)}, u32[]{:S(2)}) collective-permute-start(f32[1,1,8,64]{3,2,1,0:T(8,128)S(1)} %get-tuple-element.149), channel_id=1, source_target_pairs={{0,8},{8,16},{16,24},{1,9},{9,17},{17,25},{2,10},{10,18},{18,26},{... | collective-permute-start | bytes 6152 | tf_op jit(solution)/shard_map/ppermute | solution.py:12
  36.7 11.2 %collective-permute-start.9 = (f32[1,1,8,64]{3,2,1,0:T(8,128)S(1)}, f32[1,1,8,64]{3,2,1,0:T(8,128)S(1)}, u32[]{:S(2)}, u32[]{:S(2)}) collective-permute-start(f32[1,1,8,64]{3,2,1,0:T(8,128)S(1)} %get-tuple-element.150), channel_id=1, source_target_pairs={{8,0},{16,8},{24,16},{9,1},{17,9},{25,17},{10,2},{18,10},{26,18},{... | collective-permute-start | bytes 6152 | tf_op jit(solution)/shard_map/ppermute | solution.py:15
  41.1 10.0 %collective-permute-start.28 = (f32[1,1,4,32]{3,2,1,0:T(4,128)S(1)}, f32[1,1,4,32]{3,2,1,0:T(4,128)S(1)}, u32[]{:S(2)}, u32[]{:S(2)}) collective-permute-start(f32[1,1,4,32]{3,2,1,0:T(4,128)S(1)} %get-tuple-element.181), channel_id=1, source_target_pairs={{0,8},{8,16},{16,24},{1,9},{9,17},{17,25},{2,10},{10,18},{18,26},{... | collective-permute-start | bytes 1544 | tf_op jit(solution)/shard_map/ppermute | solution.py:12
  46.0 6.4 %collective-permute-start.29 = (f32[1,1,4,32]{3,2,1,0:T(4,128)S(1)}, f32[1,1,4,32]{3,2,1,0:T(4,128)S(1)}, u32[]{:S(2)}, u32[]{:S(2)}) collective-permute-start(f32[1,1,4,32]{3,2,1,0:T(4,128)S(1)} %get-tuple-element.182), channel_id=1, source_target_pairs={{8,0},{16,8},{24,16},{9,1},{17,9},{25,17},{10,2},{18,10},{26,18},{... | collective-permute-start | bytes 1544 | tf_op jit(solution)/shard_map/ppermute | solution.py:15
  48.0 9.6 %collective-permute-start.10 = (f32[1,18,1,64]{3,1,2,0:T(8,128)S(1)}, f32[1,18,1,64]{3,1,2,0:T(8,128)S(1)}, u32[]{:S(2)}, u32[]{:S(2)}) collective-permute-start(f32[1,18,1,64]{3,1,2,0:T(8,128)S(1)} %get-tuple-element.125), channel_id=1, source_target_pairs={{0,1},{1,2},{2,3},{3,4},{4,5},{5,6},{6,7},{8,9},{9,10},{10,11},{11... | collective-permute-start | bytes 13832 | tf_op jit(solution)/shard_map/ppermute | solution.py:12
  51.1 7.8 %collective-permute-start.11 = (f32[1,18,1,64]{3,1,2,0:T(8,128)S(1)}, f32[1,18,1,64]{3,1,2,0:T(8,128)S(1)}, u32[]{:S(2)}, u32[]{:S(2)}) collective-permute-start(f32[1,18,1,64]{3,1,2,0:T(8,128)S(1)} %get-tuple-element.126), channel_id=1, source_target_pairs={{1,0},{2,1},{3,2},{4,3},{5,4},{6,5},{7,6},{9,8},{10,9},{11,10},{12... | collective-permute-start | bytes 13832 | tf_op jit(solution)/shard_map/ppermute | solution.py:15
  53.1 115.0 %collective-permute-start.30 = (f32[1,10,1,32]{3,2,1,0:T(1,128)}, f32[1,10,1,32]{3,2,1,0:T(1,128)}, u32[]{:S(2)}, u32[]{:S(2)}) collective-permute-start(f32[1,10,1,32]{3,2,1,0:T(1,128)} %get-tuple-element.165), channel_id=1, source_target_pairs={{0,1},{1,2},{2,3},{3,4},{4,5},{5,6},{6,7},{8,9},{9,10},{10,11},{11... | collective-permute-start | bytes 3848 | tf_op jit(solution)/shard_map/ppermute | solution.py:12
  57.6 110.4 %collective-permute-start.31 = (f32[1,10,1,32]{3,2,1,0:T(1,128)}, f32[1,10,1,32]{3,2,1,0:T(1,128)}, u32[]{:S(2)}, u32[]{:S(2)}) collective-permute-start(f32[1,10,1,32]{3,2,1,0:T(1,128)} %get-tuple-element.166), channel_id=1, source_target_pairs={{1,0},{2,1},{3,2},{4,3},{5,4},{6,5},{7,6},{9,8},{10,9},{11,10},{12... | collective-permute-start | bytes 3848 | tf_op jit(solution)/shard_map/ppermute | solution.py:15
  59.2 5.5 %collective-permute-start.2 = (f32[2,34,1,128]{3,2,1,0:T(1,128)S(1)}, f32[2,34,1,128]{3,2,1,0:T(1,128)S(1)}, u32[]{:S(2)}, u32[]{:S(2)}) collective-permute-start(f32[2,34,1,128]{3,2,1,0:T(1,128)S(1)} %get-tuple-element.17), channel_id=1, source_target_pairs={{0,1},{1,2},{2,3},{3,4},{4,5},{5,6},{6,7},{8,9},{9,10},{10,11},{11... | collective-permute-start | bytes 104456 | tf_op jit(solution)/shard_map/ppermute | solution.py:12
  63.3 5.7 %collective-permute-start.3 = (f32[2,34,1,128]{3,2,1,0:T(1,128)S(1)}, f32[2,34,1,128]{3,2,1,0:T(1,128)S(1)}, u32[]{:S(2)}, u32[]{:S(2)}) collective-permute-start(f32[2,34,1,128]{3,2,1,0:T(1,128)S(1)} %get-tuple-element.18), channel_id=1, source_target_pairs={{1,0},{2,1},{3,2},{4,3},{5,4},{6,5},{7,6},{9,8},{10,9},{11,10},{12... | collective-permute-start | bytes 104456 | tf_op jit(solution)/shard_map/ppermute | solution.py:15
  72.8 7.8 %collective-permute-start.4 = (f32[1,1,16,128]{3,2,1,0:T(8,128)S(1)}, f32[1,1,16,128]{3,2,1,0:T(8,128)S(1)}, u32[]{:S(2)}, u32[]{:S(2)}) collective-permute-start(f32[1,1,16,128]{3,2,1,0:T(8,128)S(1)} %get-tuple-element.60), channel_id=1, source_target_pairs={{0,8},{8,16},{16,24},{1,9},{9,17},{17,25},{2,10},{10,18},{18,26},{... | collective-permute-start | bytes 24584 | tf_op jit(solution)/shard_map/ppermute | solution.py:12
  83.7 5.9 %collective-permute-start.6 = (f32[1,34,1,128]{3,1,2,0:T(8,128)S(1)}, f32[1,34,1,128]{3,1,2,0:T(8,128)S(1)}, u32[]{:S(2)}, u32[]{:S(2)}) collective-permute-start(f32[1,34,1,128]{3,1,2,0:T(8,128)S(1)} %get-tuple-element.52), channel_id=1, source_target_pairs={{0,1},{1,2},{2,3},{3,4},{4,5},{5,6},{6,7},{8,9},{9,10},{10,11},{11... | collective-permute-start | bytes 52232 | tf_op jit(solution)/shard_map/ppermute | solution.py:12
  95.6 5.4 %collective-permute-start.12 = (f32[1,1,16,128]{3,2,1,0:T(8,128)S(1)}, f32[1,1,16,128]{3,2,1,0:T(8,128)S(1)}, u32[]{:S(2)}, u32[]{:S(2)}) collective-permute-start(f32[1,1,16,128]{3,2,1,0:T(8,128)S(1)} %get-tuple-element.58), channel_id=1, source_target_pairs={{0,8},{8,16},{16,24},{1,9},{9,17},{17,25},{2,10},{10,18},{18,26},{... | collective-permute-start | bytes 24584 | tf_op jit(solution)/shard_map/ppermute | solution.py:12
  104.1 30.1 %collective-permute-start.14 = (f32[1,34,1,128]{3,1,2,0:T(8,128)S(1)}, f32[1,34,1,128]{3,1,2,0:T(8,128)S(1)}, u32[]{:S(2)}, u32[]{:S(2)}) collective-permute-start(f32[1,34,1,128]{3,1,2,0:T(8,128)S(1)} %get-tuple-element.50), channel_id=1, source_target_pairs={{0,1},{1,2},{2,3},{3,4},{4,5},{5,6},{6,7},{8,9},{9,10},{10,11},{11... | collective-permute-start | bytes 52232 | tf_op jit(solution)/shard_map/ppermute | solution.py:12
  106.7 27.4 %collective-permute-start.15 = (f32[1,34,1,128]{3,1,2,0:T(8,128)S(1)}, f32[1,34,1,128]{3,1,2,0:T(8,128)S(1)}, u32[]{:S(2)}, u32[]{:S(2)}) collective-permute-start(f32[1,34,1,128]{3,1,2,0:T(8,128)S(1)} %get-tuple-element.51), channel_id=1, source_target_pairs={{1,0},{2,1},{3,2},{4,3},{5,4},{6,5},{7,6},{9,8},{10,9},{11,10},{12... | collective-permute-start | bytes 52232 | tf_op jit(solution)/shard_map/ppermute | solution.py:15
  170.9 5.6 %collective-permute-start.18 = (f32[1,18,1,64]{3,1,2,0:T(8,128)S(1)}, f32[1,18,1,64]{3,1,2,0:T(8,128)S(1)}, u32[]{:S(2)}, u32[]{:S(2)}) collective-permute-start(f32[1,18,1,64]{3,1,2,0:T(8,128)S(1)} %get-tuple-element.123), channel_id=1, source_target_pairs={{0,1},{1,2},{2,3},{3,4},{4,5},{5,6},{6,7},{8,9},{9,10},{10,11},{11... | collective-permute-start | bytes 13832 | tf_op jit(solution)/shard_map/ppermute | solution.py:12
  175.2 5.6 %collective-permute-start.19 = (f32[1,18,1,64]{3,1,2,0:T(8,128)S(1)}, f32[1,18,1,64]{3,1,2,0:T(8,128)S(1)}, u32[]{:S(2)}, u32[]{:S(2)}) collective-permute-start(f32[1,18,1,64]{3,1,2,0:T(8,128)S(1)} %get-tuple-element.124), channel_id=1, source_target_pairs={{1,0},{2,1},{3,2},{4,3},{5,4},{6,5},{7,6},{9,8},{10,9},{11,10},{12... | collective-permute-start | bytes 13832 | tf_op jit(solution)/shard_map/ppermute | solution.py:15
  189.5 5.9 %collective-permute-start.22 = (f32[1,18,1,64]{3,1,2,0:T(8,128)S(1)}, f32[1,18,1,64]{3,1,2,0:T(8,128)S(1)}, u32[]{:S(2)}, u32[]{:S(2)}) collective-permute-start(f32[1,18,1,64]{3,1,2,0:T(8,128)S(1)} %get-tuple-element.121), channel_id=1, source_target_pairs={{0,1},{1,2},{2,3},{3,4},{4,5},{5,6},{6,7},{8,9},{9,10},{10,11},{11... | collective-permute-start | bytes 13832 | tf_op jit(solution)/shard_map/ppermute | solution.py:12
  199.1 5.3 %collective-permute-start.24 = (f32[1,1,8,64]{3,2,1,0:T(8,128)S(1)}, f32[1,1,8,64]{3,2,1,0:T(8,128)S(1)}, u32[]{:S(2)}, u32[]{:S(2)}) collective-permute-start(f32[1,1,8,64]{3,2,1,0:T(8,128)S(1)} %get-tuple-element.141), channel_id=1, source_target_pairs={{0,8},{8,16},{16,24},{1,9},{9,17},{17,25},{2,10},{10,18},{18,26},{... | collective-permute-start | bytes 6152 | tf_op jit(solution)/shard_map/ppermute | solution.py:12
  223.5 6.2 %collective-permute-start.34 = (f32[1,18,1,64]{3,1,2,0:T(8,128)S(1)}, f32[1,18,1,64]{3,1,2,0:T(8,128)S(1)}, u32[]{:S(2)}, u32[]{:S(2)}) collective-permute-start(f32[1,18,1,64]{3,1,2,0:T(8,128)S(1)} %get-tuple-element.117), channel_id=1, source_target_pairs={{0,1},{1,2},{2,3},{3,4},{4,5},{5,6},{6,7},{8,9},{9,10},{10,11},{11... | collective-permute-start | bytes 13832 | tf_op jit(solution)/shard_map/ppermute | solution.py:12
  246.0 5.3 %collective-permute-start.36 = (f32[1,1,4,32]{3,2,1,0:T(4,128)S(1)}, f32[1,1,4,32]{3,2,1,0:T(4,128)S(1)}, u32[]{:S(2)}, u32[]{:S(2)}) collective-permute-start(f32[1,1,4,32]{3,2,1,0:T(4,128)S(1)} %get-tuple-element.179), channel_id=1, source_target_pairs={{0,8},{8,16},{16,24},{1,9},{9,17},{17,25},{2,10},{10,18},{18,26},{... | collective-permute-start | bytes 1544 | tf_op jit(solution)/shard_map/ppermute | solution.py:12
  266.1 5.3 %collective-permute-start.40 = (f32[1,1,4,32]{3,2,1,0:T(4,128)S(1)}, f32[1,1,4,32]{3,2,1,0:T(4,128)S(1)}, u32[]{:S(2)}, u32[]{:S(2)}) collective-permute-start(f32[1,1,4,32]{3,2,1,0:T(4,128)S(1)} %get-tuple-element.177), channel_id=1, source_target_pairs={{0,8},{8,16},{16,24},{1,9},{9,17},{17,25},{2,10},{10,18},{18,26},{... | collective-permute-start | bytes 1544 | tf_op jit(solution)/shard_map/ppermute | solution.py:12
  286.3 5.3 %collective-permute-start.44 = (f32[1,1,4,32]{3,2,1,0:T(4,128)S(1)}, f32[1,1,4,32]{3,2,1,0:T(4,128)S(1)}, u32[]{:S(2)}, u32[]{:S(2)}) collective-permute-start(f32[1,1,4,32]{3,2,1,0:T(4,128)S(1)} %get-tuple-element.175), channel_id=1, source_target_pairs={{0,8},{8,16},{16,24},{1,9},{9,17},{17,25},{2,10},{10,18},{18,26},{... | collective-permute-start | bytes 1544 | tf_op jit(solution)/shard_map/ppermute | solution.py:12
  306.4 5.3 %collective-permute-start.48 = (f32[1,1,4,32]{3,2,1,0:T(4,128)S(1)}, f32[1,1,4,32]{3,2,1,0:T(4,128)S(1)}, u32[]{:S(2)}, u32[]{:S(2)}) collective-permute-start(f32[1,1,4,32]{3,2,1,0:T(4,128)S(1)} %get-tuple-element.173), channel_id=1, source_target_pairs={{0,8},{8,16},{16,24},{1,9},{9,17},{17,25},{2,10},{10,18},{18,26},{... | collective-permute-start | bytes 1544 | tf_op jit(solution)/shard_map/ppermute | solution.py:12
  326.5 5.3 %collective-permute-start.52 = (f32[1,1,4,32]{3,2,1,0:T(4,128)S(1)}, f32[1,1,4,32]{3,2,1,0:T(4,128)S(1)}, u32[]{:S(2)}, u32[]{:S(2)}) collective-permute-start(f32[1,1,4,32]{3,2,1,0:T(4,128)S(1)} %get-tuple-element.171), channel_id=1, source_target_pairs={{0,8},{8,16},{16,24},{1,9},{9,17},{17,25},{2,10},{10,18},{18,26},{... | collective-permute-start | bytes 1544 | tf_op jit(solution)/shard_map/ppermute | solution.py:12
  346.6 5.3 %collective-permute-start.56 = (f32[1,1,4,32]{3,2,1,0:T(4,128)S(1)}, f32[1,1,4,32]{3,2,1,0:T(4,128)S(1)}, u32[]{:S(2)}, u32[]{:S(2)}) collective-permute-start(f32[1,1,4,32]{3,2,1,0:T(4,128)S(1)} %get-tuple-element.169), channel_id=1, source_target_pairs={{0,8},{8,16},{16,24},{1,9},{9,17},{17,25},{2,10},{10,18},{18,26},{... | collective-permute-start | bytes 1544 | tf_op jit(solution)/shard_map/ppermute | solution.py:12
  366.7 5.3 %collective-permute-start.60 = (f32[1,1,4,32]{3,2,1,0:T(4,128)S(1)}, f32[1,1,4,32]{3,2,1,0:T(4,128)S(1)}, u32[]{:S(2)}, u32[]{:S(2)}) collective-permute-start(f32[1,1,4,32]{3,2,1,0:T(4,128)S(1)} %get-tuple-element.167), channel_id=1, source_target_pairs={{0,8},{8,16},{16,24},{1,9},{9,17},{17,25},{2,10},{10,18},{18,26},{... | collective-permute-start | bytes 1544 | tf_op jit(solution)/shard_map/ppermute | solution.py:12
  389.6 5.3 %collective-permute-start.64 = (f32[1,1,8,64]{3,2,1,0:T(8,128)S(1)}, f32[1,1,8,64]{3,2,1,0:T(8,128)S(1)}, u32[]{:S(2)}, u32[]{:S(2)}) collective-permute-start(f32[1,1,8,64]{3,2,1,0:T(8,128)S(1)} %get-tuple-element.133), channel_id=1, source_target_pairs={{0,8},{8,16},{16,24},{1,9},{9,17},{17,25},{2,10},{10,18},{18,26},{... | collective-permute-start | bytes 6152 | tf_op jit(solution)/shard_map/ppermute | solution.py:12
  405.6 5.3 %collective-permute-start.68 = (f32[1,1,8,64]{3,2,1,0:T(8,128)S(1)}, f32[1,1,8,64]{3,2,1,0:T(8,128)S(1)}, u32[]{:S(2)}, u32[]{:S(2)}) collective-permute-start(f32[1,1,8,64]{3,2,1,0:T(8,128)S(1)} %get-tuple-element.131), channel_id=1, source_target_pairs={{0,8},{8,16},{16,24},{1,9},{9,17},{17,25},{2,10},{10,18},{18,26},{... | collective-permute-start | bytes 6152 | tf_op jit(solution)/shard_map/ppermute | solution.py:12
  421.6 5.3 %collective-permute-start.72 = (f32[1,1,8,64]{3,2,1,0:T(8,128)S(1)}, f32[1,1,8,64]{3,2,1,0:T(8,128)S(1)}, u32[]{:S(2)}, u32[]{:S(2)}) collective-permute-start(f32[1,1,8,64]{3,2,1,0:T(8,128)S(1)} %get-tuple-element.129), channel_id=1, source_target_pairs={{0,8},{8,16},{16,24},{1,9},{9,17},{17,25},{2,10},{10,18},{18,26},{... | collective-permute-start | bytes 6152 | tf_op jit(solution)/shard_map/ppermute | solution.py:12
  (69 other events, 365.0 us)
where the time goes:
time: 498 us; the launch traced here: 494 us
  starting transfers between devices  216 us (43%)
  waiting for transfers between devices  117 us (23%)
  local copies, waits for them, and re-layouts  112 us (22%)
  other arithmetic  46.5 us (9%)
    ppermute x44, starting transfers between devices, padded_2(): lax.ppermute(lax.slice_in_dim(block, block.shape[dim] - width, None, axis...  145 us
    ppermute x44, waiting for transfers between devices, padded_2(): lax.ppermute(lax.slice_in_dim(block, 0, width, axis=dim), axis, backward)  117 us
    ppermute x44, starting transfers between devices, padded_2(): lax.ppermute(lax.slice_in_dim(block, 0, width, axis=dim), axis, backward)  71.5 us
    reshape x4, local copies, waits for them, and re-layouts, restrict(): field.reshape(first // 2, 2, second // 2, 2, third // 2, 2)  60.8 us
    unnamed x163, local copies, waits for them, and re-layouts  29.9 us
    reduce_sum x6, other arithmetic, restrict(): field.reshape(first // 2, 2, second // 2, 2, third // 2, 2)  24.8 us
  transfers between devices with their start and end apart: 88, of which 38 were waited for; matrix products, arithmetic and copies ran while one was open for 19% of the time, Pallas kernels for 0%

commit v1 on v0

v1 whole, which is shorter than its diff:
```python
import jax
import jax.numpy as jnp
from jax import lax
from jax.experimental import pallas as pl
from jax.experimental.pallas import tpu as pltpu
from jax.sharding import PartitionSpec as P

F32 = jnp.float32
BX, BY, NL = 32, 16, 128
H0 = 3
FX_ = BX + 2 * H0
YE = 24
X1 = BX // 2
H1 = 8
G1 = X1 + 2 * H1
LN2 = 0.6931471805599453


def rot(value, shift, axis):
    return pltpu.roll(value, shift % value.shape[axis], axis)


def iota(shape, axis):
    return lax.broadcasted_iota(jnp.int32, shape, axis)


def sds(*shape):
    return jax.ShapeDtypeStruct(shape, F32)


def by_parity(axis, action):
    odd = lax.axis_index(axis) % 2

    @pl.when(odd == 0)
    def _():
        action(0, 1)

    @pl.when(odd == 1)
    def _():
        action(1, 0)


def call(kernel, out_shape, scratch=(), vmem=24, name=None):
    return pl.pallas_call(
        kernel,
        out_shape=out_shape,
        scratch_shapes=list(scratch),
        compiler_params=pltpu.CompilerParams(vmem_limit_bytes=vmem << 20),
        name=name,
    )


def pack_y(pot, per, src, scr, fix, out0, out1):
    outs = (out0, out1)
    zlane = iota((BX // 2, NL), 1)

    def free_of(value):
        return jnp.where(value == 0, F32(1.0), F32(0.0))

    def row(ref, r):
        return ref[pl.ds(r, BX, stride=BY), :]

    def half(ref, r, parity):
        even = ref[pl.ds(r, BX // 2, stride=2 * BY), :]
        odd = ref[pl.ds(BY + r, BX // 2, stride=2 * BY), :]
        return jnp.where((r + zlane) % 2 == parity, even, odd)

    def side(out, r1, r2, r3):
        rows = [
            row(pot, r1), row(per, r1), row(src, r1), row(scr, r1), free_of(row(fix, r1)),
            row(pot, r2), row(per, r2), free_of(row(fix, r2)),
        ]
        for k, value in enumerate(rows):
            out[BX * k : BX * (k + 1), :] = value
        base = BX * len(rows)
        for k, value in enumerate([half(pot, r3, 1), half(per, r3, 1), half(src, r2, 0), half(scr, r2, 0)]):
            out[base + k * BX // 2 : base + (k + 1) * BX // 2, :] = value

    def action(hi, lo):
        side(outs[hi], BY - 1, BY - 2, BY - 3)
        side(outs[lo], 0, 1, 2)

    by_parity("gy", action)


def pack_x(pot, per, src, scr, fix, got0, got1, hpot, hper, hsrc, hscr, hfree, out0, out1):
    gots, outs = (got0, got1), (out0, out1)
    halos = (hpot, hper, hsrc, hscr, hfree)
    for h in halos:
        h[...] = jnp.zeros_like(h)

    def place(got, slots):
        def whole(ref, k, slot):
            ref[pl.ds(slot, BX, stride=8), :] = got[BX * k : BX * (k + 1), :]

        def halved(ref, k, slot):
            value = got[BX * 8 + k * BX // 2 : BX * 8 + (k + 1) * BX // 2, :]
            ref[pl.ds(slot, BX // 2, stride=16), :] = value
            ref[pl.ds(8 + slot, BX // 2, stride=16), :] = value

        s1, s2, s3 = slots
        for k, ref in enumerate(halos):
            whole(ref, k, s1)
        whole(hpot, 5, s2)
        whole(hper, 6, s2)
        whole(hfree, 7, s2)
        halved(hpot, 0, s3)
        halved(hper, 1, s3)
        halved(hsrc, 2, s2)
        halved(hscr, 3, s2)

    def action_y(hi, lo):
        place(gots[hi], (0, 1, 2))
        place(gots[lo], (7, 6, 5))

    by_parity("gy", action_y)

    def slab(out, planes):
        k = 0
        for ref, h, depth in ((pot, hpot, 3), (per, hper, 3), (src, hsrc, 2), (scr, hscr, 2), (fix, hfree, 2)):
            for x in planes[:depth]:
                own = ref[BY * x : BY * (x + 1), :]
                if ref is fix:
                    own = jnp.where(own == 0, F32(1.0), F32(0.0))
                out[YE * k : YE * k + BY, :] = own
                out[YE * k + BY : YE * (k + 1), :] = h[8 * x : 8 * (x + 1), :]
                k += 1

    def action_x(hi, lo):
        slab(outs[hi], (BX - 1, BX - 2, BX - 3))
        slab(outs[lo], (0, 1, 2))

    by_parity("gx", action_x)


def nonlinear(u, scr):
    up = jnp.exp(u - F32(LN2))
    down = jnp.exp(-u - F32(LN2))
    return scr * (up - down), scr * (up + down)


def off_sum(v, i, plane, fx, fyp, fym, fzp, fzm):
    return (
        (fx[i] * v[i + 1] + fx[i - 1] * v[i - 1])
        + (fyp[i] * rot(plane, -1, 0) + fym[i] * rot(plane, 1, 0))
        + (fzp[i] * v_z(plane, 1) + fzm[i] * v_z(plane, -1))
    )


def v_z(plane, step):
    return rot(plane, -step, 1)


def fine_half(u, i, colour, shift, refs):
    c, fx, fyp, fym, fzp, fzm, src, scr, free = refs
    plane = u[i]
    sh, ch = nonlinear(plane, scr[i])
    value = c[i] * plane - off_sum(u, i, plane, fx, fyp, fym, fzp, fzm) + sh - src[i]
    update = plane - value / (c[i] + ch)
    parity = (iota((YE, NL), 0) + iota((YE, NL), 1) + (i + shift)) % 2
    u[i] = jnp.where((parity == colour) & (free[i] > 0.5), update, plane)


def faces_of(p, i, scale, zstep, fx, fyp, fym, fzp, fzm):
    lane = iota((YE, NL), 1)
    plane = p[i]
    half = F32(0.5 * scale)
    fx[i] = half * (plane + p[i + 1])
    fyp[i] = half * (plane + rot(plane, -1, 0))
    fym[i] = half * (plane + rot(plane, 1, 0))
    fzp[i] = jnp.where(lane >= NL - zstep, F32(0.0), half * (plane + rot(plane, -zstep, 1)))
    fzm[i] = jnp.where(lane < zstep, F32(0.0), half * (plane + rot(plane, zstep, 1)))


def lane_pairs(value, step):
    lane = iota(value.shape, value.ndim - 1)
    return value + jnp.where((lane // step) % 2 == 0, rot(value, -step, value.ndim - 1), rot(value, step, value.ndim - 1))


def fine_pre(pot, per, src, scr, fix, hpot, hper, hsrc, hscr, hfree, got0, got1,
             u, c, fx, fyp, fym, fzp, fzm, esrc, escr, efree, c1, g1, m0, m1,
             ep, tr, tc, tp, p1):
    gots, outs = (got0, got1), (m0, m1)

    def own(x, _):
        i = x + H0
        at = pl.multiple_of(x * BY, 8)
        ht = pl.multiple_of(x * 8, 8)
        for ref, h, ext in ((pot, hpot, u), (per, hper, ep), (src, hsrc, esrc), (scr, hscr, escr), (fix, hfree, efree)):
            value = ref[pl.ds(at, BY), :]
            if ref is fix:
                value = jnp.where(value == 0, F32(1.0), F32(0.0))
            ext[i, 0:BY, :] = value
            ext[i, BY:YE, :] = h[pl.ds(ht, 8), :]
        return 0

    lax.fori_loop(0, BX, own, 0, unroll=4)

    def place(got, planes):
        k = 0
        for ext, depth in ((u, 3), (ep, 3), (esrc, 2), (escr, 2), (efree, 2)):
            for i in planes[:depth]:
                ext[i] = got[YE * k : YE * (k + 1), :]
                k += 1

    def action_x(hi, lo):
        place(gots[hi], (BX + H0, BX + H0 + 1, BX + H0 + 2))
        place(gots[lo], (H0 - 1, H0 - 2, H0 - 3))

    by_parity("gx", action_x)
    for ext in (esrc, escr, efree):
        ext[0] = jnp.zeros((YE, NL), F32)
        ext[FX_ - 1] = jnp.zeros((YE, NL), F32)

    fx[0] = F32(0.5) * (ep[0] + ep[1])
    refs = (c, fx, fyp, fym, fzp, fzm, esrc, escr, efree)

    def first(i, _):
        faces_of(ep, i, 1.0, 1, fx, fyp, fym, fzp, fzm)
        lane = iota((YE, NL), 1)
        ends = jnp.where((lane == 0) | (lane == NL - 1), F32(0.5) * ep[i], F32(0.0))
        c[i] = (fx[i] + fx[i - 1]) + (fyp[i] + fym[i]) + (fzp[i] + fzm[i]) + ends
        fine_half(u, i, 0, 1, refs)
        return 0

    lax.fori_loop(1, FX_ - 1, first, 0, unroll=2)

    def second(i, _):
        fine_half(u, i, 1, 1, refs)
        return 0

    lax.fori_loop(2, FX_ - 2, second, 0, unroll=2)

    def down(x1, _):
        rs, cs = [], []
        for k in (0, 1):
            i = 2 * x1 + k + H0
            plane = u[i]
            sh, ch = nonlinear(plane, escr[i])
            value = c[i] * plane - off_sum(u, i, plane, fx, fyp, fym, fzp, fzm) + sh - esrc[i]
            rs.append(jnp.where(efree[i] > 0.5, -value, F32(0.0))[0:BY])
            cs.append(ch[0:BY])
        at = pl.multiple_of(x1 * BY, 8)
        tr[pl.ds(at, BY), :] = lane_pairs(rs[0] + rs[1], 1)
        tc[pl.ds(at, BY), :] = lane_pairs(cs[0] + cs[1], 1)
        return 0

    lax.fori_loop(0, X1, down, 0, unroll=2)

    def coarse_p(k, _):
        at = pl.multiple_of(k * YE, 8)
        tp[pl.ds(at, YE), :] = lane_pairs(ep[2 * k + 1] + ep[2 * k + 2], 1)
        return 0

    lax.fori_loop(0, X1 + 2, coarse_p, 0, unroll=2)

    eighth = F32(0.125)
    sub = iota((8, NL), 0)
    lane = iota((8, NL), 1)

    def gather_p(k, _):
        p1[k] = eighth * (tp[pl.ds(k * YE, 8, stride=2), :] + tp[pl.ds(k * YE + 1, 8, stride=2), :])
        return 0

    lax.fori_loop(0, X1 + 2, gather_p, 0, unroll=2)

    def make(x1, _):
        k = x1 + 1
        p = p1[k]
        base = k * YE
        high = eighth * (tp[pl.ds(base + 2, 8, stride=2), :] + tp[pl.ds(base + 3, 8, stride=2), :])
        edge = tp[pl.ds(pl.multiple_of(base + 16, 8), 8), :]
        edge = eighth * (edge + rot(edge, 1, 0))
        low = jnp.where(sub == 0, rot(edge, 1, 0), rot(p, 1, 0))
        front = jnp.where(lane >= NL - 2, F32(0.0), rot(p, -2, 1))
        back = jnp.where(lane < 2, F32(0.0), rot(p, 2, 1))
        near = (p1[k + 1] + p1[k - 1]) + (high + low) + (front + back)
        centre = F32(3.0) * p + F32(0.5) * near
        at = x1 * BY
        r = eighth * (tr[pl.ds(at, 8, stride=2), :] + tr[pl.ds(at + 1, 8, stride=2), :])
        react = eighth * (tc[pl.ds(at, 8, stride=2), :] + tc[pl.ds(at + 1, 8, stride=2), :])
        diag = F32(0.25) * centre + react
        c1[x1] = react
        g1[x1] = diag
        message = jnp.where(lane % 2 == 0, r, F32(1.0) / diag)
        m0[pl.ds(pl.multiple_of(x1 * 8, 8), 8), :] = message
        m1[pl.ds(pl.multiple_of(x1 * 8, 8), 8), :] = message
        return 0

    lax.fori_loop(0, X1, make, 0, unroll=2)

    for a in range(X1 // 2):
        message = jnp.where(lane % 2 == 0, p1[1 + 2 * a], p1[2 + 2 * a])
        for m in outs:
            m[X1 * 8 + 8 * a : X1 * 8 + 8 * a + 8, :] = message

    zl = iota((BX // 2, NL), 1)
    base = X1 * 8 + X1 * 4

    def odd_row(out, y):
        even = u[pl.ds(H0, BX // 2, stride=2), y, :]
        odd = u[pl.ds(H0 + 1, BX // 2, stride=2), y, :]
        out[base : base + BX // 2, :] = jnp.where((y + zl) % 2 == 1, even, odd)

    def action_y(hi, lo):
        odd_row(outs[hi], BY - 2)
        odd_row(outs[lo], 1)

    by_parity("gy", action_y)


YMSG = X1 * 8 + X1 * 4 + BX // 2
XMSG = H1 * YE + (H1 // 2) * YE + BY


def pack_x1(m0, m1, got0, got1, u, out0, out1):
    own, gots, outs = m0, (got0, got1), (out0, out1)
    odd_y = lax.axis_index("gy") % 2

    def go(hi, lo):
        def slab(out, first, x):
            at = 0
            for a in range(H1):
                for ref in (own, gots[hi], gots[lo]):
                    out[at : at + 8, :] = ref[8 * (first + a) : 8 * (first + a) + 8, :]
                    at += 8
            for a in range(H1 // 2):
                row = X1 * 8 + 8 * (first // 2 + a)
                for ref in (own, gots[hi], gots[lo]):
                    out[at : at + 8, :] = ref[row : row + 8, :]
                    at += 8
            out[at : at + BY, :] = u[x + H0, 0:BY, :]

        def action(xhi, xlo):
            slab(outs[xhi], X1 - H1, BX - 2)
            slab(outs[xlo], 0, 1)

        by_parity("gx", action)

    @pl.when(odd_y == 0)
    def _():
        go(0, 1)

    @pl.when(odd_y == 1)
    def _():
        go(1, 0)


def coarse_half(e, r, d, i, colour, refs, zstep):
    fx, fyp, fym, fzp, fzm = refs
    plane = e[i]
    beside = (
        (fx[i] * e[i + 1] + fx[i - 1] * e[i - 1])
        + (fyp[i] * rot(plane, -1, 0) + fym[i] * rot(plane, 1, 0))
        + (fzp[i] * rot(plane, -zstep, 1) + fzm[i] * rot(plane, zstep, 1))
    )
    parity = (iota((YE, NL), 0) + iota((YE, NL), 1) // zstep + i) % 2
    e[i] = jnp.where(parity == colour, (r[i] + beside) * d[i], plane)


def dup_even(value):
    lane = iota(value.shape, value.ndim - 1)
    return jnp.where(lane % 2 == 0, value, rot(value, 1, value.ndim - 1))


def dup_odd(value):
    lane = iota(value.shape, value.ndim - 1)
    return jnp.where(lane % 2 == 1, value, rot(value, -1, value.ndim - 1))


def mid_pre(m0, gy0, gy1, gx0, gx1, c1, g1,
            e, r, d, fx, fyp, fym, fzp, fzm, msg,
            p, t, tr, tc, pc):
    gys, gxs = (gy0, gy1), (gx0, gx1)
    odd_y = lax.axis_index("gy") % 2

    def own(hi, lo):
        def planes(a, _):
            rows = [ref[pl.ds(pl.multiple_of(8 * a, 8), 8), :] for ref in (m0, gys[hi], gys[lo])]
            for k, value in enumerate(rows):
                r[H1 + a, 8 * k : 8 * k + 8, :] = dup_even(value)
                d[H1 + a, 8 * k : 8 * k + 8, :] = dup_odd(value)
            return 0

        lax.fori_loop(0, X1, planes, 0, unroll=2)

        def coefs(a, _):
            at = pl.multiple_of(X1 * 8 + 8 * a, 8)
            for k, ref in enumerate((m0, gys[hi], gys[lo])):
                value = ref[pl.ds(at, 8), :]
                p[H1 + 2 * a, 8 * k : 8 * k + 8, :] = dup_even(value)
                p[H1 + 2 * a + 1, 8 * k : 8 * k + 8, :] = dup_odd(value)
            return 0

        lax.fori_loop(0, X1 // 2, coefs, 0, unroll=2)

    @pl.when(odd_y == 0)
    def _():
        own(0, 1)

    @pl.when(odd_y == 1)
    def _():
        own(1, 0)

    def beyond(ref, first):
        def planes(a, _):
            value = ref[pl.ds(pl.multiple_of(YE * a, 8), YE), :]
            r[first + a] = dup_even(value)
            d[first + a] = dup_odd(value)
            return 0

        lax.fori_loop(0, H1, planes, 0, unroll=2)
        for a in range(H1 // 2):
            value = ref[H1 * YE + YE * a : H1 * YE + YE * (a + 1), :]
            p[first + 2 * a] = dup_even(value)
            p[first + 2 * a + 1] = dup_odd(value)

    def action(hi, lo):
        beyond(gxs[hi], H1 + X1)
        beyond(gxs[lo], 0)

    by_parity("gx", action)

    p[G1] = jnp.zeros((YE, NL), F32)
    refs = (fx, fyp, fym, fzp, fzm)

    def begin(i, _):
        faces_of(p, i, 0.25, 2, fx, fyp, fym, fzp, fzm)
        parity = (iota((YE, NL), 0) + iota((YE, NL), 1) // 2 + i) % 2
        e[i] = jnp.where(parity == 0, r[i] * d[i], F32(0.0))
        return 0

    lax.fori_loop(0, G1, begin, 0, unroll=2)
    for k, colour in ((1, 1), (2, 0), (3, 1)):

        def half(i, _, colour=colour):
            coarse_half(e, r, d, i, colour, refs, 2)
            return 0

        lax.fori_loop(k, G1 - k, half, 0, unroll=4)

    def down(x2, _):
        total, reacts = None, None
        for k in (0, 1):
            a = 2 * x2 + k
            i = a + H1
            plane = e[i]
            beside = (
                (fx[i] * e[i + 1] + fx[i - 1] * e[i - 1])
                + (fyp[i] * rot(plane, -1, 0) + fym[i] * rot(plane, 1, 0))
                + (fzp[i] * rot(plane, -2, 1) + fzm[i] * rot(plane, 2, 1))
            )
            left = (r[i] + beside)[0:8] - g1[a] * plane[0:8]
            total = left if total is None else total + left
            reacts = c1[a] if reacts is None else reacts + c1[a]
        at = pl.multiple_of(x2 * 8, 8)
        tr[pl.ds(at, 8), :] = lane_pairs(total, 2)
        tc[pl.ds(at, 8), :] = lane_pairs(reacts, 2)
        return 0

    lax.fori_loop(0, X1 // 2, down, 0, unroll=2)

    def coarse_p(x2, _):
        t[pl.ds(pl.multiple_of(x2 * YE, 8), YE), :] = lane_pairs(p[2 * x2] + p[2 * x2 + 1], 2)
        return 0

    lax.fori_loop(0, G1 // 2, coarse_p, 0, unroll=2)

    eighth = F32(0.125)
    n2, m2 = X1 // 2, G1 // 2

    def compact(ref, first, rows, stride):
        lane = iota((rows, NL), 1)
        out = None
        for j in range(4):
            value = ref[pl.ds(first + 2 * j, rows, stride=stride), :] + ref[pl.ds(first + 2 * j + 1, rows, stride=stride), :]
            out = value if out is None else jnp.where(lane % 4 == j, value, out)
        return eighth * out

    r2 = compact(tr, 0, n2, 8)
    react2 = compact(tc, 0, n2, 8)
    for k in range(3):
        pc[k] = compact(t, 8 * k, m2, YE)
    h2 = H1 // 2
    centre_p = pc[0, h2 : h2 + n2, :]
    j4 = iota((n2, NL), 1) % 4
    lane = iota((n2, NL), 1)
    high = jnp.where(j4 < 3, rot(centre_p, -1, 1), rot(pc[1, h2 : h2 + n2, :], 3, 1))
    low = jnp.where(j4 > 0, rot(centre_p, 1, 1), rot(pc[2, h2 : h2 + n2, :], -3, 1))
    front = jnp.where(lane >= NL - 4, F32(0.0), rot(centre_p, -4, 1))
    back = jnp.where(lane < 4, F32(0.0), rot(centre_p, 4, 1))
    near = (pc[0, h2 + 1 : h2 + 1 + n2, :] + pc[0, h2 - 1 : h2 - 1 + n2, :]) + (high + low) + (front + back)
    diag2 = F32(0.0625) * (F32(3.0) * centre_p + F32(0.5) * near) + react2
    msg[0:8, :] = r2
    msg[8:16, :] = F32(1.0) / diag2
    msg[16:24, :] = centre_p


def finish(at, got, e, r, d, fx1, fyp1, fym1, fzp1, fzm1,
           u, c, fx, fyp, fym, fzp, fzm, src, scr, free, gy0, gy1, gx0, gx1,
           result,
           e2, p2, r2, d2, k2, tx, eu):
    wx, wy = got.shape[0], got.shape[1]
    rows = wx * 8
    e2[...] = jnp.zeros_like(e2)
    p2[0] = jnp.zeros((rows, NL), F32)
    p2[wy + 1] = jnp.zeros((rows, NL), F32)

    def spread(b, _):
        for a in range(wx):
            r2[b, 8 * a : 8 * a + 8, :] = got[a, b, 0:8, :]
            d2[b, 8 * a : 8 * a + 8, :] = got[a, b, 8:16, :]
            p2[b + 1, 8 * a : 8 * a + 8, :] = got[a, b, 16:24, :]
        return 0

    lax.fori_loop(0, wy, spread, 0)
    sub = iota((rows, NL), 0)
    lane = iota((rows, NL), 1)
    j4 = lane % 4
    parity2 = (sub + j4 + lane // 4) % 2

    def shifted(ref, b):
        plane = ref[b + 1]
        return (
            rot(plane, -1, 0), rot(plane, 1, 0),
            jnp.where(j4 < 3, rot(plane, -1, 1), rot(ref[b + 2], 3, 1)),
            jnp.where(j4 > 0, rot(plane, 1, 1), rot(ref[b], -3, 1)),
            rot(plane, -4, 1), rot(plane, 4, 1),
        )

    edges = (sub == rows - 1, sub == 0, None, None, lane >= NL - 4, lane < 4)

    def begin(b, _):
        plane = p2[b + 1]
        for k, (value, edge) in enumerate(zip(shifted(p2, b), edges, strict=True)):
            face = F32(0.03125) * (plane + value)
            k2[k, b] = face if edge is None else jnp.where(edge, F32(0.0), face)
        e2[b + 1, 0:rows, :] = jnp.where(parity2 == 0, r2[b] * d2[b], F32(0.0))
        return 0

    lax.fori_loop(0, wy, begin, 0)

    def half2(step, _):
        colour = step % 2

        def one(b, _):
            total = r2[b]
            for k, value in enumerate(shifted(e2, b)):
                total = total + k2[k, b] * value
            e2[b + 1] = jnp.where(parity2 == colour, total * d2[b], e2[b + 1])
            return 0

        lax.fori_loop(0, wy, one, 0, unroll=2)
        return 0

    lax.fori_loop(1, 8, half2, 0)

    ox, oy = at[0], at[1]
    for k, step in enumerate((0, 1, -1)):
        b = oy + step + 1
        for m, (dx, first, size, to) in enumerate(((0, 0, 8, 4), (1, 0, 4, 12), (-1, 4, 4, 0))):
            a = ox + dx
            inside = (a >= 0) & (a < wx)
            block = e2[b, pl.ds(pl.multiple_of(jnp.clip(a, 0, wx - 1) * 8, 8), 8), :]
            block = jnp.where(inside, block, F32(0.0))
            l8 = iota((8, NL), 1)
            for j in range(4):
                value = jnp.where(l8 % 4 == 0, rot(block, -j, 1), F32(0.0))
                value = value + rot(value, 1, 1)
                value = value + rot(value, 2, 1)
                for y in (0, 1):
                    tx[pl.ds(to * YE + 8 * k + 2 * j + y, size, stride=YE), :] = value[first : first + size]

    def correct(x2, _):
        value = tx[pl.ds(pl.multiple_of(x2 * YE, 8), YE), :]
        eu[2 * x2] = e[2 * x2] + value
        eu[2 * x2 + 1] = e[2 * x2 + 1] + value
        return 0

    lax.fori_loop(1, G1 // 2 - 1, correct, 0, unroll=2)
    refs1 = (fx1, fyp1, fym1, fzp1, fzm1)
    for k, colour in ((4, 0), (5, 1), (6, 0), (7, 1)):

        def half1(i, _, colour=colour):
            coarse_half(eu, r, d, i, colour, refs1, 2)
            return 0

        lax.fori_loop(k, G1 - k, half1, 0, unroll=4)

    base = X1 * 8 + X1 * 4

    def rows_y(got_, y):
        value = got_[base : base + BX // 2, :]
        u[pl.ds(H0, BX // 2, stride=2), y, :] = value
        u[pl.ds(H0 + 1, BX // 2, stride=2), y, :] = value

    def action_y(hi, lo):
        rows_y((gy0, gy1)[hi], BY + 1)
        rows_y((gy0, gy1)[lo], YE - 2)

    by_parity("gy", action_y)

    def action_x(hi, lo):
        u[H0 + BX + 1, 0:BY, :] = (gx0, gx1)[hi][XMSG - BY : XMSG, :]
        u[H0 - 2, 0:BY, :] = (gx0, gx1)[lo][XMSG - BY : XMSG, :]

    by_parity("gx", action_x)

    def add(k, _):
        plane = eu[k + H1 - 1]
        for y in (0, 1):
            tx[pl.ds(k * YE + y, 8, stride=2), :] = plane[0:8]
        wide = tx[pl.ds(pl.multiple_of(k * YE, 8), BY), :]
        s8 = iota((8, NL), 0)
        hi = plane[8:16]
        lo = plane[16:24]
        halo = jnp.where(s8 < 2, jnp.where(s8 == 0, hi, rot(hi, 1, 0)), jnp.where(s8 == 7, lo, rot(lo, -1, 0)))
        for z in (0, 1):
            i = 2 * k + z + H0 - 2
            u[i, 0:BY, :] = jnp.where(free[i, 0:BY, :] > 0.5, u[i, 0:BY, :] + wide, u[i, 0:BY, :])
            u[i, BY:YE, :] = jnp.where(free[i, BY:YE, :] > 0.5, u[i, BY:YE, :] + halo, u[i, BY:YE, :])
        return 0

    lax.fori_loop(0, X1 + 2, add, 0, unroll=2)
    refs = (c, fx, fyp, fym, fzp, fzm, src, scr, free)

    def third(i, _):
        fine_half(u, i, 0, 1, refs)
        return 0

    lax.fori_loop(2, FX_ - 2, third, 0, unroll=2)

    def last(i, _):
        fine_half(u, i, 1, 1, refs)
        result[pl.ds(pl.multiple_of((i - H0) * BY, 8), BY), :] = u[i, 0:BY, :]
        return 0

    lax.fori_loop(H0, H0 + BX, last, 0, unroll=2)


def swap(pair, axis):
    count = lax.axis_size(axis)
    got = []
    for first, message in enumerate(pair):
        route = []
        for i in range(first, count - 1, 2):
            route += [(i, i + 1), (i + 1, i)]
        got.append(lax.ppermute(message, axis, route))
    return tuple(got)


def body(source, permittivity, screening, potential, fixed_cell):
    gx, gy = lax.axis_size("gx"), lax.axis_size("gy")
    args = [a.reshape(BX * BY, NL) for a in (potential, permittivity, source, screening, fixed_cell)]

    y0 = call(pack_y, (sds(10 * BX, NL),) * 2, name="pack_y")(*args)
    y0 = swap(y0, "gy")
    *halos, x0, x1 = call(pack_x, (sds(BX * 8, NL),) * 5 + (sds(12 * YE, NL),) * 2, name="pack_x")(*args, *y0)
    gotx = swap((x0, x1), "gx")

    ext = (FX_, YE, NL)
    fine = call(
        fine_pre,
        (sds(*ext),) * 10 + (sds(X1, 8, NL),) * 2 + (sds(YMSG, NL),) * 2,
        [
            pltpu.VMEM(ext, F32),
            pltpu.VMEM((X1 * BY, NL), F32),
            pltpu.VMEM((X1 * BY, NL), F32),
            pltpu.VMEM(((X1 + 2) * YE, NL), F32),
            pltpu.VMEM((X1 + 2, 8, NL), F32),
        ],
        name="fine_pre",
    )(*args, *halos, *gotx)
    state, (c1, g1, m0, m1) = fine[:10], fine[10:]
    goty1 = swap((m0, m1), "gy")
    x1msg = call(pack_x1, (sds(XMSG, NL),) * 2, name="pack_x1")(m0, m1, *goty1, state[0])
    gotx1 = swap(x1msg, "gx")

    mid = (G1, YE, NL)
    *level1, message = call(
        mid_pre,
        (sds(*mid),) * 8 + (sds(24, NL),),
        [
            pltpu.VMEM((G1 + 1, YE, NL), F32),
            pltpu.VMEM((G1 // 2 * YE, NL), F32),
            pltpu.VMEM((X1 // 2 * 8, NL), F32),
            pltpu.VMEM((X1 // 2 * 8, NL), F32),
            pltpu.VMEM((3, G1 // 2, NL), F32),
        ],
        name="mid_pre",
    )(m0, *goty1, *gotx1, c1, g1)

    everyone = gx * gy
    gathered = lax.all_to_all(jnp.broadcast_to(message[None], (everyone, 24, NL)), ("gx", "gy"), 0, 0)
    gathered = gathered.reshape(gx, gy, 24, NL)
    wx, wy = min(gx, 5), min(gy, 8)
    ix, iy = lax.axis_index("gx"), lax.axis_index("gy")
    fx = jnp.clip(ix - 2, 0, gx - wx)
    fy = jnp.clip(iy - 3, 0, gy - wy)
    if (wx, wy) != (gx, gy):
        gathered = lax.dynamic_slice(gathered, (fx, fy, 0, 0), (wx, wy, 24, NL))
    at = jnp.stack([ix - fx, iy - fy]).astype(jnp.int32)

    spec = pl.BlockSpec(memory_space=pltpu.VMEM)
    inputs = (gathered, *level1, *state, *goty1, *gotx1)
    result = pl.pallas_call(
        finish_kernel(len(inputs)),
        out_shape=sds(BX * BY, NL),
        in_specs=[pl.BlockSpec(memory_space=pltpu.SMEM)] + [spec] * len(inputs),
        out_specs=spec,
        scratch_shapes=[
            pltpu.VMEM((wy + 2, wx * 8, NL), F32),
            pltpu.VMEM((wy + 2, wx * 8, NL), F32),
            pltpu.VMEM((wy, wx * 8, NL), F32),
            pltpu.VMEM((wy, wx * 8, NL), F32),
            pltpu.VMEM((6, wy, wx * 8, NL), F32),
            pltpu.VMEM(((X1 + 2) * YE, NL), F32),
            pltpu.VMEM(mid, F32),
            pltpu.VMEM(ext, F32),
        ],
        compiler_params=pltpu.CompilerParams(vmem_limit_bytes=24 << 20),
        name="finish",
    )(at, *inputs)
    return result.reshape(BX, BY, NL)


def finish_kernel(count):
    def kernel(*refs):
        at, ins, result, scratch = refs[0], list(refs[1 : 1 + count]), refs[1 + count], list(refs[2 + count :])
        field = scratch.pop()
        before = ins[9]
        field[...] = before[...]
        ins[9] = field
        finish(at, *ins, result, *scratch)

    return kernel


def solution(mesh):
    placed = (P("gx", "gy", None),) * 5
    return jax.shard_map(
        body, mesh=mesh, in_specs=placed, out_specs=P("gx", "gy", None), check_vma=False
    )
```

time: 498 us -> 107 us (0.21)
  starting transfers between devices: 216 us -> 26.2 us
  waiting for transfers between devices: 117 us -> 23.8 us
  local copies, waits for them, and re-layouts: 112 us -> 27.1 us
  other arithmetic: 46.5 us -> 0.08 us
  Pallas kernels: 0 us -> 28 us
    ppermute x88 -> x8, starting transfers between devices: 216 us -> 16.7 us  [swap(): got.append(lax.ppermute(message, axis, route))]
    ppermute x88 -> x8, waiting for transfers between devices: 117 us -> 11 us  [swap(): got.append(lax.ppermute(message, axis, route))]
    reshape x8 -> x0, local copies, waits for them, and re-layouts: 64.5 us -> none  [the longest x4 60.8 us: restrict(): field.reshape(first // 2, 2, second // 2, 2, third // 2, 2)]
    reduce_sum x28 -> x0, other arithmetic: 33.6 us -> none  [the longest x6 24.8 us: restrict(): field.reshape(first // 2, 2, second // 2, 2, third // 2, 2)]
    pallas_call x0 -> x6, Pallas kernels: none -> 28 us  [the longest x1 13.7 us: body(): pl.pallas_call(finish_kernel(len(inputs)), out_shape=sds(BX * BY, NL), in...]
    all_to_all x0 -> x1, waiting for transfers between devices: none -> 12.8 us  [body(): lax.all_to_all(jnp.broadcast_to(message[None], (everyone, 24, NL)), ('gx'...]
    all_to_all x0 -> x1, starting transfers between devices: none -> 9.49 us  [body(): lax.all_to_all(jnp.broadcast_to(message[None], (everyone, 24, NL)), ('gx'...]
    another operation x25 -> x0, local copies, waits for them, and re-layouts: 6.6 us -> none  [neighbours(): jnp.stack([padded[2:, 1:-1], padded[:-2, 1:-1], padded[1:-1, 2:], padded[...]
  transfers between devices with their start and end apart: 88 -> 9, of which waited for: 38 -> 5; matrix products, arithmetic and copies ran while one was open for 19% -> 0% of each run, Pallas kernels for 0% -> 0%
where the time goes in v1:
time: 107 us; the launch traced here: 105 us
  Pallas kernels  28 us (26%)
  local copies, waits for them, and re-layouts  27.1 us (25%)
  starting transfers between devices  26.2 us (24%)
  waiting for transfers between devices  23.8 us (22%)
    unnamed x62, local copies, waits for them, and re-layouts  26.2 us
    ppermute x8, starting transfers between devices, swap(): got.append(lax.ppermute(message, axis, route))  16.7 us
    pallas_call x1, Pallas kernels, body(): pl.pallas_call(finish_kernel(len(inputs)), out_shape=sds(BX * BY, NL), in...  13.7 us
    all_to_all x1, waiting for transfers between devices, body(): lax.all_to_all(jnp.broadcast_to(message[None], (everyone, 24, NL)), ('gx'...  12.8 us
    ppermute x8, waiting for transfers between devices, swap(): got.append(lax.ppermute(message, axis, route))  11 us
    all_to_all x1, starting transfers between devices, body(): lax.all_to_all(jnp.broadcast_to(message[None], (everyone, 24, NL)), ('gx'...  9.49 us
    pallas_call x1, Pallas kernels, body(): call(mid_pre, (sds(*mid),) * 8 + (sds(24, NL),), [pltpu.VMEM((G1 + 1, YE,...  7.23 us
    pallas_call x1, Pallas kernels, body(): call(fine_pre, (sds(*ext),) * 10 + (sds(X1, 8, NL),) * 2 + (sds(YMSG, NL)...  6.76 us
  transfers between devices with their start and end apart: 9, of which 5 were waited for; matrix products, arithmetic and copies ran while one was open for 0% of the time, Pallas kernels for 0%

profile of v1, /device:TPU:1, one launch (start us, length us, event | category | flops | bytes accessed | tf_op | source)
XLA Modules:
  0.0 105.4 jit_solution(3113418564690565932)
XLA Ops:
  0.0 0.9 copy-done
  1.0 0.9 copy-done.1
  1.9 0.9 copy-done.2
  2.9 0.9 copy-done.3
  3.8 0.9 copy-done.4
  4.9 2.1 %collective-permute-start = (f32[320,128]{1,0:T(8,128)S(1)}, f32[320,128]{1,0:T(8,128)S(1)}, u32[]{:S(2)}, u32[]{:S(2)}) collective-permute-start(f32[320,128]{1,0:T(8,128)S(1)} %get-tuple-element.39), channel_id=1, source_target_pairs={{0,1},{1,0},{2,3},{3,2},{4,5},{5,4},{6,7},{7,6},{8,9},{9,8},{10,11... | collective-permute-start | bytes 491528 | tf_op jit(solution)/shard_map/ppermute | solution.py:648
  7.7 3.2 %collective-permute-done.got0 = f32[320,128]{1,0:T(8,128)S(1)} collective-permute-done((f32[320,128]{1,0:T(8,128)S(1)}, f32[320,128]{1,0:T(8,128)S(1)}, u32[]{:S(2)}, u32[]{:S(2)}) %collective-permute-start) | collective-permute-done | bytes 163872 | tf_op jit(solution)/shard_map/ppermute | solution.py:648
  11.1 4.1 %collective-permute-start.2 = (f32[288,128]{1,0:T(8,128)S(1)}, f32[288,128]{1,0:T(8,128)S(1)}, u32[]{:S(2)}, u32[]{:S(2)}) collective-permute-start(f32[288,128]{1,0:T(8,128)S(1)} %get-tuple-element.46), channel_id=1, source_target_pairs={{0,8},{8,0},{16,24},{24,16},{1,9},{9,1},{17,25},{25,17},{2,10},{10... | collective-permute-start | bytes 442376 | tf_op jit(solution)/shard_map/ppermute | solution.py:648
  15.2 3.0 %collective-permute-start.3 = (f32[288,128]{1,0:T(8,128)S(1)}, f32[288,128]{1,0:T(8,128)S(1)}, u32[]{:S(2)}, u32[]{:S(2)}) collective-permute-start(f32[288,128]{1,0:T(8,128)S(1)} %get-tuple-element.47), channel_id=1, source_target_pairs={{8,16},{16,8},{9,17},{17,9},{10,18},{18,10},{11,19},{19,11},{12,20... | collective-permute-start | bytes 442376 | tf_op jit(solution)/shard_map/ppermute | solution.py:648
  18.3 3.4 %collective-permute-done.3.got1 = f32[288,128]{1,0:T(8,128)S(1)} collective-permute-done((f32[288,128]{1,0:T(8,128)S(1)}, f32[288,128]{1,0:T(8,128)S(1)}, u32[]{:S(2)}, u32[]{:S(2)}) %collective-permute-start.3) | collective-permute-done | bytes 147488 | tf_op jit(solution)/shard_map/ppermute | solution.py:648
  21.7 6.8 %fine_pre.1 = (f32[38,24,128]{2,1,0:T(8,128)S(1)}, f32[38,24,128]{2,1,0:T(8,128)S(1)}, f32[38,24,128]{2,1,0:T(8,128)S(1)}, f32[38,24,128]{2,1,0:T(8,128)S(1)}, f...) custom-call(f32[512,128]{1,0:T(8,128)S(1)} %bitcast.11, ...), custom_call_target="tpu_custom_call" | custom-call | tf_op jit(solution)/shard_map/fine_pre/pallas_call | solution.py:662
  31.6 2.2 %collective-permute-start.4 = (f32[208,128]{1,0:T(8,128)S(1)}, f32[208,128]{1,0:T(8,128)S(1)}, u32[]{:S(2)}, u32[]{:S(2)}) collective-permute-start(f32[208,128]{1,0:T(8,128)S(1)} %get-tuple-element.48.m0), channel_id=1, source_target_pairs={{0,1},{1,0},{2,3},{3,2},{4,5},{5,4},{6,7},{7,6},{8,9},{9,8},{10,11... | collective-permute-start | bytes 319496 | tf_op jit(solution)/shard_map/ppermute | solution.py:648
  34.4 1.4 %collective-permute-done.4.got0.gy0.refs_20_ = f32[208,128]{1,0:T(8,128)S(1)} collective-permute-done((f32[208,128]{1,0:T(8,128)S(1)}, f32[208,128]{1,0:T(8,128)S(1)}, u32[]{:S(2)}, u32[]{:S(2)}) %collective-permute-start.4) | collective-permute-done | bytes 106528 | tf_op jit(solution)/shard_map/ppermute | solution.py:648
  35.9 3.9 %collective-permute-start.7 = (f32[304,128]{1,0:T(8,128)S(1)}, f32[304,128]{1,0:T(8,128)S(1)}, u32[]{:S(2)}, u32[]{:S(2)}) collective-permute-start(f32[304,128]{1,0:T(8,128)S(1)} %get-tuple-element.52), channel_id=1, source_target_pairs={{8,16},{16,8},{9,17},{17,9},{10,18},{18,10},{11,19},{19,11},{12,20... | collective-permute-start | bytes 466952 | tf_op jit(solution)/shard_map/ppermute | solution.py:648
  39.9 2.9 %collective-permute-done.7.gx1.refs_23_ = f32[304,128]{1,0:T(8,128)S(1)} collective-permute-done((f32[304,128]{1,0:T(8,128)S(1)}, f32[304,128]{1,0:T(8,128)S(1)}, u32[]{:S(2)}, u32[]{:S(2)}) %collective-permute-start.7) | collective-permute-done | bytes 155680 | tf_op jit(solution)/shard_map/ppermute | solution.py:648
  42.8 7.2 %mid_pre.1 = (f32[32,24,128]{2,1,0:T(8,128)S(1)}, f32[32,24,128]{2,1,0:T(8,128)S(1)}, f32[32,24,128]{2,1,0:T(8,128)S(1)}, f32[32,24,128]{2,1,0:T(8,128)S(1)}, f3...) custom-call(f32[208,128]{1,0:T(8,128)S(1)} %get-tuple-element.48.m0,, ...), custom_call_target="tpu_custom_call" | custom-call | tf_op jit(solution)/shard_map/mid_pre/pallas_call | solution.py:680
  56.2 9.5 %all-to-all-start = ((f32[32,24,128]{2,1,0:T(8,128)}), f32[32,24,128]{2,1,0:T(8,128)S(1)}, u32[]{:S(2)}, u32[]{:S(2)}) async-start(f32[32,24,128]{2,1,0:T(8,128)} %broadcast_in_dim.2), calls=%async_computation | async-start | bytes 786432 | tf_op jit(solution)/shard_map/all_to_all | solution.py:694
  65.8 12.8 %all-to-all-done = f32[32,24,128]{2,1,0:T(8,128)S(1)} async-done(((f32[32,24,128]{2,1,0:T(8,128)}), f32[32,24,128]{2,1,0:T(8,128)S(1)}, u32[]{:S(2)}, u32[]{:S(2)}) %all-to-all-start) | async-done | bytes 393248 | tf_op jit(solution)/shard_map/all_to_all | solution.py:694
  78.6 1.0 copy-done.6
  79.7 1.0 copy-done.8
  80.7 1.0 copy-done.10
  81.7 1.0 copy-done.12
  82.7 1.0 copy-done.14
  83.8 1.0 copy-done.16
  84.8 1.0 copy-done.18
  85.8 1.0 copy-done.20
  86.7 1.0 copy-done.22
  87.7 1.0 copy-done.24
  88.7 1.0 copy-done.26
  89.7 1.0 copy-done.28
  90.7 1.0 copy-done.30
  91.7 13.7 %finish.1 = f32[512,128]{1,0:T(8,128)} custom-call(s32[2]{0:T(128)S(1)} %pad_add_fusion.refs_0_, f32[4,8,24,128]{3,2,1,0:T(8,128)S(1)} %bitcast.24, f32[32,24,128]{2,1,0:T(8,128)S(1)} %copy-done.16, f32[32,24,128]{2,1,0:T(8,128)S(1)} %copy-done.18, f32[32,24,128]{2,1,0:T(8,128)S(1)} %copy-done.20, f32[32,24,128]{2,1,0:T(8,128)S(1)} %copy-done.22, ...), custom_call_target="tpu_custom_call" | custom-call | tf_op jit(solution)/shard_map/finish/pallas_call | solution.py:706
  (56 shorter events, 11.2 us)
Async XLA Ops:
  0.0 0.9 copy-start
  1.0 0.9 copy-start.1
  1.9 0.9 copy-start.2
  2.9 0.9 copy-start.3
  3.8 0.9 copy-start.4
  4.9 6.0 %collective-permute-start = (f32[320,128]{1,0:T(8,128)S(1)}, f32[320,128]{1,0:T(8,128)S(1)}, u32[]{:S(2)}, u32[]{:S(2)}) collective-permute-start(f32[320,128]{1,0:T(8,128)S(1)} %get-tuple-element.39), channel_id=1, source_target_pairs={{0,1},{1,0},{2,3},{3,2},{4,5},{5,4},{6,7},{7,6},{8,9},{9,8},{10,11... | collective-permute-start | bytes 491528 | tf_op jit(solution)/shard_map/ppermute | solution.py:648
  7.0 3.9 %collective-permute-start.1 = (f32[320,128]{1,0:T(8,128)S(1)}, f32[320,128]{1,0:T(8,128)S(1)}, u32[]{:S(2)}, u32[]{:S(2)}) collective-permute-start(f32[320,128]{1,0:T(8,128)S(1)} %get-tuple-element.40), channel_id=1, source_target_pairs={{1,2},{2,1},{3,4},{4,3},{5,6},{6,5},{9,10},{10,9},{11,12},{12,11},... | collective-permute-start | bytes 491528 | tf_op jit(solution)/shard_map/ppermute | solution.py:648
  11.1 7.2 %collective-permute-start.2 = (f32[288,128]{1,0:T(8,128)S(1)}, f32[288,128]{1,0:T(8,128)S(1)}, u32[]{:S(2)}, u32[]{:S(2)}) collective-permute-start(f32[288,128]{1,0:T(8,128)S(1)} %get-tuple-element.46), channel_id=1, source_target_pairs={{0,8},{8,0},{16,24},{24,16},{1,9},{9,1},{17,25},{25,17},{2,10},{10... | collective-permute-start | bytes 442376 | tf_op jit(solution)/shard_map/ppermute | solution.py:648
  15.2 6.5 %collective-permute-start.3 = (f32[288,128]{1,0:T(8,128)S(1)}, f32[288,128]{1,0:T(8,128)S(1)}, u32[]{:S(2)}, u32[]{:S(2)}) collective-permute-start(f32[288,128]{1,0:T(8,128)S(1)} %get-tuple-element.47), channel_id=1, source_target_pairs={{8,16},{16,8},{9,17},{17,9},{10,18},{18,10},{11,19},{19,11},{12,20... | collective-permute-start | bytes 442376 | tf_op jit(solution)/shard_map/ppermute | solution.py:648
  28.5 0.8 copy-start.5
  30.0 0.8 copy-start.11
  31.6 11.2 %copy-start.7 = (f32[38,24,128]{2,1,0:T(8,128)}, f32[38,24,128]{2,1,0:T(8,128)S(1)}, u32[]{:S(2)}) copy-start(f32[38,24,128]{2,1,0:T(8,128)S(1)} %get-tuple-element.69.refs_16_) | copy-start | bytes 1400836
  31.6 4.3 %collective-permute-start.4 = (f32[208,128]{1,0:T(8,128)S(1)}, f32[208,128]{1,0:T(8,128)S(1)}, u32[]{:S(2)}, u32[]{:S(2)}) collective-permute-start(f32[208,128]{1,0:T(8,128)S(1)} %get-tuple-element.48.m0), channel_id=1, source_target_pairs={{0,1},{1,0},{2,3},{3,2},{4,5},{5,4},{6,7},{7,6},{8,9},{9,8},{10,11... | collective-permute-start | bytes 319496 | tf_op jit(solution)/shard_map/ppermute | solution.py:648
  33.7 2.1 %collective-permute-start.5 = (f32[208,128]{1,0:T(8,128)S(1)}, f32[208,128]{1,0:T(8,128)S(1)}, u32[]{:S(2)}, u32[]{:S(2)}) collective-permute-start(f32[208,128]{1,0:T(8,128)S(1)} %get-tuple-element.49.m1), channel_id=1, source_target_pairs={{1,2},{2,1},{3,4},{4,3},{5,6},{6,5},{9,10},{10,9},{11,12},{12,11},... | collective-permute-start | bytes 319496 | tf_op jit(solution)/shard_map/ppermute | solution.py:648
  35.9 4.0 %collective-permute-start.6 = (f32[304,128]{1,0:T(8,128)S(1)}, f32[304,128]{1,0:T(8,128)S(1)}, u32[]{:S(2)}, u32[]{:S(2)}) collective-permute-start(f32[304,128]{1,0:T(8,128)S(1)} %get-tuple-element.51), channel_id=1, source_target_pairs={{0,8},{8,0},{16,24},{24,16},{1,9},{9,1},{17,25},{25,17},{2,10},{10... | collective-permute-start | bytes 466952 | tf_op jit(solution)/shard_map/ppermute | solution.py:648
  35.9 6.8 %collective-permute-start.7 = (f32[304,128]{1,0:T(8,128)S(1)}, f32[304,128]{1,0:T(8,128)S(1)}, u32[]{:S(2)}, u32[]{:S(2)}) collective-permute-start(f32[304,128]{1,0:T(8,128)S(1)} %get-tuple-element.52), channel_id=1, source_target_pairs={{8,16},{16,8},{9,17},{17,9},{10,18},{18,10},{11,19},{19,11},{12,20... | collective-permute-start | bytes 466952 | tf_op jit(solution)/shard_map/ppermute | solution.py:648
  53.0 0.8 copy-start.25
  55.3 0.9 copy-start.15
  56.2 22.4 %all-to-all-start = ((f32[32,24,128]{2,1,0:T(8,128)}), f32[32,24,128]{2,1,0:T(8,128)S(1)}, u32[]{:S(2)}, u32[]{:S(2)}) async-start(f32[32,24,128]{2,1,0:T(8,128)} %broadcast_in_dim.2), calls=%async_computation | async-start | bytes 786432 | tf_op jit(solution)/shard_map/all_to_all | solution.py:694
  78.6 1.0 copy-start.6
  79.7 1.0 copy-start.8
  80.7 1.0 copy-start.10
  81.7 1.0 copy-start.12
  82.7 1.0 copy-start.14
  83.8 1.0 copy-start.16
  84.8 1.0 copy-start.18
  85.8 1.0 copy-start.20
  86.7 1.0 copy-start.22
  87.7 1.0 copy-start.24
  88.7 1.0 copy-start.26
  89.7 1.0 copy-start.28
  90.7 1.0 copy-start.30
  (8 other events, 6.1 us)

commit v2 on v1

--- a/solution.py
+++ b/solution.py
@@ -13,6 +13,8 @@
 X1 = BX // 2
 H1 = 8
 G1 = X1 + 2 * H1
+GF = 4
+GM = 6
 LN2 = 0.6931471805599453
 
 
@@ -40,18 +42,25 @@
         action(1, 0)
 
 
-def call(kernel, out_shape, scratch=(), vmem=24, name=None):
+def call(kernel, out_shape, scratch=(), vmem=24, hbm=0):
+    specs = {"in_specs": [pl.BlockSpec(memory_space=pltpu.HBM)] * hbm} if hbm else {}
     return pl.pallas_call(
         kernel,
         out_shape=out_shape,
+        **specs,
         scratch_shapes=list(scratch),
         compiler_params=pltpu.CompilerParams(vmem_limit_bytes=vmem << 20),
-        name=name,
     )
 
 
-def pack_y(pot, per, src, scr, fix, out0, out1):
+def pack_y(hpot, hper, hsrc, hscr, hfix, pot, per, src, scr, fix, out0, out1, sems):
     outs = (out0, out1)
+    pairs = ((hpot, pot), (hper, per), (hsrc, src), (hscr, scr), (hfix, fix))
+    copies = [pltpu.make_async_copy(a, b, sems.at[k]) for k, (a, b) in enumerate(pairs)]
+    for copy in copies:
+        copy.start()
+    for copy in copies:
+        copy.wait()
     zlane = iota((BX // 2, NL), 1)
 
     def free_of(value):
@@ -139,37 +148,62 @@
     return scr * (up - down), scr * (up + down)
 
 
-def off_sum(v, i, plane, fx, fyp, fym, fzp, fzm):
+def beside_of(v, fa, at, n, zstep):
+    fx, fyp, fym, fzp, fzm = fa
+    here = pl.ds(at, n)
+    f = fx[pl.ds(at - 1, n + 1)]
+    mid = v[1 : n + 1]
     return (
-        (fx[i] * v[i + 1] + fx[i - 1] * v[i - 1])
-        + (fyp[i] * rot(plane, -1, 0) + fym[i] * rot(plane, 1, 0))
-        + (fzp[i] * v_z(plane, 1) + fzm[i] * v_z(plane, -1))
+        (f[1:] * v[2:] + f[:n] * v[:n])
+        + (fyp[here] * rot(mid, -1, 1) + fym[here] * rot(mid, 1, 1))
+        + (fzp[here] * rot(mid, -zstep, 2) + fzm[here] * rot(mid, zstep, 2))
     )
 
 
-def v_z(plane, step):
-    return rot(plane, -step, 1)
-
-
-def fine_half(u, i, colour, shift, refs):
-    c, fx, fyp, fym, fzp, fzm, src, scr, free = refs
-    plane = u[i]
-    sh, ch = nonlinear(plane, scr[i])
-    value = c[i] * plane - off_sum(u, i, plane, fx, fyp, fym, fzp, fzm) + sh - src[i]
-    update = plane - value / (c[i] + ch)
-    parity = (iota((YE, NL), 0) + iota((YE, NL), 1) + (i + shift)) % 2
-    u[i] = jnp.where((parity == colour) & (free[i] > 0.5), update, plane)
-
-
-def faces_of(p, i, scale, zstep, fx, fyp, fym, fzp, fzm):
-    lane = iota((YE, NL), 1)
-    plane = p[i]
+def checker(at, n, shift, zstep):
+    shape = (n, YE, NL)
+    return (iota(shape, 0) + iota(shape, 1) + iota(shape, 2) // zstep + (at + shift)) % 2
+
+
+def planes_of(u, at, n, refs):
+    c, fx, fyp, fym, fzp, fzm, src, scr, _ = refs
+    here = pl.ds(at, n)
+    v = u[pl.ds(at - 1, n + 2)]
+    plane = v[1 : n + 1]
+    sh, ch = nonlinear(plane, scr[here])
+    centre = c[here]
+    value = centre * plane - beside_of(v, (fx, fyp, fym, fzp, fzm), at, n, 1) + sh - src[here]
+    return plane, value, centre, ch
+
+
+def fine_half(u, at, n, colour, refs):
+    plane, value, centre, ch = planes_of(u, at, n, refs)
+    update = plane - value / (centre + ch)
+    keep = (checker(at, n, 1, 1) == colour) & (refs[-1][pl.ds(at, n)] > 0.5)
+    u[pl.ds(at, n)] = jnp.where(keep, update, plane)
+
+
+def groups(first, count, n, step):
+    assert count % n == 0
+
+    def one(g, _):
+        step(first + g * n)
+        return 0
+
+    lax.fori_loop(0, count // n, one, 0)
+
+
+def faces_of(p, at, n, scale, zstep, fx, fyp, fym, fzp, fzm):
+    here = pl.ds(at, n)
+    lane = iota((n, YE, NL), 2)
+    v = p[pl.ds(at, n + 1)]
+    plane = v[:n]
     half = F32(0.5 * scale)
-    fx[i] = half * (plane + p[i + 1])
-    fyp[i] = half * (plane + rot(plane, -1, 0))
-    fym[i] = half * (plane + rot(plane, 1, 0))
-    fzp[i] = jnp.where(lane >= NL - zstep, F32(0.0), half * (plane + rot(plane, -zstep, 1)))
-    fzm[i] = jnp.where(lane < zstep, F32(0.0), half * (plane + rot(plane, zstep, 1)))
+    fx[here] = half * (plane + v[1:])
+    fyp[here] = half * (plane + rot(plane, -1, 1))
+    fym[here] = half * (plane + rot(plane, 1, 1))
+    fzp[here] = jnp.where(lane >= NL - zstep, F32(0.0), half * (plane + rot(plane, -zstep, 2)))
+    fzm[here] = jnp.where(lane < zstep, F32(0.0), half * (plane + rot(plane, zstep, 2)))
 
 
 def lane_pairs(value, step):
@@ -215,37 +249,29 @@
     fx[0] = F32(0.5) * (ep[0] + ep[1])
     refs = (c, fx, fyp, fym, fzp, fzm, esrc, escr, efree)
 
-    def first(i, _):
-        faces_of(ep, i, 1.0, 1, fx, fyp, fym, fzp, fzm)
-        lane = iota((YE, NL), 1)
-        ends = jnp.where((lane == 0) | (lane == NL - 1), F32(0.5) * ep[i], F32(0.0))
-        c[i] = (fx[i] + fx[i - 1]) + (fyp[i] + fym[i]) + (fzp[i] + fzm[i]) + ends
-        fine_half(u, i, 0, 1, refs)
-        return 0
-
-    lax.fori_loop(1, FX_ - 1, first, 0, unroll=2)
-
-    def second(i, _):
-        fine_half(u, i, 1, 1, refs)
-        return 0
-
-    lax.fori_loop(2, FX_ - 2, second, 0, unroll=2)
-
-    def down(x1, _):
-        rs, cs = [], []
-        for k in (0, 1):
-            i = 2 * x1 + k + H0
-            plane = u[i]
-            sh, ch = nonlinear(plane, escr[i])
-            value = c[i] * plane - off_sum(u, i, plane, fx, fyp, fym, fzp, fzm) + sh - esrc[i]
-            rs.append(jnp.where(efree[i] > 0.5, -value, F32(0.0))[0:BY])
-            cs.append(ch[0:BY])
-        at = pl.multiple_of(x1 * BY, 8)
-        tr[pl.ds(at, BY), :] = lane_pairs(rs[0] + rs[1], 1)
-        tc[pl.ds(at, BY), :] = lane_pairs(cs[0] + cs[1], 1)
-        return 0
-
-    lax.fori_loop(0, X1, down, 0, unroll=2)
+    def first(at):
+        n = GF
+        faces_of(ep, at, n, 1.0, 1, fx, fyp, fym, fzp, fzm)
+        here = pl.ds(at, n)
+        lane = iota((n, YE, NL), 2)
+        ends = jnp.where((lane == 0) | (lane == NL - 1), F32(0.5) * ep[here], F32(0.0))
+        f = fx[pl.ds(at - 1, n + 1)]
+        c[here] = (f[1:] + f[:n]) + (fyp[here] + fym[here]) + (fzp[here] + fzm[here]) + ends
+        fine_half(u, at, n, 0, refs)
+
+    groups(1, FX_ - 2, GF, first)
+    groups(1, FX_ - 2, GF, lambda at: fine_half(u, at, GF, 1, refs))
+
+    def down(at):
+        n = 4
+        _, value, _, ch = planes_of(u, at, n, refs)
+        left = jnp.where(efree[pl.ds(at, n)] > 0.5, -value, F32(0.0))
+        for a in range(0, n, 2):
+            to = pl.multiple_of((at - H0 + a) * (BY // 2), 8)
+            tr[pl.ds(to, BY), :] = lane_pairs(left[a, 0:BY] + left[a + 1, 0:BY], 1)
+            tc[pl.ds(to, BY), :] = lane_pairs(ch[a, 0:BY] + ch[a + 1, 0:BY], 1)
+
+    groups(H0, BX, 4, down)
 
     def coarse_p(k, _):
         at = pl.multiple_of(k * YE, 8)
@@ -346,16 +372,11 @@
         go(1, 0)
 
 
-def coarse_half(e, r, d, i, colour, refs, zstep):
-    fx, fyp, fym, fzp, fzm = refs
-    plane = e[i]
-    beside = (
-        (fx[i] * e[i + 1] + fx[i - 1] * e[i - 1])
-        + (fyp[i] * rot(plane, -1, 0) + fym[i] * rot(plane, 1, 0))
-        + (fzp[i] * rot(plane, -zstep, 1) + fzm[i] * rot(plane, zstep, 1))
-    )
-    parity = (iota((YE, NL), 0) + iota((YE, NL), 1) // zstep + i) % 2
-    e[i] = jnp.where(parity == colour, (r[i] + beside) * d[i], plane)
+def coarse_half(e, r, d, at, n, colour, refs, zstep):
+    v = e[pl.ds(at - 1, n + 2)]
+    here = pl.ds(at, n)
+    update = (r[here] + beside_of(v, refs, at, n, zstep)) * d[here]
+    e[here] = jnp.where(checker(at, n, 0, zstep) == colour, update, v[1 : n + 1])
 
 
 def dup_even(value):
@@ -424,41 +445,28 @@
     p[G1] = jnp.zeros((YE, NL), F32)
     refs = (fx, fyp, fym, fzp, fzm)
 
-    def begin(i, _):
-        faces_of(p, i, 0.25, 2, fx, fyp, fym, fzp, fzm)
-        parity = (iota((YE, NL), 0) + iota((YE, NL), 1) // 2 + i) % 2
-        e[i] = jnp.where(parity == 0, r[i] * d[i], F32(0.0))
-        return 0
-
-    lax.fori_loop(0, G1, begin, 0, unroll=2)
-    for k, colour in ((1, 1), (2, 0), (3, 1)):
-
-        def half(i, _, colour=colour):
-            coarse_half(e, r, d, i, colour, refs, 2)
-            return 0
-
-        lax.fori_loop(k, G1 - k, half, 0, unroll=4)
-
-    def down(x2, _):
-        total, reacts = None, None
-        for k in (0, 1):
-            a = 2 * x2 + k
-            i = a + H1
-            plane = e[i]
-            beside = (
-                (fx[i] * e[i + 1] + fx[i - 1] * e[i - 1])
-                + (fyp[i] * rot(plane, -1, 0) + fym[i] * rot(plane, 1, 0))
-                + (fzp[i] * rot(plane, -2, 1) + fzm[i] * rot(plane, 2, 1))
-            )
-            left = (r[i] + beside)[0:8] - g1[a] * plane[0:8]
-            total = left if total is None else total + left
-            reacts = c1[a] if reacts is None else reacts + c1[a]
-        at = pl.multiple_of(x2 * 8, 8)
-        tr[pl.ds(at, 8), :] = lane_pairs(total, 2)
-        tc[pl.ds(at, 8), :] = lane_pairs(reacts, 2)
-        return 0
-
-    lax.fori_loop(0, X1 // 2, down, 0, unroll=2)
+    def begin(at):
+        n = 4
+        here = pl.ds(at, n)
+        faces_of(p, at, n, 0.25, 2, fx, fyp, fym, fzp, fzm)
+        e[here] = jnp.where(checker(at, n, 0, 2) == 0, r[here] * d[here], F32(0.0))
+
+    groups(0, G1, 4, begin)
+    for colour in (1, 0, 1):
+        groups(1, G1 - 2, GM, lambda at, colour=colour: coarse_half(e, r, d, at, GM, colour, refs, 2))
+
+    def down(at):
+        n = 4
+        v = e[pl.ds(at - 1, n + 2)]
+        here = pl.ds(at, n)
+        left = (r[here] + beside_of(v, refs, at, n, 2))[:, 0:8] - g1[pl.ds(at - H1, n)] * v[1 : n + 1, 0:8]
+        react = c1[pl.ds(at - H1, n)]
+        for a in range(0, n, 2):
+            to = pl.multiple_of((at - H1 + a) * 4, 8)
+            tr[pl.ds(to, 8), :] = lane_pairs(left[a] + left[a + 1], 2)
+            tc[pl.ds(to, 8), :] = lane_pairs(react[a] + react[a + 1], 2)
+
+    groups(H1, X1, 4, down)
 
     def coarse_p(x2, _):
         t[pl.ds(pl.multiple_of(x2 * YE, 8), YE), :] = lane_pairs(p[2 * x2] + p[2 * x2 + 1], 2)
@@ -491,9 +499,15 @@
     back = jnp.where(lane < 4, F32(0.0), rot(centre_p, 4, 1))
     near = (pc[0, h2 + 1 : h2 + 1 + n2, :] + pc[0, h2 - 1 : h2 - 1 + n2, :]) + (high + low) + (front + back)
     diag2 = F32(0.0625) * (F32(3.0) * centre_p + F32(0.5) * near) + react2
-    msg[0:8, :] = r2
-    msg[8:16, :] = F32(1.0) / diag2
-    msg[16:24, :] = centre_p
+    inverse2 = F32(1.0) / diag2
+
+    def every(k, _):
+        msg[k, 0:8, :] = r2
+        msg[k, 8:16, :] = inverse2
+        msg[k, 16:24, :] = centre_p
+        return 0
+
+    lax.fori_loop(0, msg.shape[0], every, 0)
 
 
 def finish(at, got, e, r, d, fx1, fyp1, fym1, fzp1, fzm1,
@@ -519,38 +533,42 @@
     j4 = lane % 4
     parity2 = (sub + j4 + lane // 4) % 2
 
-    def shifted(ref, b):
-        plane = ref[b + 1]
+    span = 4 if wy % 4 == 0 else 1
+
+    def shifted(v):
+        mid = v[1 : span + 1]
+        near = j4[None] < 3
         return (
-            rot(plane, -1, 0), rot(plane, 1, 0),
-            jnp.where(j4 < 3, rot(plane, -1, 1), rot(ref[b + 2], 3, 1)),
-            jnp.where(j4 > 0, rot(plane, 1, 1), rot(ref[b], -3, 1)),
-            rot(plane, -4, 1), rot(plane, 4, 1),
+            rot(mid, -1, 1), rot(mid, 1, 1),
+            jnp.where(near, rot(mid, -1, 2), rot(v[2:], 3, 2)),
+            jnp.where(j4[None] > 0, rot(mid, 1, 2), rot(v[:span], -3, 2)),
+            rot(mid, -4, 2), rot(mid, 4, 2),
         )
 
     edges = (sub == rows - 1, sub == 0, None, None, lane >= NL - 4, lane < 4)
 
-    def begin(b, _):
-        plane = p2[b + 1]
-        for k, (value, edge) in enumerate(zip(shifted(p2, b), edges, strict=True)):
-            face = F32(0.03125) * (plane + value)
-            k2[k, b] = face if edge is None else jnp.where(edge, F32(0.0), face)
-        e2[b + 1, 0:rows, :] = jnp.where(parity2 == 0, r2[b] * d2[b], F32(0.0))
-        return 0
-
-    lax.fori_loop(0, wy, begin, 0)
+    def begin(b):
+        here = pl.ds(b, span)
+        v = p2[pl.ds(b, span + 2)]
+        for k, (value, edge) in enumerate(zip(shifted(v), edges, strict=True)):
+            face = F32(0.03125) * (v[1 : span + 1] + value)
+            k2[k, here] = face if edge is None else jnp.where(edge[None], F32(0.0), face)
+        e2[pl.ds(b + 1, span)] = jnp.where(parity2[None] == 0, r2[here] * d2[here], F32(0.0))
+
+    groups(0, wy, span, begin)
 
     def half2(step, _):
         colour = step % 2
 
-        def one(b, _):
-            total = r2[b]
-            for k, value in enumerate(shifted(e2, b)):
-                total = total + k2[k, b] * value
-            e2[b + 1] = jnp.where(parity2 == colour, total * d2[b], e2[b + 1])
-            return 0
-
-        lax.fori_loop(0, wy, one, 0, unroll=2)
+        def one(b):
+            here = pl.ds(b, span)
+            v = e2[pl.ds(b, span + 2)]
+            total = r2[here]
+            for k, value in enumerate(shifted(v)):
+                total = total + k2[k, here] * value
+            e2[pl.ds(b + 1, span)] = jnp.where(parity2[None] == colour, total * d2[here], v[1 : span + 1])
+
+        groups(0, wy, span, one)
         return 0
 
     lax.fori_loop(1, 8, half2, 0)
@@ -558,7 +576,7 @@
     ox, oy = at[0], at[1]
     for k, step in enumerate((0, 1, -1)):
         b = oy + step + 1
-        for m, (dx, first, size, to) in enumerate(((0, 0, 8, 4), (1, 0, 4, 12), (-1, 4, 4, 0))):
+        for dx, first, size, to in ((0, 0, 8, 4), (1, 0, 4, 12), (-1, 4, 4, 0)):
             a = ox + dx
             inside = (a >= 0) & (a < wx)
             block = e2[b, pl.ds(pl.multiple_of(jnp.clip(a, 0, wx - 1) * 8, 8), 8), :]
@@ -579,13 +597,8 @@
 
     lax.fori_loop(1, G1 // 2 - 1, correct, 0, unroll=2)
     refs1 = (fx1, fyp1, fym1, fzp1, fzm1)
-    for k, colour in ((4, 0), (5, 1), (6, 0), (7, 1)):
-
-        def half1(i, _, colour=colour):
-            coarse_half(eu, r, d, i, colour, refs1, 2)
-            return 0
-
-        lax.fori_loop(k, G1 - k, half1, 0, unroll=4)
+    for first, count, colour in ((4, 24, 0), (4, 24, 1), (4, 24, 0), (7, 18, 1)):
+        groups(first, count, GM, lambda at, colour=colour: coarse_half(eu, r, d, at, GM, colour, refs1, 2))
 
     base = X1 * 8 + X1 * 4
 
@@ -624,38 +637,40 @@
     lax.fori_loop(0, X1 + 2, add, 0, unroll=2)
     refs = (c, fx, fyp, fym, fzp, fzm, src, scr, free)
 
-    def third(i, _):
-        fine_half(u, i, 0, 1, refs)
-        return 0
-
-    lax.fori_loop(2, FX_ - 2, third, 0, unroll=2)
-
-    def last(i, _):
-        fine_half(u, i, 1, 1, refs)
-        result[pl.ds(pl.multiple_of((i - H0) * BY, 8), BY), :] = u[i, 0:BY, :]
-        return 0
-
-    lax.fori_loop(H0, H0 + BX, last, 0, unroll=2)
+    groups(1, FX_ - 2, GF, lambda at: fine_half(u, at, GF, 0, refs))
+
+    def last(at):
+        n = 4
+        plane, value, centre, ch = planes_of(u, at, n, refs)
+        update = plane - value / (centre + ch)
+        keep = (checker(at, n, 1, 1) == 1) & (free[pl.ds(at, n)] > 0.5)
+        out = jnp.where(keep, update, plane)[:, 0:BY]
+        result[pl.ds(pl.multiple_of((at - H0) * BY, 8), n * BY), :] = out.reshape(n * BY, NL)
+
+    groups(H0, BX, 4, last)
 
 
 def swap(pair, axis):
     count = lax.axis_size(axis)
-    got = []
-    for first, message in enumerate(pair):
+    got = [None, None]
+    for first in (1, 0):
         route = []
         for i in range(first, count - 1, 2):
             route += [(i, i + 1), (i + 1, i)]
-        got.append(lax.ppermute(message, axis, route))
+        got[first] = lax.ppermute(pair[first], axis, route)
     return tuple(got)
 
 
 def body(source, permittivity, screening, potential, fixed_cell):
     gx, gy = lax.axis_size("gx"), lax.axis_size("gy")
     args = [a.reshape(BX * BY, NL) for a in (potential, permittivity, source, screening, fixed_cell)]
-
-    y0 = call(pack_y, (sds(10 * BX, NL),) * 2, name="pack_y")(*args)
+    args = [pltpu.with_memory_space_constraint(a, pltpu.HBM) for a in args]
+
+    whole = (sds(BX * BY, NL),) * 4 + (jax.ShapeDtypeStruct((BX * BY, NL), jnp.int32),)
+    *args, y0, y1 = call(pack_y, whole + (sds(10 * BX, NL),) * 2, [pltpu.SemaphoreType.DMA((5,))], hbm=5)(*args)
+    y0 = (y0, y1)
     y0 = swap(y0, "gy")
-    *halos, x0, x1 = call(pack_x, (sds(BX * 8, NL),) * 5 + (sds(12 * YE, NL),) * 2, name="pack_x")(*args, *y0)
+    *halos, x0, x1 = call(pack_x, (sds(BX * 8, NL),) * 5 + (sds(12 * YE, NL),) * 2)(*args, *y0)
     gotx = swap((x0, x1), "gx")
 
     ext = (FX_, YE, NL)
@@ -669,17 +684,16 @@
             pltpu.VMEM(((X1 + 2) * YE, NL), F32),
             pltpu.VMEM((X1 + 2, 8, NL), F32),
         ],
-        name="fine_pre",
     )(*args, *halos, *gotx)
     state, (c1, g1, m0, m1) = fine[:10], fine[10:]
     goty1 = swap((m0, m1), "gy")
-    x1msg = call(pack_x1, (sds(XMSG, NL),) * 2, name="pack_x1")(m0, m1, *goty1, state[0])
+    x1msg = call(pack_x1, (sds(XMSG, NL),) * 2)(m0, m1, *goty1, state[0])
     gotx1 = swap(x1msg, "gx")
 
     mid = (G1, YE, NL)
     *level1, message = call(
         mid_pre,
-        (sds(*mid),) * 8 + (sds(24, NL),),
+        (sds(*mid),) * 8 + (sds(gx * gy, 24, NL),),
         [
             pltpu.VMEM((G1 + 1, YE, NL), F32),
             pltpu.VMEM((G1 // 2 * YE, NL), F32),
@@ -687,27 +701,18 @@
             pltpu.VMEM((X1 // 2 * 8, NL), F32),
             pltpu.VMEM((3, G1 // 2, NL), F32),
         ],
-        name="mid_pre",
     )(m0, *goty1, *gotx1, c1, g1)
 
-    everyone = gx * gy
-    gathered = lax.all_to_all(jnp.broadcast_to(message[None], (everyone, 24, NL)), ("gx", "gy"), 0, 0)
-    gathered = gathered.reshape(gx, gy, 24, NL)
+    gathered = lax.all_to_all(message, ("gx", "gy"), 0, 0).reshape(gx, gy, 24, NL)
     wx, wy = min(gx, 5), min(gy, 8)
-    ix, iy = lax.axis_index("gx"), lax.axis_index("gy")
-    fx = jnp.clip(ix - 2, 0, gx - wx)
-    fy = jnp.clip(iy - 3, 0, gy - wy)
     if (wx, wy) != (gx, gy):
-        gathered = lax.dynamic_slice(gathered, (fx, fy, 0, 0), (wx, wy, 24, NL))
-    at = jnp.stack([ix - fx, iy - fy]).astype(jnp.int32)
-
-    spec = pl.BlockSpec(memory_space=pltpu.VMEM)
+        first = (*window(gx, gy, wx, wy)[:2], 0, 0)
+        gathered = lax.dynamic_slice(gathered, first, (wx, wy, 24, NL))
+
     inputs = (gathered, *level1, *state, *goty1, *gotx1)
     result = pl.pallas_call(
-        finish_kernel(len(inputs)),
+        finish_kernel(len(inputs), (gx, gy, wx, wy)),
         out_shape=sds(BX * BY, NL),
-        in_specs=[pl.BlockSpec(memory_space=pltpu.SMEM)] + [spec] * len(inputs),
-        out_specs=spec,
         scratch_shapes=[
             pltpu.VMEM((wy + 2, wx * 8, NL), F32),
             pltpu.VMEM((wy + 2, wx * 8, NL), F32),
@@ -720,24 +725,30 @@
         ],
         compiler_params=pltpu.CompilerParams(vmem_limit_bytes=24 << 20),
         name="finish",
-    )(at, *inputs)
+    )(*inputs)
     return result.reshape(BX, BY, NL)
 
 
-def finish_kernel(count):
+def window(gx, gy, wx, wy):
+    ix, iy = lax.axis_index("gx"), lax.axis_index("gy")
+    fx = jnp.clip(ix - 2, 0, gx - wx)
+    fy = jnp.clip(iy - 3, 0, gy - wy)
+    return fx, fy, ix - fx, iy - fy
+
+
+def finish_kernel(count, sizes):
     def kernel(*refs):
-        at, ins, result, scratch = refs[0], list(refs[1 : 1 + count]), refs[1 + count], list(refs[2 + count :])
+        ins, result, scratch = list(refs[:count]), refs[count], list(refs[1 + count :])
         field = scratch.pop()
         before = ins[9]
         field[...] = before[...]
         ins[9] = field
-        finish(at, *ins, result, *scratch)
+        finish(window(*sizes)[2:], *ins, result, *scratch)
 
     return kernel
 
 
 def solution(mesh):
     placed = (P("gx", "gy", None),) * 5
-    return jax.shard_map(
-        body, mesh=mesh, in_specs=placed, out_specs=P("gx", "gy", None), check_vma=False
-    )
+
+    return jax.shard_map(body, mesh=mesh, in_specs=placed, out_specs=P("gx", "gy", None), check_vma=False)

time: 107 us -> 72.2 us (0.67)
  local copies, waits for them, and re-layouts: 27.1 us -> 0 us
  blocking collectives: 0 us -> 18.9 us
  waiting for transfers between devices: 23.8 us -> 11.6 us
  Pallas kernels: 28 us -> 20.5 us
  starting transfers between devices: 26.2 us -> 20.1 us
    unnamed x62 -> x0, local copies, waits for them, and re-layouts: 26.2 us -> none
    all_to_all x0 -> x1, blocking collectives: none -> 18.9 us  [body(): lax.all_to_all(message, ('gx', 'gy'), 0, 0).reshape(gx, gy, 24, NL)]
    all_to_all x1 -> x0, waiting for transfers between devices: 12.8 us -> none  [body(): lax.all_to_all(jnp.broadcast_to(message[None], (everyone, 24, NL)), ('gx'...]
    all_to_all x1 -> x0, starting transfers between devices: 9.49 us -> none  [body(): lax.all_to_all(jnp.broadcast_to(message[None], (everyone, 24, NL)), ('gx'...]
    pallas_call x5, Pallas kernels: 21.3 us -> 15.2 us  [the longest x1 7.66 us: body(): pl.pallas_call(finish_kernel(len(inputs), (gx, gy, wx, wy)), out_shape=sd...]
    ppermute x8, starting transfers between devices: 16.7 us -> 20.1 us  [swap(): got[first] = lax.ppermute(pair[first], axis, route)]
    pallas_call x1, Pallas kernels: 6.76 us -> 5.3 us  [body(): call(fine_pre, (sds(*ext),) * 10 + (sds(X1, 8, NL),) * 2 + (sds(YMSG, NL)...]
  transfers between devices with their start and end apart: 9 -> 8, of which waited for: 5 -> 4; matrix products, arithmetic and copies ran while one was open for 0% -> 0% of each run, Pallas kernels for 0% -> 0%
where the time goes in v2:
time: 72.2 us; the launch traced here: 71.2 us
  Pallas kernels  20.5 us (28%)
  starting transfers between devices  20.1 us (28%)
  blocking collectives  18.9 us (26%)
  waiting for transfers between devices  11.6 us (16%)
    ppermute x8, starting transfers between devices, swap(): got[first] = lax.ppermute(pair[first], axis, route)  20.1 us
    all_to_all x1, blocking collectives, body(): lax.all_to_all(message, ('gx', 'gy'), 0, 0).reshape(gx, gy, 24, NL)  18.9 us
    ppermute x8, waiting for transfers between devices, swap(): got[first] = lax.ppermute(pair[first], axis, route)  11.6 us
    pallas_call x1, Pallas kernels, body(): pl.pallas_call(finish_kernel(len(inputs), (gx, gy, wx, wy)), out_shape=sd...  7.66 us
    pallas_call x1, Pallas kernels, body(): call(mid_pre, (sds(*mid),) * 8 + (sds(gx * gy, 24, NL),), [pltpu.VMEM((G1...  5.85 us
    pallas_call x1, Pallas kernels, body(): call(fine_pre, (sds(*ext),) * 10 + (sds(X1, 8, NL),) * 2 + (sds(YMSG, NL)...  5.3 us
    pallas_call x1, Pallas kernels, body(): call(pack_y, whole + (sds(10 * BX, NL),) * 2, [pltpu.SemaphoreType.DMA((5...  1.49 us
  transfers between devices with their start and end apart: 8, of which 4 were waited for; matrix products, arithmetic and copies ran while one was open for 0% of the time, Pallas kernels for 0%

profile of v2, /device:TPU:1, one launch (start us, length us, event | category | flops | bytes accessed | tf_op | source)
XLA Modules:
  0.0 71.2 jit_solution(7097588992798274108)
XLA Ops:
  0.0 1.5 %shard_map.55 = (f32[512,128]{1,0:T(8,128)S(1)}, f32[512,128]{1,0:T(8,128)S(1)}, f32[512,128]{1,0:T(8,128)S(1)}, f32[512,128]{1,0:T(8,128)S(1)}, s32[512,128]{1,...) custom-call(f32[512,128]{1,0:T(8,128)} %bitcast.8, f32[512,128]{1,0:T(8,128)} %bitcast.9, ...), custom_call_target="tpu_custom_call" | custom-call | tf_op jit(solution)/shard_map/pallas_call | solution.py:670
  1.5 2.1 %collective-permute-start = (f32[320,128]{1,0:T(8,128)S(1)}, f32[320,128]{1,0:T(8,128)S(1)}, u32[]{:S(2)}, u32[]{:S(2)}) collective-permute-start(f32[320,128]{1,0:T(8,128)S(1)} %get-tuple-element.49), channel_id=1, source_target_pairs={{0,1},{1,0},{2,3},{3,2},{4,5},{5,4},{6,7},{7,6},{8,9},{9,8},{10,11... | collective-permute-start | bytes 491528 | tf_op jit(solution)/shard_map/ppermute | solution.py:660
  3.6 0.7 collective-permute-start.1
  4.3 3.2 %collective-permute-done.got0 = f32[320,128]{1,0:T(8,128)S(1)} collective-permute-done((f32[320,128]{1,0:T(8,128)S(1)}, f32[320,128]{1,0:T(8,128)S(1)}, u32[]{:S(2)}, u32[]{:S(2)}) %collective-permute-start) | collective-permute-done | bytes 163872 | tf_op jit(solution)/shard_map/ppermute | solution.py:660
  7.5 0.0 collective-permute-done.1.got1
  7.5 0.2 shard_map.56
  7.7 4.1 %collective-permute-start.2 = (f32[288,128]{1,0:T(8,128)S(1)}, f32[288,128]{1,0:T(8,128)S(1)}, u32[]{:S(2)}, u32[]{:S(2)}) collective-permute-start(f32[288,128]{1,0:T(8,128)S(1)} %get-tuple-element.56), channel_id=1, source_target_pairs={{0,8},{8,0},{16,24},{24,16},{1,9},{9,1},{17,25},{25,17},{2,10},{10... | collective-permute-start | bytes 442376 | tf_op jit(solution)/shard_map/ppermute | solution.py:660
  11.8 3.0 %collective-permute-start.3 = (f32[288,128]{1,0:T(8,128)S(1)}, f32[288,128]{1,0:T(8,128)S(1)}, u32[]{:S(2)}, u32[]{:S(2)}) collective-permute-start(f32[288,128]{1,0:T(8,128)S(1)} %get-tuple-element.57), channel_id=1, source_target_pairs={{8,16},{16,8},{9,17},{17,9},{10,18},{18,10},{11,19},{19,11},{12,20... | collective-permute-start | bytes 442376 | tf_op jit(solution)/shard_map/ppermute | solution.py:660
  14.9 0.0 collective-permute-done.2.got0
  14.9 3.4 %collective-permute-done.3.got1 = f32[288,128]{1,0:T(8,128)S(1)} collective-permute-done((f32[288,128]{1,0:T(8,128)S(1)}, f32[288,128]{1,0:T(8,128)S(1)}, u32[]{:S(2)}, u32[]{:S(2)}) %collective-permute-start.3) | collective-permute-done | bytes 147488 | tf_op jit(solution)/shard_map/ppermute | solution.py:660
  18.3 5.3 %shard_map.57 = (f32[38,24,128]{2,1,0:T(8,128)S(1)}, f32[38,24,128]{2,1,0:T(8,128)S(1)}, f32[38,24,128]{2,1,0:T(8,128)S(1)}, f32[38,24,128]{2,1,0:T(8,128)S(1)},...) custom-call(f32[512,128]{1,0:T(8,128)S(1)} %get-tuple-element.44.pot, ...), custom_call_target="tpu_custom_call" | custom-call | tf_op jit(solution)/shard_map/pallas_call | solution.py:677
  23.6 0.7 collective-permute-start.5
  24.2 5.2 %collective-permute-start.4 = (f32[208,128]{1,0:T(8,128)S(1)}, f32[208,128]{1,0:T(8,128)S(1)}, u32[]{:S(2)}, u32[]{:S(2)}) collective-permute-start(f32[208,128]{1,0:T(8,128)S(1)} %get-tuple-element.58.m0), channel_id=1, source_target_pairs={{0,1},{1,0},{2,3},{3,2},{4,5},{5,4},{6,7},{7,6},{8,9},{9,8},{10,11... | collective-permute-start | bytes 319496 | tf_op jit(solution)/shard_map/ppermute | solution.py:660
  29.5 0.0 collective-permute-done.5.got1.gy1.refs_20_
  29.5 2.1 %collective-permute-done.4.got0.gy0.refs_19_ = f32[208,128]{1,0:T(8,128)S(1)} collective-permute-done((f32[208,128]{1,0:T(8,128)S(1)}, f32[208,128]{1,0:T(8,128)S(1)}, u32[]{:S(2)}, u32[]{:S(2)}) %collective-permute-start.4) | collective-permute-done | bytes 106528 | tf_op jit(solution)/shard_map/ppermute | solution.py:660
  31.6 0.1 collective-permute-start.6
  31.7 4.2 %collective-permute-start.7 = (f32[304,128]{1,0:T(8,128)S(1)}, f32[304,128]{1,0:T(8,128)S(1)}, u32[]{:S(2)}, u32[]{:S(2)}) collective-permute-start(f32[304,128]{1,0:T(8,128)S(1)} %get-tuple-element.62), channel_id=1, source_target_pairs={{8,16},{16,8},{9,17},{17,9},{10,18},{18,10},{11,19},{19,11},{12,20... | collective-permute-start | bytes 466952 | tf_op jit(solution)/shard_map/ppermute | solution.py:660
  35.9 0.0 collective-permute-done.6.gx0.refs_21_
  35.9 2.9 %collective-permute-done.7.gx1.refs_22_ = f32[304,128]{1,0:T(8,128)S(1)} collective-permute-done((f32[304,128]{1,0:T(8,128)S(1)}, f32[304,128]{1,0:T(8,128)S(1)}, u32[]{:S(2)}, u32[]{:S(2)}) %collective-permute-start.7) | collective-permute-done | bytes 155680 | tf_op jit(solution)/shard_map/ppermute | solution.py:660
  38.8 5.9 %shard_map.59 = (f32[32,24,128]{2,1,0:T(8,128)S(1)}, f32[32,24,128]{2,1,0:T(8,128)S(1)}, f32[32,24,128]{2,1,0:T(8,128)S(1)}, f32[32,24,128]{2,1,0:T(8,128)S(1)},...) custom-call(f32[208,128]{1,0:T(8,128)S(1)} %get-tuple-element.58.m0,, ...), custom_call_target="tpu_custom_call" | custom-call | tf_op jit(solution)/shard_map/pallas_call | solution.py:694
  44.6 18.9 %all_to_all.5 = f32[32,24,128]{2,1,0:T(8,128)S(1)} all-to-all(f32[32,24,128]{2,1,0:T(8,128)S(1)} %get-tuple-element.65), channel_id=1, replica_groups=mesh['gx'=4,'gy'=8] {'gx','gy'}, dimensions={0} | all-to-all | bytes 786432 | tf_op jit(solution)/shard_map/all_to_all | solution.py:706
  63.6 7.7 %finish.1 = f32[512,128]{1,0:T(8,128)} custom-call(f32[4,8,24,128]{3,2,1,0:T(8,128)S(1)} %bitcast.7, f32[32,24,128]{2,1,0:T(8,128)S(1)} %get-tuple-element.66.refs_1_, f32[32,24,128]{2,1,0:T(8,128)S(1)} %get-tuple-element.67.refs_2_, f32[32,24,128]{2,1,0:T(8,128)S(1)} %get-tuple-element.68.refs_3_, f32[32,24,128]{2,1,0:T(8,128)S(1)} %get-tuple-element.69.refs_4_, ...), custom_call_target="tpu_custom_call" | custom-call | tf_op jit(solution)/shard_map/finish/pallas_call | solution.py:713
  (1 shorter events, 0.0 us)
Async XLA Ops:
  1.5 6.0 %collective-permute-start = (f32[320,128]{1,0:T(8,128)S(1)}, f32[320,128]{1,0:T(8,128)S(1)}, u32[]{:S(2)}, u32[]{:S(2)}) collective-permute-start(f32[320,128]{1,0:T(8,128)S(1)} %get-tuple-element.49), channel_id=1, source_target_pairs={{0,1},{1,0},{2,3},{3,2},{4,5},{5,4},{6,7},{7,6},{8,9},{9,8},{10,11... | collective-permute-start | bytes 491528 | tf_op jit(solution)/shard_map/ppermute | solution.py:660
  3.6 3.9 %collective-permute-start.1 = (f32[320,128]{1,0:T(8,128)S(1)}, f32[320,128]{1,0:T(8,128)S(1)}, u32[]{:S(2)}, u32[]{:S(2)}) collective-permute-start(f32[320,128]{1,0:T(8,128)S(1)} %get-tuple-element.50), channel_id=1, source_target_pairs={{1,2},{2,1},{3,4},{4,3},{5,6},{6,5},{9,10},{10,9},{11,12},{12,11},... | collective-permute-start | bytes 491528 | tf_op jit(solution)/shard_map/ppermute | solution.py:660
  7.7 7.2 %collective-permute-start.2 = (f32[288,128]{1,0:T(8,128)S(1)}, f32[288,128]{1,0:T(8,128)S(1)}, u32[]{:S(2)}, u32[]{:S(2)}) collective-permute-start(f32[288,128]{1,0:T(8,128)S(1)} %get-tuple-element.56), channel_id=1, source_target_pairs={{0,8},{8,0},{16,24},{24,16},{1,9},{9,1},{17,25},{25,17},{2,10},{10... | collective-permute-start | bytes 442376 | tf_op jit(solution)/shard_map/ppermute | solution.py:660
  11.8 6.5 %collective-permute-start.3 = (f32[288,128]{1,0:T(8,128)S(1)}, f32[288,128]{1,0:T(8,128)S(1)}, u32[]{:S(2)}, u32[]{:S(2)}) collective-permute-start(f32[288,128]{1,0:T(8,128)S(1)} %get-tuple-element.57), channel_id=1, source_target_pairs={{8,16},{16,8},{9,17},{17,9},{10,18},{18,10},{11,19},{19,11},{12,20... | collective-permute-start | bytes 442376 | tf_op jit(solution)/shard_map/ppermute | solution.py:660
  23.6 5.9 %collective-permute-start.5 = (f32[208,128]{1,0:T(8,128)S(1)}, f32[208,128]{1,0:T(8,128)S(1)}, u32[]{:S(2)}, u32[]{:S(2)}) collective-permute-start(f32[208,128]{1,0:T(8,128)S(1)} %get-tuple-element.59.m1), channel_id=1, source_target_pairs={{1,2},{2,1},{3,4},{4,3},{5,6},{6,5},{9,10},{10,9},{11,12},{12,11},... | collective-permute-start | bytes 319496 | tf_op jit(solution)/shard_map/ppermute | solution.py:660
  24.2 7.3 %collective-permute-start.4 = (f32[208,128]{1,0:T(8,128)S(1)}, f32[208,128]{1,0:T(8,128)S(1)}, u32[]{:S(2)}, u32[]{:S(2)}) collective-permute-start(f32[208,128]{1,0:T(8,128)S(1)} %get-tuple-element.58.m0), channel_id=1, source_target_pairs={{0,1},{1,0},{2,3},{3,2},{4,5},{5,4},{6,7},{7,6},{8,9},{9,8},{10,11... | collective-permute-start | bytes 319496 | tf_op jit(solution)/shard_map/ppermute | solution.py:660
  31.6 4.3 %collective-permute-start.6 = (f32[304,128]{1,0:T(8,128)S(1)}, f32[304,128]{1,0:T(8,128)S(1)}, u32[]{:S(2)}, u32[]{:S(2)}) collective-permute-start(f32[304,128]{1,0:T(8,128)S(1)} %get-tuple-element.61), channel_id=1, source_target_pairs={{0,8},{8,0},{16,24},{24,16},{1,9},{9,1},{17,25},{25,17},{2,10},{10... | collective-permute-start | bytes 466952 | tf_op jit(solution)/shard_map/ppermute | solution.py:660
  31.7 7.1 %collective-permute-start.7 = (f32[304,128]{1,0:T(8,128)S(1)}, f32[304,128]{1,0:T(8,128)S(1)}, u32[]{:S(2)}, u32[]{:S(2)}) collective-permute-start(f32[304,128]{1,0:T(8,128)S(1)} %get-tuple-element.62), channel_id=1, source_target_pairs={{8,16},{16,8},{9,17},{17,9},{10,18},{18,10},{11,19},{19,11},{12,20... | collective-permute-start | bytes 466952 | tf_op jit(solution)/shard_map/ppermute | solution.py:660

commit v3 on v2

--- a/solution.py
+++ b/solution.py
@@ -7,14 +7,14 @@
 
 F32 = jnp.float32
 BX, BY, NL = 32, 16, 128
-H0 = 3
-FX_ = BX + 2 * H0
 YE = 24
 X1 = BX // 2
 H1 = 8
 G1 = X1 + 2 * H1
-GF = 4
-GM = 6
+NF = X1 + 4
+NM = G1 // 2 + 2
+GF = 3
+GM = 4
 LN2 = 0.6931471805599453
 
 
@@ -148,39 +148,42 @@
     return scr * (up - down), scr * (up + down)
 
 
-def beside_of(v, fa, at, n, zstep):
-    fx, fyp, fym, fzp, fzm = fa
+def colour_mask(n, zstep):
+    shape = (n, YE, NL)
+    return (iota(shape, 1) + iota(shape, 2) // zstep) % 2 == 0
+
+
+def beside_of(other, colour, faces, at, n, zstep):
+    fin, fout, fyp, fym, fzp, fzm = faces
     here = pl.ds(at, n)
-    f = fx[pl.ds(at - 1, n + 1)]
+    v = other[1 - colour, pl.ds(at - 1, n + 2)]
     mid = v[1 : n + 1]
+    first = colour_mask(n, zstep)
+    across = jnp.where(first, v[:n], v[2:]) if colour == 0 else jnp.where(first, v[2:], v[:n])
     return (
-        (f[1:] * v[2:] + f[:n] * v[:n])
-        + (fyp[here] * rot(mid, -1, 1) + fym[here] * rot(mid, 1, 1))
-        + (fzp[here] * rot(mid, -zstep, 2) + fzm[here] * rot(mid, zstep, 2))
+        (fin[here] * mid + fout[colour, here] * across)
+        + (fyp[colour, here] * rot(mid, -1, 1) + fym[colour, here] * rot(mid, 1, 1))
+        + (fzp[colour, here] * rot(mid, -zstep, 2) + fzm[colour, here] * rot(mid, zstep, 2))
     )
 
 
-def checker(at, n, shift, zstep):
-    shape = (n, YE, NL)
-    return (iota(shape, 0) + iota(shape, 1) + iota(shape, 2) // zstep + (at + shift)) % 2
-
-
-def planes_of(u, at, n, refs):
-    c, fx, fyp, fym, fzp, fzm, src, scr, _ = refs
+def pairs_of(u, at, n, colour, refs):
+    c, fin, fout, fyp, fym, fzp, fzm, src, scr, _ = refs
     here = pl.ds(at, n)
-    v = u[pl.ds(at - 1, n + 2)]
-    plane = v[1 : n + 1]
-    sh, ch = nonlinear(plane, scr[here])
-    centre = c[here]
-    value = centre * plane - beside_of(v, (fx, fyp, fym, fzp, fzm), at, n, 1) + sh - src[here]
-    return plane, value, centre, ch
+    plane = u[colour, here]
+    sh, ch = nonlinear(plane, scr[colour, here])
+    centre = c[colour, here]
+    beside = beside_of(u, colour, (fin, fout, fyp, fym, fzp, fzm), at, n, 1)
+    return plane, centre * plane - beside + sh - src[colour, here], centre, ch
+
+
+def fine_new(u, at, n, colour, refs):
+    plane, value, centre, ch = pairs_of(u, at, n, colour, refs)
+    return jnp.where(refs[-1][colour, pl.ds(at, n)] > 0.5, plane - value / (centre + ch), plane)
 
 
 def fine_half(u, at, n, colour, refs):
-    plane, value, centre, ch = planes_of(u, at, n, refs)
-    update = plane - value / (centre + ch)
-    keep = (checker(at, n, 1, 1) == colour) & (refs[-1][pl.ds(at, n)] > 0.5)
-    u[pl.ds(at, n)] = jnp.where(keep, update, plane)
+    u[colour, pl.ds(at, n)] = fine_new(u, at, n, colour, refs)
 
 
 def groups(first, count, n, step):
@@ -193,17 +196,23 @@
     lax.fori_loop(0, count // n, one, 0)
 
 
-def faces_of(p, at, n, scale, zstep, fx, fyp, fym, fzp, fzm):
+def faces_of(p, at, n, scale, zstep, fin, fout, fyp, fym, fzp, fzm):
     here = pl.ds(at, n)
     lane = iota((n, YE, NL), 2)
-    v = p[pl.ds(at, n + 1)]
-    plane = v[:n]
+    first = colour_mask(n, zstep)
     half = F32(0.5 * scale)
-    fx[here] = half * (plane + v[1:])
-    fyp[here] = half * (plane + rot(plane, -1, 1))
-    fym[here] = half * (plane + rot(plane, 1, 1))
-    fzp[here] = jnp.where(lane >= NL - zstep, F32(0.0), half * (plane + rot(plane, -zstep, 2)))
-    fzm[here] = jnp.where(lane < zstep, F32(0.0), half * (plane + rot(plane, zstep, 2)))
+    for colour in (0, 1):
+        plane = p[colour, here]
+        v = p[1 - colour, pl.ds(at - 1, n + 2)]
+        mid = v[1 : n + 1]
+        across = jnp.where(first, v[:n], v[2:]) if colour == 0 else jnp.where(first, v[2:], v[:n])
+        if colour == 0:
+            fin[here] = half * (plane + mid)
+        fout[colour, here] = half * (plane + across)
+        fyp[colour, here] = half * (plane + rot(mid, -1, 1))
+        fym[colour, here] = half * (plane + rot(mid, 1, 1))
+        fzp[colour, here] = jnp.where(lane >= NL - zstep, F32(0.0), half * (plane + rot(mid, -zstep, 2)))
+        fzm[colour, here] = jnp.where(lane < zstep, F32(0.0), half * (plane + rot(mid, zstep, 2)))
 
 
 def lane_pairs(value, step):
@@ -212,70 +221,78 @@
 
 
 def fine_pre(pot, per, src, scr, fix, hpot, hper, hsrc, hscr, hfree, got0, got1,
-             u, c, fx, fyp, fym, fzp, fzm, esrc, escr, efree, c1, g1, m0, m1,
+             u, c, fin, fout, fyp, fym, fzp, fzm, esrc, escr, efree, csum, g1, m0, m1,
              ep, tr, tc, tp, p1):
     gots, outs = (got0, got1), (m0, m1)
-
-    def own(x, _):
-        i = x + H0
-        at = pl.multiple_of(x * BY, 8)
-        ht = pl.multiple_of(x * 8, 8)
+    first = colour_mask(1, 1)[0]
+
+    def own(k, _):
         for ref, h, ext in ((pot, hpot, u), (per, hper, ep), (src, hsrc, esrc), (scr, hscr, escr), (fix, hfree, efree)):
-            value = ref[pl.ds(at, BY), :]
+            value = ref[pl.ds(pl.multiple_of(2 * k * BY, 8), 2 * BY), :]
             if ref is fix:
                 value = jnp.where(value == 0, F32(1.0), F32(0.0))
-            ext[i, 0:BY, :] = value
-            ext[i, BY:YE, :] = h[pl.ds(ht, 8), :]
-        return 0
-
-    lax.fori_loop(0, BX, own, 0, unroll=4)
-
-    def place(got, planes):
+            halo = h[pl.ds(pl.multiple_of(16 * k, 8), 16), :]
+            for rows, one, two in (
+                (slice(0, BY), value[:BY], value[BY:]),
+                (slice(BY, YE), halo[:8], halo[8:]),
+            ):
+                ext[0, k + 2, rows, :] = jnp.where(first[rows], one, two)
+                ext[1, k + 2, rows, :] = jnp.where(first[rows], two, one)
+        return 0
+
+    lax.fori_loop(0, X1, own, 0, unroll=2)
+
+    def place(got, near, far, flip):
         k = 0
         for ext, depth in ((u, 3), (ep, 3), (esrc, 2), (escr, 2), (efree, 2)):
-            for i in planes[:depth]:
-                ext[i] = got[YE * k : YE * (k + 1), :]
-                k += 1
+            planes = [got[YE * (k + j) : YE * (k + j + 1), :] for j in range(depth)]
+            k += depth
+            one, two = (planes[1], planes[0]) if flip else (planes[0], planes[1])
+            ext[0, near] = jnp.where(first, one, two)
+            ext[1, near] = jnp.where(first, two, one)
+            third = planes[2] if depth == 3 else jnp.zeros((YE, NL), F32)
+            ext[0, far] = third
+            ext[1, far] = third
 
     def action_x(hi, lo):
-        place(gots[hi], (BX + H0, BX + H0 + 1, BX + H0 + 2))
-        place(gots[lo], (H0 - 1, H0 - 2, H0 - 3))
+        place(gots[hi], X1 + 2, X1 + 3, False)
+        place(gots[lo], 1, 0, True)
 
     by_parity("gx", action_x)
-    for ext in (esrc, escr, efree):
-        ext[0] = jnp.zeros((YE, NL), F32)
-        ext[FX_ - 1] = jnp.zeros((YE, NL), F32)
-
-    fx[0] = F32(0.5) * (ep[0] + ep[1])
-    refs = (c, fx, fyp, fym, fzp, fzm, esrc, escr, efree)
-
-    def first(at):
+    refs = (c, fin, fout, fyp, fym, fzp, fzm, esrc, escr, efree)
+
+    def begin(at):
         n = GF
-        faces_of(ep, at, n, 1.0, 1, fx, fyp, fym, fzp, fzm)
+        faces_of(ep, at, n, 1.0, 1, fin, fout, fyp, fym, fzp, fzm)
         here = pl.ds(at, n)
         lane = iota((n, YE, NL), 2)
-        ends = jnp.where((lane == 0) | (lane == NL - 1), F32(0.5) * ep[here], F32(0.0))
-        f = fx[pl.ds(at - 1, n + 1)]
-        c[here] = (f[1:] + f[:n]) + (fyp[here] + fym[here]) + (fzp[here] + fzm[here]) + ends
+        for colour in (0, 1):
+            ends = jnp.where((lane == 0) | (lane == NL - 1), F32(0.5) * ep[colour, here], F32(0.0))
+            c[colour, here] = (
+                (fin[here] + fout[colour, here]) + (fyp[colour, here] + fym[colour, here])
+                + (fzp[colour, here] + fzm[colour, here]) + ends
+            )
         fine_half(u, at, n, 0, refs)
 
-    groups(1, FX_ - 2, GF, first)
-    groups(1, FX_ - 2, GF, lambda at: fine_half(u, at, GF, 1, refs))
+    groups(1, X1 + 2, GF, begin)
+    groups(1, X1 + 2, GF, lambda at: fine_half(u, at, GF, 1, refs))
 
     def down(at):
-        n = 4
-        _, value, _, ch = planes_of(u, at, n, refs)
-        left = jnp.where(efree[pl.ds(at, n)] > 0.5, -value, F32(0.0))
-        for a in range(0, n, 2):
-            to = pl.multiple_of((at - H0 + a) * (BY // 2), 8)
-            tr[pl.ds(to, BY), :] = lane_pairs(left[a, 0:BY] + left[a + 1, 0:BY], 1)
-            tc[pl.ds(to, BY), :] = lane_pairs(ch[a, 0:BY] + ch[a + 1, 0:BY], 1)
-
-    groups(H0, BX, 4, down)
+        n = 2
+        left, react = F32(0.0), F32(0.0)
+        for colour in (0, 1):
+            _, value, _, ch = pairs_of(u, at, n, colour, refs)
+            left += jnp.where(efree[colour, pl.ds(at, n)] > 0.5, -value, F32(0.0))
+            react += ch
+        to = pl.multiple_of((at - 2) * BY, 8)
+        tr[pl.ds(to, n * BY), :] = lane_pairs(left[:, 0:BY], 1).reshape(n * BY, NL)
+        tc[pl.ds(to, n * BY), :] = lane_pairs(react[:, 0:BY], 1).reshape(n * BY, NL)
+
+    groups(2, X1, 2, down)
 
     def coarse_p(k, _):
         at = pl.multiple_of(k * YE, 8)
-        tp[pl.ds(at, YE), :] = lane_pairs(ep[2 * k + 1] + ep[2 * k + 2], 1)
+        tp[pl.ds(at, YE), :] = lane_pairs(ep[0, k + 1] + ep[1, k + 1], 1)
         return 0
 
     lax.fori_loop(0, X1 + 2, coarse_p, 0, unroll=2)
@@ -290,7 +307,9 @@
 
     lax.fori_loop(0, X1 + 2, gather_p, 0, unroll=2)
 
-    def make(x1, _):
+    first8 = (sub + lane // 2) % 2 == 0
+
+    def coarse(x1):
         k = x1 + 1
         p = p1[k]
         base = k * YE
@@ -306,27 +325,30 @@
         r = eighth * (tr[pl.ds(at, 8, stride=2), :] + tr[pl.ds(at + 1, 8, stride=2), :])
         react = eighth * (tc[pl.ds(at, 8, stride=2), :] + tc[pl.ds(at + 1, 8, stride=2), :])
         diag = F32(0.25) * centre + react
-        c1[x1] = react
-        g1[x1] = diag
         message = jnp.where(lane % 2 == 0, r, F32(1.0) / diag)
         m0[pl.ds(pl.multiple_of(x1 * 8, 8), 8), :] = message
         m1[pl.ds(pl.multiple_of(x1 * 8, 8), 8), :] = message
-        return 0
-
-    lax.fori_loop(0, X1, make, 0, unroll=2)
+        return diag, react
+
+    def make(k, _):
+        diag0, react0 = coarse(2 * k)
+        diag1, react1 = coarse(2 * k + 1)
+        csum[k] = react0 + react1
+        g1[0, k] = jnp.where(first8, diag0, diag1)
+        g1[1, k] = jnp.where(first8, diag1, diag0)
+        return 0
+
+    lax.fori_loop(0, X1 // 2, make, 0)
 
     for a in range(X1 // 2):
         message = jnp.where(lane % 2 == 0, p1[1 + 2 * a], p1[2 + 2 * a])
         for m in outs:
             m[X1 * 8 + 8 * a : X1 * 8 + 8 * a + 8, :] = message
 
-    zl = iota((BX // 2, NL), 1)
     base = X1 * 8 + X1 * 4
 
     def odd_row(out, y):
-        even = u[pl.ds(H0, BX // 2, stride=2), y, :]
-        odd = u[pl.ds(H0 + 1, BX // 2, stride=2), y, :]
-        out[base : base + BX // 2, :] = jnp.where((y + zl) % 2 == 1, even, odd)
+        out[base : base + X1, :] = u[1, pl.ds(2, X1), y, :]
 
     def action_y(hi, lo):
         odd_row(outs[hi], BY - 2)
@@ -355,11 +377,11 @@
                 for ref in (own, gots[hi], gots[lo]):
                     out[at : at + 8, :] = ref[row : row + 8, :]
                     at += 8
-            out[at : at + BY, :] = u[x + H0, 0:BY, :]
+            out[at : at + BY, :] = u[1, x, 0:BY, :]
 
         def action(xhi, xlo):
-            slab(outs[xhi], X1 - H1, BX - 2)
-            slab(outs[xlo], 0, 1)
+            slab(outs[xhi], X1 - H1, X1 + 1)
+            slab(outs[xlo], 0, 2)
 
         by_parity("gx", action)
 
@@ -372,11 +394,9 @@
         go(1, 0)
 
 
-def coarse_half(e, r, d, at, n, colour, refs, zstep):
-    v = e[pl.ds(at - 1, n + 2)]
+def coarse_half(e, r, d, at, n, colour, faces, zstep):
     here = pl.ds(at, n)
-    update = (r[here] + beside_of(v, refs, at, n, zstep)) * d[here]
-    e[here] = jnp.where(checker(at, n, 0, zstep) == colour, update, v[1 : n + 1])
+    e[colour, here] = (r[colour, here] + beside_of(e, colour, faces, at, n, zstep)) * d[colour, here]
 
 
 def dup_even(value):
@@ -389,31 +409,33 @@
     return jnp.where(lane % 2 == 1, value, rot(value, -1, value.ndim - 1))
 
 
-def mid_pre(m0, gy0, gy1, gx0, gx1, c1, g1,
-            e, r, d, fx, fyp, fym, fzp, fzm, msg,
+def mid_pre(m0, gy0, gy1, gx0, gx1, csum, g1,
+            e, r, d, fin, fout, fyp, fym, fzp, fzm, msg,
             p, t, tr, tc, pc):
     gys, gxs = (gy0, gy1), (gx0, gx1)
     odd_y = lax.axis_index("gy") % 2
+    first = colour_mask(1, 2)[0]
+
+    def put(k, rows, one, two, both):
+        mask = first[rows]
+        for colour in (0, 1):
+            a, b = (one, two) if colour == 0 else (two, one)
+            value = jnp.where(mask, a, b)
+            r[colour, k, rows, :] = dup_even(value)
+            d[colour, k, rows, :] = dup_odd(value)
+        a, b = dup_even(both), dup_odd(both)
+        p[0, k, rows, :] = jnp.where(mask, a, b)
+        p[1, k, rows, :] = jnp.where(mask, b, a)
 
     def own(hi, lo):
-        def planes(a, _):
-            rows = [ref[pl.ds(pl.multiple_of(8 * a, 8), 8), :] for ref in (m0, gys[hi], gys[lo])]
-            for k, value in enumerate(rows):
-                r[H1 + a, 8 * k : 8 * k + 8, :] = dup_even(value)
-                d[H1 + a, 8 * k : 8 * k + 8, :] = dup_odd(value)
+        def pairs(k, _):
+            for j, ref in enumerate((m0, gys[hi], gys[lo])):
+                two = ref[pl.ds(pl.multiple_of(16 * k, 8), 16), :]
+                both = ref[pl.ds(pl.multiple_of(X1 * 8 + 8 * k, 8), 8), :]
+                put(1 + H1 // 2 + k, slice(8 * j, 8 * j + 8), two[:8], two[8:], both)
             return 0
 
-        lax.fori_loop(0, X1, planes, 0, unroll=2)
-
-        def coefs(a, _):
-            at = pl.multiple_of(X1 * 8 + 8 * a, 8)
-            for k, ref in enumerate((m0, gys[hi], gys[lo])):
-                value = ref[pl.ds(at, 8), :]
-                p[H1 + 2 * a, 8 * k : 8 * k + 8, :] = dup_even(value)
-                p[H1 + 2 * a + 1, 8 * k : 8 * k + 8, :] = dup_odd(value)
-            return 0
-
-        lax.fori_loop(0, X1 // 2, coefs, 0, unroll=2)
+        lax.fori_loop(0, X1 // 2, pairs, 0, unroll=2)
 
     @pl.when(odd_y == 0)
     def _():
@@ -423,53 +445,52 @@
     def _():
         own(1, 0)
 
-    def beyond(ref, first):
-        def planes(a, _):
-            value = ref[pl.ds(pl.multiple_of(YE * a, 8), YE), :]
-            r[first + a] = dup_even(value)
-            d[first + a] = dup_odd(value)
+    def beyond(ref, at):
+        def pairs(k, _):
+            one = ref[pl.ds(pl.multiple_of(2 * YE * k, 8), YE), :]
+            two = ref[pl.ds(pl.multiple_of(2 * YE * k + YE, 8), YE), :]
+            both = ref[pl.ds(pl.multiple_of(H1 * YE + YE * k, 8), YE), :]
+            put(at + k, slice(0, YE), one, two, both)
             return 0
 
-        lax.fori_loop(0, H1, planes, 0, unroll=2)
-        for a in range(H1 // 2):
-            value = ref[H1 * YE + YE * a : H1 * YE + YE * (a + 1), :]
-            p[first + 2 * a] = dup_even(value)
-            p[first + 2 * a + 1] = dup_odd(value)
+        lax.fori_loop(0, H1 // 2, pairs, 0, unroll=2)
 
     def action(hi, lo):
-        beyond(gxs[hi], H1 + X1)
-        beyond(gxs[lo], 0)
+        beyond(gxs[hi], 1 + H1 // 2 + X1 // 2)
+        beyond(gxs[lo], 1)
 
     by_parity("gx", action)
-
-    p[G1] = jnp.zeros((YE, NL), F32)
-    refs = (fx, fyp, fym, fzp, fzm)
+    for ref in (p, e):
+        for colour in (0, 1):
+            ref[colour, 0] = jnp.zeros((YE, NL), F32)
+            ref[colour, NM - 1] = jnp.zeros((YE, NL), F32)
+    faces = (fin, fout, fyp, fym, fzp, fzm)
 
     def begin(at):
-        n = 4
+        here = pl.ds(at, 2)
+        faces_of(p, at, 2, 0.25, 2, *faces)
+        e[0, here] = r[0, here] * d[0, here]
+
+    groups(1, NM - 2, 2, begin)
+    for colour in (1, 0, 1):
+        groups(1, NM - 2, GM, lambda at, colour=colour: coarse_half(e, r, d, at, GM, colour, faces, 2))
+
+    def down(at):
+        n = 2
         here = pl.ds(at, n)
-        faces_of(p, at, n, 0.25, 2, fx, fyp, fym, fzp, fzm)
-        e[here] = jnp.where(checker(at, n, 0, 2) == 0, r[here] * d[here], F32(0.0))
-
-    groups(0, G1, 4, begin)
-    for colour in (1, 0, 1):
-        groups(1, G1 - 2, GM, lambda at, colour=colour: coarse_half(e, r, d, at, GM, colour, refs, 2))
-
-    def down(at):
-        n = 4
-        v = e[pl.ds(at - 1, n + 2)]
-        here = pl.ds(at, n)
-        left = (r[here] + beside_of(v, refs, at, n, 2))[:, 0:8] - g1[pl.ds(at - H1, n)] * v[1 : n + 1, 0:8]
-        react = c1[pl.ds(at - H1, n)]
-        for a in range(0, n, 2):
-            to = pl.multiple_of((at - H1 + a) * 4, 8)
-            tr[pl.ds(to, 8), :] = lane_pairs(left[a] + left[a + 1], 2)
-            tc[pl.ds(to, 8), :] = lane_pairs(react[a] + react[a + 1], 2)
-
-    groups(H1, X1, 4, down)
+        k = pl.ds(at - 1 - H1 // 2, n)
+        left = F32(0.0)
+        for colour in (0, 1):
+            part = r[colour, here] + beside_of(e, colour, faces, at, n, 2)
+            left += part[:, 0:8] - g1[colour, k] * e[colour, here, 0:8, :]
+        to = pl.multiple_of((at - 1 - H1 // 2) * 8, 8)
+        tr[pl.ds(to, n * 8), :] = lane_pairs(left, 2).reshape(n * 8, NL)
+        tc[pl.ds(to, n * 8), :] = lane_pairs(csum[k], 2).reshape(n * 8, NL)
+
+    groups(1 + H1 // 2, X1 // 2, 2, down)
 
     def coarse_p(x2, _):
-        t[pl.ds(pl.multiple_of(x2 * YE, 8), YE), :] = lane_pairs(p[2 * x2] + p[2 * x2 + 1], 2)
+        t[pl.ds(pl.multiple_of(x2 * YE, 8), YE), :] = lane_pairs(p[0, x2 + 1] + p[1, x2 + 1], 2)
         return 0
 
     lax.fori_loop(0, G1 // 2, coarse_p, 0, unroll=2)
@@ -510,10 +531,10 @@
     lax.fori_loop(0, msg.shape[0], every, 0)
 
 
-def finish(at, got, e, r, d, fx1, fyp1, fym1, fzp1, fzm1,
-           u, c, fx, fyp, fym, fzp, fzm, src, scr, free, gy0, gy1, gx0, gx1,
+def finish(at, got, e, r, d, fin1, fout1, fyp1, fym1, fzp1, fzm1,
+           before, c, fin, fout, fyp, fym, fzp, fzm, src, scr, free, gy0, gy1, gx0, gx1,
            result,
-           e2, p2, r2, d2, k2, tx, eu):
+           e2, p2, r2, d2, k2, tx, eu, u, hal):
     wx, wy = got.shape[0], got.shape[1]
     rows = wx * 8
     e2[...] = jnp.zeros_like(e2)
@@ -591,63 +612,79 @@
 
     def correct(x2, _):
         value = tx[pl.ds(pl.multiple_of(x2 * YE, 8), YE), :]
-        eu[2 * x2] = e[2 * x2] + value
-        eu[2 * x2 + 1] = e[2 * x2 + 1] + value
-        return 0
-
-    lax.fori_loop(1, G1 // 2 - 1, correct, 0, unroll=2)
-    refs1 = (fx1, fyp1, fym1, fzp1, fzm1)
-    for first, count, colour in ((4, 24, 0), (4, 24, 1), (4, 24, 0), (7, 18, 1)):
-        groups(first, count, GM, lambda at, colour=colour: coarse_half(eu, r, d, at, GM, colour, refs1, 2))
+        for colour in (0, 1):
+            eu[colour, x2 + 1] = e[colour, x2 + 1] + value
+        return 0
+
+    lax.fori_loop(0, G1 // 2, correct, 0, unroll=2)
+    faces1 = (fin1, fout1, fyp1, fym1, fzp1, fzm1)
+    for at1, count, n, colour in ((3, 12, 4, 0), (3, 12, 4, 1), (4, 10, 5, 0), (4, 10, 5, 1)):
+        groups(at1, count, n, lambda at, n=n, colour=colour: coarse_half(eu, r, d, at, n, colour, faces1, 2))
 
     base = X1 * 8 + X1 * 4
 
-    def rows_y(got_, y):
-        value = got_[base : base + BX // 2, :]
-        u[pl.ds(H0, BX // 2, stride=2), y, :] = value
-        u[pl.ds(H0 + 1, BX // 2, stride=2), y, :] = value
-
     def action_y(hi, lo):
-        rows_y((gy0, gy1)[hi], BY + 1)
-        rows_y((gy0, gy1)[lo], YE - 2)
+        hal[pl.ds(1, X1, stride=8), :] = (gy0, gy1)[hi][base : base + X1, :]
+        hal[pl.ds(6, X1, stride=8), :] = (gy0, gy1)[lo][base : base + X1, :]
 
     by_parity("gy", action_y)
-
-    def action_x(hi, lo):
-        u[H0 + BX + 1, 0:BY, :] = (gx0, gx1)[hi][XMSG - BY : XMSG, :]
-        u[H0 - 2, 0:BY, :] = (gx0, gx1)[lo][XMSG - BY : XMSG, :]
-
-    by_parity("gx", action_x)
-
-    def add(k, _):
-        plane = eu[k + H1 - 1]
+    first = colour_mask(1, 1)[0]
+    first1 = colour_mask(1, 2)[0]
+    s8 = iota((8, NL), 0)
+    added = (s8 == 1) | (s8 == 6)
+    own_rows = slice(0, BY)
+
+    def widen(k, plane, now1, halo1):
         for y in (0, 1):
             tx[pl.ds(k * YE + y, 8, stride=2), :] = plane[0:8]
         wide = tx[pl.ds(pl.multiple_of(k * YE, 8), BY), :]
-        s8 = iota((8, NL), 0)
-        hi = plane[8:16]
-        lo = plane[16:24]
+        hi, lo = plane[8:16], plane[16:24]
         halo = jnp.where(s8 < 2, jnp.where(s8 == 0, hi, rot(hi, 1, 0)), jnp.where(s8 == 7, lo, rot(lo, -1, 0)))
-        for z in (0, 1):
-            i = 2 * k + z + H0 - 2
-            u[i, 0:BY, :] = jnp.where(free[i, 0:BY, :] > 0.5, u[i, 0:BY, :] + wide, u[i, 0:BY, :])
-            u[i, BY:YE, :] = jnp.where(free[i, BY:YE, :] > 0.5, u[i, BY:YE, :] + halo, u[i, BY:YE, :])
-        return 0
-
-    lax.fori_loop(0, X1 + 2, add, 0, unroll=2)
-    refs = (c, fx, fyp, fym, fzp, fzm, src, scr, free)
-
-    groups(1, FX_ - 2, GF, lambda at: fine_half(u, at, GF, 0, refs))
+        now = ((before[0, k, own_rows, :], before[0, k, BY:YE, :]), (now1, halo1))
+        for colour in (0, 1):
+            one, two = now[colour]
+            u[colour, k, own_rows, :] = jnp.where(free[colour, k, own_rows, :] > 0.5, one + wide, one)
+            u[colour, k, BY:YE, :] = jnp.where(free[colour, k, BY:YE, :] > 0.5, two + halo, two)
+
+    def level1_plane(m, second):
+        one, two = (eu[1, m], eu[0, m]) if second else (eu[0, m], eu[1, m])
+        return jnp.where(first1, one, two)
+
+    def add(m, _):
+        for second in (0, 1):
+            k = 2 * m + second + 2
+            halo = jnp.where(added, hal[pl.ds(pl.multiple_of(8 * (k - 2), 8), 8), :], before[1, k, BY:YE, :])
+            widen(k, level1_plane(m + 1 + H1 // 2, second), before[1, k, own_rows, :], halo)
+        return 0
+
+    lax.fori_loop(0, X1 // 2, add, 0)
+
+    def action_x(hi, lo):
+        row = (gx0, gx1)[hi][XMSG - BY : XMSG, :]
+        k = X1 + 2
+        now = jnp.where(first[own_rows], row, before[1, k, own_rows, :])
+        widen(k, level1_plane(1 + H1 // 2 + X1 // 2, 0), now, before[1, k, BY:YE, :])
+        row = (gx0, gx1)[lo][XMSG - BY : XMSG, :]
+        now = jnp.where(first[own_rows], before[1, 1, own_rows, :], row)
+        widen(1, level1_plane(H1 // 2, 1), now, before[1, 1, BY:YE, :])
+
+    by_parity("gx", action_x)
+    for k in (0, NF - 1):
+        u[1, k] = before[1, k]
+    refs = (c, fin, fout, fyp, fym, fzp, fzm, src, scr, free)
+    groups(1, X1 + 2, GF, lambda at: fine_half(u, at, GF, 0, refs))
 
     def last(at):
-        n = 4
-        plane, value, centre, ch = planes_of(u, at, n, refs)
-        update = plane - value / (centre + ch)
-        keep = (checker(at, n, 1, 1) == 1) & (free[pl.ds(at, n)] > 0.5)
-        out = jnp.where(keep, update, plane)[:, 0:BY]
-        result[pl.ds(pl.multiple_of((at - H0) * BY, 8), n * BY), :] = out.reshape(n * BY, NL)
-
-    groups(H0, BX, 4, last)
+        n = 2
+        new = fine_new(u, at, n, 1, refs)[:, own_rows]
+        even = u[0, pl.ds(at, n), own_rows, :]
+        mask = first[own_rows]
+        for k in range(n):
+            to = pl.multiple_of((at - 2 + k) * 2 * BY, 8)
+            result[pl.ds(to, BY), :] = jnp.where(mask, even[k], new[k])
+            result[pl.ds(to + BY, BY), :] = jnp.where(mask, new[k], even[k])
+
+    groups(2, X1, 2, last)
 
 
 def swap(pair, axis):
@@ -673,10 +710,11 @@
     *halos, x0, x1 = call(pack_x, (sds(BX * 8, NL),) * 5 + (sds(12 * YE, NL),) * 2)(*args, *y0)
     gotx = swap((x0, x1), "gx")
 
-    ext = (FX_, YE, NL)
+    ext, one = (2, NF, YE, NL), (NF, YE, NL)
     fine = call(
         fine_pre,
-        (sds(*ext),) * 10 + (sds(X1, 8, NL),) * 2 + (sds(YMSG, NL),) * 2,
+        (sds(*ext),) * 2 + (sds(*one),) + (sds(*ext),) * 8
+        + (sds(X1 // 2, 8, NL), sds(2, X1 // 2, 8, NL)) + (sds(YMSG, NL),) * 2,
         [
             pltpu.VMEM(ext, F32),
             pltpu.VMEM((X1 * BY, NL), F32),
@@ -685,17 +723,17 @@
             pltpu.VMEM((X1 + 2, 8, NL), F32),
         ],
     )(*args, *halos, *gotx)
-    state, (c1, g1, m0, m1) = fine[:10], fine[10:]
+    state, (c1, g1, m0, m1) = fine[:11], fine[11:]
     goty1 = swap((m0, m1), "gy")
     x1msg = call(pack_x1, (sds(XMSG, NL),) * 2)(m0, m1, *goty1, state[0])
     gotx1 = swap(x1msg, "gx")
 
-    mid = (G1, YE, NL)
+    mid, mid1 = (2, NM, YE, NL), (NM, YE, NL)
     *level1, message = call(
         mid_pre,
-        (sds(*mid),) * 8 + (sds(gx * gy, 24, NL),),
+        (sds(*mid),) * 3 + (sds(*mid1),) + (sds(*mid),) * 5 + (sds(gx * gy, 24, NL),),
         [
-            pltpu.VMEM((G1 + 1, YE, NL), F32),
+            pltpu.VMEM(mid, F32),
             pltpu.VMEM((G1 // 2 * YE, NL), F32),
             pltpu.VMEM((X1 // 2 * 8, NL), F32),
             pltpu.VMEM((X1 // 2 * 8, NL), F32),
@@ -719,9 +757,10 @@
             pltpu.VMEM((wy, wx * 8, NL), F32),
             pltpu.VMEM((wy, wx * 8, NL), F32),
             pltpu.VMEM((6, wy, wx * 8, NL), F32),
-            pltpu.VMEM(((X1 + 2) * YE, NL), F32),
+            pltpu.VMEM((NF * YE, NL), F32),
             pltpu.VMEM(mid, F32),
             pltpu.VMEM(ext, F32),
+            pltpu.VMEM((BX // 2 * 8, NL), F32),
         ],
         compiler_params=pltpu.CompilerParams(vmem_limit_bytes=24 << 20),
         name="finish",
@@ -739,10 +778,6 @@
 def finish_kernel(count, sizes):
     def kernel(*refs):
         ins, result, scratch = list(refs[:count]), refs[count], list(refs[1 + count :])
-        field = scratch.pop()
-        before = ins[9]
-        field[...] = before[...]
-        ins[9] = field
         finish(window(*sizes)[2:], *ins, result, *scratch)
 
     return kernel

time: 72.2 us -> 68.7 us (0.952)
  Pallas kernels: 20.5 us -> 17 us
    pallas_call x2, Pallas kernels: 11.2 us -> 8.97 us  [the longest x1 4.52 us: body(): call(fine_pre, (sds(*ext),) * 2 + (sds(*one),) + (sds(*ext),) * 8 + (sds(...]
    pallas_call x1, Pallas kernels: 7.66 us -> 6.35 us  [body(): pl.pallas_call(finish_kernel(len(inputs), (gx, gy, wx, wy)), out_shape=sd...]
where the time goes in v3:
time: 68.7 us; the launch traced here: 67.8 us
  starting transfers between devices  20.1 us (29%)
  blocking collectives  18.9 us (28%)
  Pallas kernels  17 us (25%)
  waiting for transfers between devices  11.6 us (17%)
    ppermute x8, starting transfers between devices, swap(): got[first] = lax.ppermute(pair[first], axis, route)  20.1 us
    all_to_all x1, blocking collectives, body(): lax.all_to_all(message, ('gx', 'gy'), 0, 0).reshape(gx, gy, 24, NL)  18.9 us
    ppermute x8, waiting for transfers between devices, swap(): got[first] = lax.ppermute(pair[first], axis, route)  11.6 us
    pallas_call x1, Pallas kernels, body(): pl.pallas_call(finish_kernel(len(inputs), (gx, gy, wx, wy)), out_shape=sd...  6.35 us
    pallas_call x1, Pallas kernels, body(): call(fine_pre, (sds(*ext),) * 2 + (sds(*one),) + (sds(*ext),) * 8 + (sds(...  4.52 us
    pallas_call x1, Pallas kernels, body(): call(mid_pre, (sds(*mid),) * 3 + (sds(*mid1),) + (sds(*mid),) * 5 + (sds(...  4.45 us
    pallas_call x1, Pallas kernels, body(): call(pack_y, whole + (sds(10 * BX, NL),) * 2, [pltpu.SemaphoreType.DMA((5...  1.49 us
  transfers between devices with their start and end apart: 8, of which 4 were waited for; matrix products, arithmetic and copies ran while one was open for 0% of the time, Pallas kernels for 0%

profile of v3, /device:TPU:1, one launch (start us, length us, event | category | flops | bytes accessed | tf_op | source)
XLA Modules:
  0.0 67.8 jit_solution(590596684722079757)
XLA Ops:
  0.0 1.5 %shard_map.55 = (f32[512,128]{1,0:T(8,128)S(1)}, f32[512,128]{1,0:T(8,128)S(1)}, f32[512,128]{1,0:T(8,128)S(1)}, f32[512,128]{1,0:T(8,128)S(1)}, s32[512,128]{1,...) custom-call(f32[512,128]{1,0:T(8,128)} %bitcast.8, f32[512,128]{1,0:T(8,128)} %bitcast.9, ...), custom_call_target="tpu_custom_call" | custom-call | tf_op jit(solution)/shard_map/pallas_call | solution.py:707
  1.5 2.1 %collective-permute-start = (f32[320,128]{1,0:T(8,128)S(1)}, f32[320,128]{1,0:T(8,128)S(1)}, u32[]{:S(2)}, u32[]{:S(2)}) collective-permute-start(f32[320,128]{1,0:T(8,128)S(1)} %get-tuple-element.51), channel_id=1, source_target_pairs={{0,1},{1,0},{2,3},{3,2},{4,5},{5,4},{6,7},{7,6},{8,9},{9,8},{10,11... | collective-permute-start | bytes 491528 | tf_op jit(solution)/shard_map/ppermute | solution.py:697
  3.6 0.7 collective-permute-start.1
  4.3 3.2 %collective-permute-done.got0 = f32[320,128]{1,0:T(8,128)S(1)} collective-permute-done((f32[320,128]{1,0:T(8,128)S(1)}, f32[320,128]{1,0:T(8,128)S(1)}, u32[]{:S(2)}, u32[]{:S(2)}) %collective-permute-start) | collective-permute-done | bytes 163872 | tf_op jit(solution)/shard_map/ppermute | solution.py:697
  7.5 0.0 collective-permute-done.1.got1
  7.5 0.2 shard_map.56
  7.7 4.1 %collective-permute-start.2 = (f32[288,128]{1,0:T(8,128)S(1)}, f32[288,128]{1,0:T(8,128)S(1)}, u32[]{:S(2)}, u32[]{:S(2)}) collective-permute-start(f32[288,128]{1,0:T(8,128)S(1)} %get-tuple-element.58), channel_id=1, source_target_pairs={{0,8},{8,0},{16,24},{24,16},{1,9},{9,1},{17,25},{25,17},{2,10},{10... | collective-permute-start | bytes 442376 | tf_op jit(solution)/shard_map/ppermute | solution.py:697
  11.8 3.0 %collective-permute-start.3 = (f32[288,128]{1,0:T(8,128)S(1)}, f32[288,128]{1,0:T(8,128)S(1)}, u32[]{:S(2)}, u32[]{:S(2)}) collective-permute-start(f32[288,128]{1,0:T(8,128)S(1)} %get-tuple-element.59), channel_id=1, source_target_pairs={{8,16},{16,8},{9,17},{17,9},{10,18},{18,10},{11,19},{19,11},{12,20... | collective-permute-start | bytes 442376 | tf_op jit(solution)/shard_map/ppermute | solution.py:697
  14.9 0.0 collective-permute-done.2.got0
  14.9 3.4 %collective-permute-done.3.got1 = f32[288,128]{1,0:T(8,128)S(1)} collective-permute-done((f32[288,128]{1,0:T(8,128)S(1)}, f32[288,128]{1,0:T(8,128)S(1)}, u32[]{:S(2)}, u32[]{:S(2)}) %collective-permute-start.3) | collective-permute-done | bytes 147488 | tf_op jit(solution)/shard_map/ppermute | solution.py:697
  18.3 4.5 %shard_map.57 = (f32[2,20,24,128]{3,2,1,0:T(8,128)S(1)}, f32[2,20,24,128]{3,2,1,0:T(8,128)S(1)}, f32[20,24,128]{2,1,0:T(8,128)S(1)}, f32[2,20,24,128]{3,2,1,0:T(...) custom-call(f32[512,128]{1,0:T(8,128)S(1)} %get-tuple-element.46.pot, ...), custom_call_target="tpu_custom_call" | custom-call | tf_op jit(solution)/shard_map/pallas_call | solution.py:714
  22.8 0.7 collective-permute-start.5
  23.5 5.2 %collective-permute-start.4 = (f32[208,128]{1,0:T(8,128)S(1)}, f32[208,128]{1,0:T(8,128)S(1)}, u32[]{:S(2)}, u32[]{:S(2)}) collective-permute-start(f32[208,128]{1,0:T(8,128)S(1)} %get-tuple-element.60.m0), channel_id=1, source_target_pairs={{0,1},{1,0},{2,3},{3,2},{4,5},{5,4},{6,7},{7,6},{8,9},{9,8},{10,11... | collective-permute-start | bytes 319496 | tf_op jit(solution)/shard_map/ppermute | solution.py:697
  28.7 0.0 collective-permute-done.5.got1.gy1.refs_22_
  28.7 2.1 %collective-permute-done.4.got0.gy0.refs_21_ = f32[208,128]{1,0:T(8,128)S(1)} collective-permute-done((f32[208,128]{1,0:T(8,128)S(1)}, f32[208,128]{1,0:T(8,128)S(1)}, u32[]{:S(2)}, u32[]{:S(2)}) %collective-permute-start.4) | collective-permute-done | bytes 106528 | tf_op jit(solution)/shard_map/ppermute | solution.py:697
  30.8 0.1 collective-permute-start.6
  30.9 4.2 %collective-permute-start.7 = (f32[304,128]{1,0:T(8,128)S(1)}, f32[304,128]{1,0:T(8,128)S(1)}, u32[]{:S(2)}, u32[]{:S(2)}) collective-permute-start(f32[304,128]{1,0:T(8,128)S(1)} %get-tuple-element.64), channel_id=1, source_target_pairs={{8,16},{16,8},{9,17},{17,9},{10,18},{18,10},{11,19},{19,11},{12,20... | collective-permute-start | bytes 466952 | tf_op jit(solution)/shard_map/ppermute | solution.py:697
  35.1 0.0 collective-permute-done.6.gx0.refs_23_
  35.1 2.9 %collective-permute-done.7.gx1.refs_24_ = f32[304,128]{1,0:T(8,128)S(1)} collective-permute-done((f32[304,128]{1,0:T(8,128)S(1)}, f32[304,128]{1,0:T(8,128)S(1)}, u32[]{:S(2)}, u32[]{:S(2)}) %collective-permute-start.7) | collective-permute-done | bytes 155680 | tf_op jit(solution)/shard_map/ppermute | solution.py:697
  38.0 4.4 %shard_map.59 = (f32[2,18,24,128]{3,2,1,0:T(8,128)S(1)}, f32[2,18,24,128]{3,2,1,0:T(8,128)S(1)}, f32[2,18,24,128]{3,2,1,0:T(8,128)S(1)}, f32[18,24,128]{2,1,0:T(...) custom-call(f32[208,128]{1,0:T(8,128)S(1)} %get-tuple-element.60.m0,, ...), custom_call_target="tpu_custom_call" | custom-call | tf_op jit(solution)/shard_map/pallas_call | solution.py:732
  42.5 18.9 %all_to_all.5 = f32[32,24,128]{2,1,0:T(8,128)S(1)} all-to-all(f32[32,24,128]{2,1,0:T(8,128)S(1)} %get-tuple-element.67), channel_id=1, replica_groups=mesh['gx'=4,'gy'=8] {'gx','gy'}, dimensions={0} | all-to-all | bytes 786432 | tf_op jit(solution)/shard_map/all_to_all | solution.py:744
  61.4 6.4 %finish.1 = f32[512,128]{1,0:T(8,128)} custom-call(f32[4,8,24,128]{3,2,1,0:T(8,128)S(1)} %bitcast.7, f32[2,18,24,128]{3,2,1,0:T(8,128)S(1)} %get-tuple-element.68.refs_1_, f32[2,18,24,128]{3,2,1,0:T(8,128)S(1)} %get-tuple-element.69.refs_2_, f32[2,18,24,128]{3,2,1,0:T(8,128)S(1)} %get-tuple-element.70.refs_3_, f32[18,24,128]{2,1,0:T(8,128)S(1)} %get-tuple-element.71.refs_4_, ...), custom_call_target="tpu_custom_call" | custom-call | tf_op jit(solution)/shard_map/finish/pallas_call | solution.py:751
  (1 shorter events, 0.0 us)
Async XLA Ops:
  1.5 6.0 %collective-permute-start = (f32[320,128]{1,0:T(8,128)S(1)}, f32[320,128]{1,0:T(8,128)S(1)}, u32[]{:S(2)}, u32[]{:S(2)}) collective-permute-start(f32[320,128]{1,0:T(8,128)S(1)} %get-tuple-element.51), channel_id=1, source_target_pairs={{0,1},{1,0},{2,3},{3,2},{4,5},{5,4},{6,7},{7,6},{8,9},{9,8},{10,11... | collective-permute-start | bytes 491528 | tf_op jit(solution)/shard_map/ppermute | solution.py:697
  3.6 3.9 %collective-permute-start.1 = (f32[320,128]{1,0:T(8,128)S(1)}, f32[320,128]{1,0:T(8,128)S(1)}, u32[]{:S(2)}, u32[]{:S(2)}) collective-permute-start(f32[320,128]{1,0:T(8,128)S(1)} %get-tuple-element.52), channel_id=1, source_target_pairs={{1,2},{2,1},{3,4},{4,3},{5,6},{6,5},{9,10},{10,9},{11,12},{12,11},... | collective-permute-start | bytes 491528 | tf_op jit(solution)/shard_map/ppermute | solution.py:697
  7.7 7.2 %collective-permute-start.2 = (f32[288,128]{1,0:T(8,128)S(1)}, f32[288,128]{1,0:T(8,128)S(1)}, u32[]{:S(2)}, u32[]{:S(2)}) collective-permute-start(f32[288,128]{1,0:T(8,128)S(1)} %get-tuple-element.58), channel_id=1, source_target_pairs={{0,8},{8,0},{16,24},{24,16},{1,9},{9,1},{17,25},{25,17},{2,10},{10... | collective-permute-start | bytes 442376 | tf_op jit(solution)/shard_map/ppermute | solution.py:697
  11.8 6.5 %collective-permute-start.3 = (f32[288,128]{1,0:T(8,128)S(1)}, f32[288,128]{1,0:T(8,128)S(1)}, u32[]{:S(2)}, u32[]{:S(2)}) collective-permute-start(f32[288,128]{1,0:T(8,128)S(1)} %get-tuple-element.59), channel_id=1, source_target_pairs={{8,16},{16,8},{9,17},{17,9},{10,18},{18,10},{11,19},{19,11},{12,20... | collective-permute-start | bytes 442376 | tf_op jit(solution)/shard_map/ppermute | solution.py:697
  22.8 5.9 %collective-permute-start.5 = (f32[208,128]{1,0:T(8,128)S(1)}, f32[208,128]{1,0:T(8,128)S(1)}, u32[]{:S(2)}, u32[]{:S(2)}) collective-permute-start(f32[208,128]{1,0:T(8,128)S(1)} %get-tuple-element.61.m1), channel_id=1, source_target_pairs={{1,2},{2,1},{3,4},{4,3},{5,6},{6,5},{9,10},{10,9},{11,12},{12,11},... | collective-permute-start | bytes 319496 | tf_op jit(solution)/shard_map/ppermute | solution.py:697
  23.5 7.3 %collective-permute-start.4 = (f32[208,128]{1,0:T(8,128)S(1)}, f32[208,128]{1,0:T(8,128)S(1)}, u32[]{:S(2)}, u32[]{:S(2)}) collective-permute-start(f32[208,128]{1,0:T(8,128)S(1)} %get-tuple-element.60.m0), channel_id=1, source_target_pairs={{0,1},{1,0},{2,3},{3,2},{4,5},{5,4},{6,7},{7,6},{8,9},{9,8},{10,11... | collective-permute-start | bytes 319496 | tf_op jit(solution)/shard_map/ppermute | solution.py:697
  30.8 4.3 %collective-permute-start.6 = (f32[304,128]{1,0:T(8,128)S(1)}, f32[304,128]{1,0:T(8,128)S(1)}, u32[]{:S(2)}, u32[]{:S(2)}) collective-permute-start(f32[304,128]{1,0:T(8,128)S(1)} %get-tuple-element.63), channel_id=1, source_target_pairs={{0,8},{8,0},{16,24},{24,16},{1,9},{9,1},{17,25},{25,17},{2,10},{10... | collective-permute-start | bytes 466952 | tf_op jit(solution)/shard_map/ppermute | solution.py:697
  30.9 7.1 %collective-permute-start.7 = (f32[304,128]{1,0:T(8,128)S(1)}, f32[304,128]{1,0:T(8,128)S(1)}, u32[]{:S(2)}, u32[]{:S(2)}) collective-permute-start(f32[304,128]{1,0:T(8,128)S(1)} %get-tuple-element.64), channel_id=1, source_target_pairs={{8,16},{16,8},{9,17},{17,9},{10,18},{18,10},{11,19},{19,11},{12,20... | collective-permute-start | bytes 466952 | tf_op jit(solution)/shard_map/ppermute | solution.py:697

commit v4 on v3

--- a/solution.py
+++ b/solution.py
@@ -13,8 +13,8 @@
 G1 = X1 + 2 * H1
 NF = X1 + 4
 NM = G1 // 2 + 2
-GF = 3
-GM = 4
+GF = 6
+GM = 8
 LN2 = 0.6931471805599453
 
 
@@ -53,7 +53,18 @@
     )
 
 
-def pack_y(hpot, hper, hsrc, hscr, hfix, pot, per, src, scr, fix, out0, out1, sems):
+YROWS = 10 * BX
+XROWS = 12 * YE
+
+
+def split_rows(ref, at):
+    one, two = ref[pl.ds(at, 4, stride=2), :], ref[pl.ds(at + 1, 4, stride=2), :]
+    lane = iota((4, NL), 1)
+    even = (lane % 4 + lane // 4) % 2 == 0
+    return jnp.concatenate([jnp.where(even, one, two), jnp.where(even, two, one)], axis=0)
+
+
+def pack_y(hpot, hper, hsrc, hscr, hfix, pot, per, src, scr, fix, p2, out0, out1, sems, t, pk):
     outs = (out0, out1)
     pairs = ((hpot, pot), (hper, per), (hsrc, src), (hscr, scr), (hfix, fix))
     copies = [pltpu.make_async_copy(a, b, sems.at[k]) for k, (a, b) in enumerate(pairs)]
@@ -85,14 +96,29 @@
         for k, value in enumerate([half(pot, r3, 1), half(per, r3, 1), half(src, r2, 0), half(scr, r2, 0)]):
             out[base + k * BX // 2 : base + (k + 1) * BX // 2, :] = value
 
+    v = per[...].reshape(BX // 4, 4, BY, NL)
+    v = (v[:, 0] + v[:, 1]) + (v[:, 2] + v[:, 3])
+    t[...] = lane_pairs(lane_pairs(v, 1), 2).reshape(BX // 4 * BY, NL)
+    n2 = BX // 4
+    lane = iota((n2, NL), 1)
+    total = None
+    for j in range(4):
+        r = [t[pl.ds(4 * j + k, n2, stride=BY), :] for k in range(4)]
+        value = (r[0] + r[1]) + (r[2] + r[3])
+        total = value if total is None else jnp.where(lane % 4 == j, value, total)
+    pk[...] = F32(1.0 / 64) * total
+    p2[...] = split_rows(pk, 0)
+
     def action(hi, lo):
         side(outs[hi], BY - 1, BY - 2, BY - 3)
         side(outs[lo], 0, 1, 2)
+        for out in outs:
+            out[YROWS : YROWS + 8, :] = p2[...]
 
     by_parity("gy", action)
 
 
-def pack_x(pot, per, src, scr, fix, got0, got1, hpot, hper, hsrc, hscr, hfree, out0, out1):
+def pack_x(pot, per, src, scr, fix, p2, got0, got1, hpot, hper, hsrc, hscr, hfree, out0, out1):
     gots, outs = (got0, got1), (out0, out1)
     halos = (hpot, hper, hsrc, hscr, hfree)
     for h in halos:
@@ -134,6 +160,14 @@
                 out[YE * k : YE * k + BY, :] = own
                 out[YE * k + BY : YE * (k + 1), :] = h[8 * x : 8 * (x + 1), :]
                 k += 1
+
+    def action_p(hi, lo):
+        for out in outs:
+            out[XROWS : XROWS + 8, :] = p2[...]
+            out[XROWS + 8 : XROWS + 16, :] = gots[hi][YROWS : YROWS + 8, :]
+            out[XROWS + 16 : XROWS + 24, :] = gots[lo][YROWS : YROWS + 8, :]
+
+    by_parity("gy", action_p)
 
     def action_x(hi, lo):
         slab(outs[hi], (BX - 1, BX - 2, BX - 3))
@@ -220,7 +254,7 @@
     return value + jnp.where((lane // step) % 2 == 0, rot(value, -step, value.ndim - 1), rot(value, step, value.ndim - 1))
 
 
-def fine_pre(pot, per, src, scr, fix, hpot, hper, hsrc, hscr, hfree, got0, got1,
+def fine_pre(pot, per, src, scr, fix, hpot, hper, hsrc, hscr, hfree, goty0, goty1, got0, got1,
              u, c, fin, fout, fyp, fym, fzp, fzm, esrc, escr, efree, csum, g1, m0, m1,
              ep, tr, tc, tp, p1):
     gots, outs = (got0, got1), (m0, m1)
@@ -278,7 +312,7 @@
     groups(1, X1 + 2, GF, lambda at: fine_half(u, at, GF, 1, refs))
 
     def down(at):
-        n = 2
+        n = 4
         left, react = F32(0.0), F32(0.0)
         for colour in (0, 1):
             _, value, _, ch = pairs_of(u, at, n, colour, refs)
@@ -288,7 +322,7 @@
         tr[pl.ds(to, n * BY), :] = lane_pairs(left[:, 0:BY], 1).reshape(n * BY, NL)
         tc[pl.ds(to, n * BY), :] = lane_pairs(react[:, 0:BY], 1).reshape(n * BY, NL)
 
-    groups(2, X1, 2, down)
+    groups(2, X1, 4, down)
 
     def coarse_p(k, _):
         at = pl.multiple_of(k * YE, 8)
@@ -353,20 +387,23 @@
     def action_y(hi, lo):
         odd_row(outs[hi], BY - 2)
         odd_row(outs[lo], 1)
+        outs[hi][base + X1 : base + X1 + 8, :] = (goty0, goty1)[lo][YROWS : YROWS + 8, :]
+        outs[lo][base + X1 : base + X1 + 8, :] = (goty0, goty1)[hi][YROWS : YROWS + 8, :]
 
     by_parity("gy", action_y)
 
 
-YMSG = X1 * 8 + X1 * 4 + BX // 2
-XMSG = H1 * YE + (H1 // 2) * YE + BY
-
-
-def pack_x1(m0, m1, got0, got1, u, out0, out1):
-    own, gots, outs = m0, (got0, got1), (out0, out1)
+YMSG = X1 * 8 + X1 * 4 + BX // 2 + 8
+XOWN = H1 * YE + (H1 // 2) * YE
+XMSG = XOWN + BY + 40
+
+
+def pack_x1(m0, m1, got0, got1, fx0, fx1, u, out0, out1):
+    own, gots, outs, fines = m0, (got0, got1), (out0, out1), (fx0, fx1)
     odd_y = lax.axis_index("gy") % 2
 
     def go(hi, lo):
-        def slab(out, first, x):
+        def slab(out, first, x, behind):
             at = 0
             for a in range(H1):
                 for ref in (own, gots[hi], gots[lo]):
@@ -378,10 +415,15 @@
                     out[at : at + 8, :] = ref[row : row + 8, :]
                     at += 8
             out[at : at + BY, :] = u[1, x, 0:BY, :]
+            at += BY
+            for got in (gots[hi], gots[lo]):
+                out[at : at + 8, :] = got[YMSG - 8 : YMSG, :]
+                at += 8
+            out[at : at + 24, :] = behind[XROWS : XROWS + 24, :]
 
         def action(xhi, xlo):
-            slab(outs[xhi], X1 - H1, X1 + 1)
-            slab(outs[xlo], 0, 2)
+            slab(outs[xhi], X1 - H1, X1 + 1, fines[xlo])
+            slab(outs[xlo], 0, 2, fines[xhi])
 
         by_parity("gx", action)
 
@@ -411,7 +453,7 @@
 
 def mid_pre(m0, gy0, gy1, gx0, gx1, csum, g1,
             e, r, d, fin, fout, fyp, fym, fzp, fzm, msg,
-            p, t, tr, tc, pc):
+            p, t, tr, tc, pc, pk):
     gys, gxs = (gy0, gy1), (gx0, gx1)
     odd_y = lax.axis_index("gy") % 2
     first = colour_mask(1, 2)[0]
@@ -476,7 +518,7 @@
         groups(1, NM - 2, GM, lambda at, colour=colour: coarse_half(e, r, d, at, GM, colour, faces, 2))
 
     def down(at):
-        n = 2
+        n = 4
         here = pl.ds(at, n)
         k = pl.ds(at - 1 - H1 // 2, n)
         left = F32(0.0)
@@ -487,7 +529,7 @@
         tr[pl.ds(to, n * 8), :] = lane_pairs(left, 2).reshape(n * 8, NL)
         tc[pl.ds(to, n * 8), :] = lane_pairs(csum[k], 2).reshape(n * 8, NL)
 
-    groups(1 + H1 // 2, X1 // 2, 2, down)
+    groups(1 + H1 // 2, X1 // 2, 4, down)
 
     def coarse_p(x2, _):
         t[pl.ds(pl.multiple_of(x2 * YE, 8), YE), :] = lane_pairs(p[0, x2 + 1] + p[1, x2 + 1], 2)
@@ -520,95 +562,138 @@
     back = jnp.where(lane < 4, F32(0.0), rot(centre_p, 4, 1))
     near = (pc[0, h2 + 1 : h2 + 1 + n2, :] + pc[0, h2 - 1 : h2 - 1 + n2, :]) + (high + low) + (front + back)
     diag2 = F32(0.0625) * (F32(3.0) * centre_p + F32(0.5) * near) + react2
-    inverse2 = F32(1.0) / diag2
+    for k, value in enumerate((r2, F32(1.0) / diag2, centre_p)):
+        pk[8 * k : 8 * k + 8, :] = value
+    r2, inverse2, own_p = (split_rows(pk, 8 * k) for k in range(3))
+    near_rows = iota((8, NL), 1) % 4 >= 2
+    ahead = jnp.where(near_rows, r2, rot(own_p, -2, 1))
+    behind = jnp.where(near_rows, rot(own_p, 2, 1), r2)
+    count = lax.axis_size("gy")
+    place = lax.axis_index("gy")
 
     def every(k, _):
-        msg[k, 0:8, :] = r2
+        step = k % count - place
+        msg[k, 0:8, :] = jnp.where(step == 3, ahead, jnp.where(step == -3, behind, r2))
         msg[k, 8:16, :] = inverse2
-        msg[k, 16:24, :] = centre_p
-        return 0
-
-    lax.fori_loop(0, msg.shape[0], every, 0)
-
-
-def finish(at, got, e, r, d, fin1, fout1, fyp1, fym1, fzp1, fzm1,
+        return 0
+
+    lax.fori_loop(0, msg.shape[0], every, 0, unroll=2)
+
+
+def finish(at, got, p2own, yf0, yf1, xf0, xf1, e, r, d, fin1, fout1, fyp1, fym1, fzp1, fzm1,
            before, c, fin, fout, fyp, fym, fzp, fzm, src, scr, free, gy0, gy1, gx0, gx1,
            result,
-           e2, p2, r2, d2, k2, tx, eu, u, hal):
+           e2, p2, r2, d2, k2, blk, tx, eu, u, hal):
     wx, wy = got.shape[0], got.shape[1]
-    rows = wx * 8
+    rows = wx * 4
+    ox, oy = at
+    blk[...] = jnp.zeros_like(blk)
     e2[...] = jnp.zeros_like(e2)
-    p2[0] = jnp.zeros((rows, NL), F32)
-    p2[wy + 1] = jnp.zeros((rows, NL), F32)
+
+    def keep(da, db, ref, first):
+        blk[oy + db + 3, ox + da + 2] = ref[first : first + 8, :]
+
+    keep(0, 0, p2own, 0)
+
+    def blocks_y(hi, lo):
+        for db, k in ((1, hi), (-1, lo)):
+            keep(0, db, (yf0, yf1)[k], YROWS)
+            keep(0, 2 * db, (gy0, gy1)[k], YMSG - 8)
+
+    by_parity("gy", blocks_y)
+
+    def blocks_x(hi, lo):
+        for da, k in ((1, hi), (-1, lo)):
+            fine, mid = (xf0, xf1)[k], (gx0, gx1)[k]
+            for n, db in enumerate((0, 1, -1)):
+                keep(da, db, fine, XROWS + 8 * n)
+                keep(2 * da, db, mid, XOWN + BY + 16 + 8 * n)
+            keep(da, 2, mid, XOWN + BY)
+            keep(da, -2, mid, XOWN + BY + 8)
+
+    by_parity("gx", blocks_x)
+    l4 = iota((8, NL), 1) % 4
+    for db in (3, -3):
+
+        @pl.when((oy + db >= 0) & (oy + db < wy))
+        def _(db=db):
+            for a in range(wx):
+                value = got[a, oy + db, 0:8, :]
+                value = jnp.where(l4 < 2, rot(value, -2, 1), F32(0.0)) if db > 0 else jnp.where(l4 >= 2, rot(value, 2, 1), F32(0.0))
+                blk[oy + db + 3, a + 2] = value
 
     def spread(b, _):
         for a in range(wx):
-            r2[b, 8 * a : 8 * a + 8, :] = got[a, b, 0:8, :]
-            d2[b, 8 * a : 8 * a + 8, :] = got[a, b, 8:16, :]
-            p2[b + 1, 8 * a : 8 * a + 8, :] = got[a, b, 16:24, :]
-        return 0
-
-    lax.fori_loop(0, wy, spread, 0)
-    sub = iota((rows, NL), 0)
-    lane = iota((rows, NL), 1)
+            for colour in (0, 1):
+                own, to = slice(4 * colour, 4 * colour + 4), slice(4 * a, 4 * a + 4)
+                r2[colour, b, to, :] = got[a, b, own, :]
+                d2[colour, b, to, :] = got[a, b, 8 + 4 * colour : 12 + 4 * colour, :]
+                p2[colour, b + 1, to, :] = blk[b + 3, a + 2, own, :]
+        return 0
+
+    lax.fori_loop(0, wy, spread, 0, unroll=2)
+    for b in (0, wy + 1):
+        for colour in (0, 1):
+            p2[colour, b] = jnp.zeros((rows, NL), F32)
+    shape = (wy, rows, NL)
+    sub, lane = iota(shape, 1), iota(shape, 2)
     j4 = lane % 4
-    parity2 = (sub + j4 + lane // 4) % 2
-
-    span = 4 if wy % 4 == 0 else 1
-
-    def shifted(v):
-        mid = v[1 : span + 1]
-        near = j4[None] < 3
+    even = (j4 + lane // 4) % 2 == 0
+
+    def around(ref, colour):
+        v = ref[1 - colour]
+        mid = v[1 : wy + 1]
+        one, two = rot(mid, 1, 1), rot(mid, -1, 1)
         return (
-            rot(mid, -1, 1), rot(mid, 1, 1),
-            jnp.where(near, rot(mid, -1, 2), rot(v[2:], 3, 2)),
-            jnp.where(j4[None] > 0, rot(mid, 1, 2), rot(v[:span], -3, 2)),
+            mid,
+            jnp.where(even, one, two) if colour == 0 else jnp.where(even, two, one),
+            jnp.where(j4 < 3, rot(mid, -1, 2), rot(v[2:], 3, 2)),
+            jnp.where(j4 > 0, rot(mid, 1, 2), rot(v[:wy], -3, 2)),
             rot(mid, -4, 2), rot(mid, 4, 2),
         )
 
-    edges = (sub == rows - 1, sub == 0, None, None, lane >= NL - 4, lane < 4)
-
-    def begin(b):
-        here = pl.ds(b, span)
-        v = p2[pl.ds(b, span + 2)]
-        for k, (value, edge) in enumerate(zip(shifted(v), edges, strict=True)):
-            face = F32(0.03125) * (v[1 : span + 1] + value)
-            k2[k, here] = face if edge is None else jnp.where(edge[None], F32(0.0), face)
-        e2[pl.ds(b + 1, span)] = jnp.where(parity2[None] == 0, r2[here] * d2[here], F32(0.0))
-
-    groups(0, wy, span, begin)
-
-    def half2(step, _):
-        colour = step % 2
-
-        def one(b):
-            here = pl.ds(b, span)
-            v = e2[pl.ds(b, span + 2)]
-            total = r2[here]
-            for k, value in enumerate(shifted(v)):
-                total = total + k2[k, here] * value
-            e2[pl.ds(b + 1, span)] = jnp.where(parity2[None] == colour, total * d2[here], v[1 : span + 1])
-
-        groups(0, wy, span, one)
-        return 0
-
-    lax.fori_loop(1, 8, half2, 0)
-
-    ox, oy = at[0], at[1]
+    for colour in (0, 1):
+        at_first = even if colour == 0 else ~even
+        outside = (at_first & (sub == 0)) | (~at_first & (sub == rows - 1))
+        edges = (None, outside, None, None, lane >= NL - 4, lane < 4)
+        mine = p2[colour, 1 : wy + 1]
+        for k, (value, edge) in enumerate(zip(around(p2, colour), edges, strict=True)):
+            face = F32(0.03125) * (mine + value)
+            k2[colour, k] = face if edge is None else jnp.where(edge, F32(0.0), face)
+    e2[0, 1 : wy + 1] = r2[0] * d2[0]
+
+    def half2(colour):
+        total = r2[colour]
+        for k, value in enumerate(around(e2, colour)):
+            total = total + k2[colour, k] * value
+        e2[colour, 1 : wy + 1] = total * d2[colour]
+
+    half2(1)
+
+    def sweep2(_, carry):
+        half2(0)
+        half2(1)
+        return carry
+
+    lax.fori_loop(0, 3, sweep2, 0)
+
+    s8, l8 = iota((8, NL), 0), iota((8, NL), 1)
+    even8 = (l8 % 4 + l8 // 4) % 2 == 0
+    start = 4 * ox - 2
+    inside = (s8 + start >= 0) & (s8 + start < rows)
     for k, step in enumerate((0, 1, -1)):
-        b = oy + step + 1
-        for dx, first, size, to in ((0, 0, 8, 4), (1, 0, 4, 12), (-1, 4, 4, 0)):
-            a = ox + dx
-            inside = (a >= 0) & (a < wx)
-            block = e2[b, pl.ds(pl.multiple_of(jnp.clip(a, 0, wx - 1) * 8, 8), 8), :]
-            block = jnp.where(inside, block, F32(0.0))
-            l8 = iota((8, NL), 1)
+        near = []
+        for colour in (0, 1):
+            block = pltpu.roll(e2[colour, oy + step + 1], (rows - start) % rows, 0)[0:8]
+            near.append(jnp.where(inside, block, F32(0.0)))
+        planes = (jnp.where(even8, near[0], near[1]), jnp.where(even8, near[1], near[0]))
+        for second in (0, 1):
             for j in range(4):
-                value = jnp.where(l8 % 4 == 0, rot(block, -j, 1), F32(0.0))
+                value = jnp.where(l8 % 4 == 0, rot(planes[second], -j, 1), F32(0.0))
                 value = value + rot(value, 1, 1)
                 value = value + rot(value, 2, 1)
                 for y in (0, 1):
-                    tx[pl.ds(to * YE + 8 * k + 2 * j + y, size, stride=YE), :] = value[first : first + size]
+                    tx[pl.ds(second * YE + 8 * k + 2 * j + y, 8, stride=2 * YE), :] = value
 
     def correct(x2, _):
         value = tx[pl.ds(pl.multiple_of(x2 * YE, 8), YE), :]
@@ -630,7 +715,6 @@
     by_parity("gy", action_y)
     first = colour_mask(1, 1)[0]
     first1 = colour_mask(1, 2)[0]
-    s8 = iota((8, NL), 0)
     added = (s8 == 1) | (s8 == 6)
     own_rows = slice(0, BY)
 
@@ -660,11 +744,11 @@
     lax.fori_loop(0, X1 // 2, add, 0)
 
     def action_x(hi, lo):
-        row = (gx0, gx1)[hi][XMSG - BY : XMSG, :]
+        row = (gx0, gx1)[hi][XOWN : XOWN + BY, :]
         k = X1 + 2
         now = jnp.where(first[own_rows], row, before[1, k, own_rows, :])
         widen(k, level1_plane(1 + H1 // 2 + X1 // 2, 0), now, before[1, k, BY:YE, :])
-        row = (gx0, gx1)[lo][XMSG - BY : XMSG, :]
+        row = (gx0, gx1)[lo][XOWN : XOWN + BY, :]
         now = jnp.where(first[own_rows], before[1, 1, own_rows, :], row)
         widen(1, level1_plane(H1 // 2, 1), now, before[1, 1, BY:YE, :])
 
@@ -675,7 +759,7 @@
     groups(1, X1 + 2, GF, lambda at: fine_half(u, at, GF, 0, refs))
 
     def last(at):
-        n = 2
+        n = 4
         new = fine_new(u, at, n, 1, refs)[:, own_rows]
         even = u[0, pl.ds(at, n), own_rows, :]
         mask = first[own_rows]
@@ -684,7 +768,7 @@
             result[pl.ds(to, BY), :] = jnp.where(mask, even[k], new[k])
             result[pl.ds(to + BY, BY), :] = jnp.where(mask, new[k], even[k])
 
-    groups(2, X1, 2, last)
+    groups(2, X1, 4, last)
 
 
 def swap(pair, axis):
@@ -704,10 +788,15 @@
     args = [pltpu.with_memory_space_constraint(a, pltpu.HBM) for a in args]
 
     whole = (sds(BX * BY, NL),) * 4 + (jax.ShapeDtypeStruct((BX * BY, NL), jnp.int32),)
-    *args, y0, y1 = call(pack_y, whole + (sds(10 * BX, NL),) * 2, [pltpu.SemaphoreType.DMA((5,))], hbm=5)(*args)
+    *args, p2, y0, y1 = call(
+        pack_y,
+        whole + (sds(8, NL),) + (sds(YROWS + 8, NL),) * 2,
+        [pltpu.SemaphoreType.DMA((5,)), pltpu.VMEM((BX // 4 * BY, NL), F32), pltpu.VMEM((8, NL), F32)],
+        hbm=5,
+    )(*args)
     y0 = (y0, y1)
     y0 = swap(y0, "gy")
-    *halos, x0, x1 = call(pack_x, (sds(BX * 8, NL),) * 5 + (sds(12 * YE, NL),) * 2)(*args, *y0)
+    *halos, x0, x1 = call(pack_x, (sds(BX * 8, NL),) * 5 + (sds(XROWS + 24, NL),) * 2)(*args, p2, *y0)
     gotx = swap((x0, x1), "gx")
 
     ext, one = (2, NF, YE, NL), (NF, YE, NL)
@@ -722,41 +811,43 @@
             pltpu.VMEM(((X1 + 2) * YE, NL), F32),
             pltpu.VMEM((X1 + 2, 8, NL), F32),
         ],
-    )(*args, *halos, *gotx)
+    )(*args, *halos, *y0, *gotx)
     state, (c1, g1, m0, m1) = fine[:11], fine[11:]
     goty1 = swap((m0, m1), "gy")
-    x1msg = call(pack_x1, (sds(XMSG, NL),) * 2)(m0, m1, *goty1, state[0])
+    x1msg = call(pack_x1, (sds(XMSG, NL),) * 2)(m0, m1, *goty1, *gotx, state[0])
     gotx1 = swap(x1msg, "gx")
 
     mid, mid1 = (2, NM, YE, NL), (NM, YE, NL)
     *level1, message = call(
         mid_pre,
-        (sds(*mid),) * 3 + (sds(*mid1),) + (sds(*mid),) * 5 + (sds(gx * gy, 24, NL),),
+        (sds(*mid),) * 3 + (sds(*mid1),) + (sds(*mid),) * 5 + (sds(gx * gy, 16, NL),),
         [
             pltpu.VMEM(mid, F32),
             pltpu.VMEM((G1 // 2 * YE, NL), F32),
             pltpu.VMEM((X1 // 2 * 8, NL), F32),
             pltpu.VMEM((X1 // 2 * 8, NL), F32),
             pltpu.VMEM((3, G1 // 2, NL), F32),
+            pltpu.VMEM((24, NL), F32),
         ],
     )(m0, *goty1, *gotx1, c1, g1)
 
-    gathered = lax.all_to_all(message, ("gx", "gy"), 0, 0).reshape(gx, gy, 24, NL)
-    wx, wy = min(gx, 5), min(gy, 8)
+    gathered = lax.all_to_all(message, ("gx", "gy"), 0, 0).reshape(gx, gy, 16, NL)
+    wx, wy = min(gx, 6), min(gy, 8)
     if (wx, wy) != (gx, gy):
         first = (*window(gx, gy, wx, wy)[:2], 0, 0)
-        gathered = lax.dynamic_slice(gathered, first, (wx, wy, 24, NL))
-
-    inputs = (gathered, *level1, *state, *goty1, *gotx1)
+        gathered = lax.dynamic_slice(gathered, first, (wx, wy, 16, NL))
+
+    inputs = (gathered, p2, *y0, *gotx, *level1, *state, *goty1, *gotx1)
     result = pl.pallas_call(
         finish_kernel(len(inputs), (gx, gy, wx, wy)),
         out_shape=sds(BX * BY, NL),
         scratch_shapes=[
-            pltpu.VMEM((wy + 2, wx * 8, NL), F32),
-            pltpu.VMEM((wy + 2, wx * 8, NL), F32),
-            pltpu.VMEM((wy, wx * 8, NL), F32),
-            pltpu.VMEM((wy, wx * 8, NL), F32),
-            pltpu.VMEM((6, wy, wx * 8, NL), F32),
+            pltpu.VMEM((2, wy + 2, wx * 4, NL), F32),
+            pltpu.VMEM((2, wy + 2, wx * 4, NL), F32),
+            pltpu.VMEM((2, wy, wx * 4, NL), F32),
+            pltpu.VMEM((2, wy, wx * 4, NL), F32),
+            pltpu.VMEM((2, 6, wy, wx * 4, NL), F32),
+            pltpu.VMEM((wy + 6, wx + 4, 8, NL), F32),
             pltpu.VMEM((NF * YE, NL), F32),
             pltpu.VMEM(mid, F32),
             pltpu.VMEM(ext, F32),

time: 68.7 us -> 63.3 us (0.921)
  Pallas kernels: 17 us -> 14 us
  blocking collectives: 18.9 us -> 16.2 us
    all_to_all x1, blocking collectives: 18.9 us -> 16.2 us  [body(): lax.all_to_all(message, ('gx', 'gy'), 0, 0).reshape(gx, gy, 16, NL)]
    pallas_call x1, Pallas kernels: 6.35 us -> 4.59 us  [body(): pl.pallas_call(finish_kernel(len(inputs), (gx, gy, wx, wy)), out_shape=sd...]
    pallas_call x1, Pallas kernels: 4.52 us -> 3.77 us  [body(): call(fine_pre, (sds(*ext),) * 2 + (sds(*one),) + (sds(*ext),) * 8 + (sds(...]
where the time goes in v4:
time: 63.3 us; the launch traced here: 62.5 us
  starting transfers between devices  20.1 us (32%)
  blocking collectives  16.2 us (26%)
  Pallas kernels  14 us (22%)
  waiting for transfers between devices  12.1 us (19%)
    ppermute x8, starting transfers between devices, swap(): got[first] = lax.ppermute(pair[first], axis, route)  20.1 us
    all_to_all x1, blocking collectives, body(): lax.all_to_all(message, ('gx', 'gy'), 0, 0).reshape(gx, gy, 16, NL)  16.2 us
    ppermute x8, waiting for transfers between devices, swap(): got[first] = lax.ppermute(pair[first], axis, route)  12.1 us
    pallas_call x1, Pallas kernels, body(): pl.pallas_call(finish_kernel(len(inputs), (gx, gy, wx, wy)), out_shape=sd...  4.59 us
    pallas_call x1, Pallas kernels, body(): call(mid_pre, (sds(*mid),) * 3 + (sds(*mid1),) + (sds(*mid),) * 5 + (sds(...  3.79 us
    pallas_call x1, Pallas kernels, body(): call(fine_pre, (sds(*ext),) * 2 + (sds(*one),) + (sds(*ext),) * 8 + (sds(...  3.77 us
    pallas_call x1, Pallas kernels, body(): call(pack_y, whole + (sds(8, NL),) + (sds(YROWS + 8, NL),) * 2, [pltpu.Se...  1.69 us
  transfers between devices with their start and end apart: 8, of which 4 were waited for; matrix products, arithmetic and copies ran while one was open for 0% of the time, Pallas kernels for 0%

profile of v4, /device:TPU:1, one launch (start us, length us, event | category | flops | bytes accessed | tf_op | source)
XLA Modules:
  0.0 62.5 jit_solution(17946632979566744004)
XLA Ops:
  0.0 1.7 %shard_map.55 = (f32[512,128]{1,0:T(8,128)S(1)}, f32[512,128]{1,0:T(8,128)S(1)}, f32[512,128]{1,0:T(8,128)S(1)}, f32[512,128]{1,0:T(8,128)S(1)}, s32[512,128]{1,...) custom-call(f32[512,128]{1,0:T(8,128)} %bitcast.8, f32[512,128]{1,0:T(8,128)} %bitcast.9, ...), custom_call_target="tpu_custom_call" | custom-call | tf_op jit(solution)/shard_map/pallas_call | solution.py:791
  1.7 2.1 %collective-permute-start = (f32[328,128]{1,0:T(8,128)S(1)}, f32[328,128]{1,0:T(8,128)S(1)}, u32[]{:S(2)}, u32[]{:S(2)}) collective-permute-start(f32[328,128]{1,0:T(8,128)S(1)} %get-tuple-element.53), channel_id=1, source_target_pairs={{0,1},{1,0},{2,3},{3,2},{4,5},{5,4},{6,7},{7,6},{8,9},{9,8},{10,11... | collective-permute-start | bytes 503816 | tf_op jit(solution)/shard_map/ppermute | solution.py:781
  3.8 0.7 %collective-permute-start.1 = (f32[328,128]{1,0:T(8,128)S(1)}, f32[328,128]{1,0:T(8,128)S(1)}, u32[]{:S(2)}, u32[]{:S(2)}) collective-permute-start(f32[328,128]{1,0:T(8,128)S(1)} %get-tuple-element.54), channel_id=1, source_target_pairs={{1,2},{2,1},{3,4},{4,3},{5,6},{6,5},{9,10},{10,9},{11,12},{12,11},... | collective-permute-start | bytes 503816 | tf_op jit(solution)/shard_map/ppermute | solution.py:781
  4.5 3.3 %collective-permute-done.got0.goty0.refs_2_ = f32[328,128]{1,0:T(8,128)S(1)} collective-permute-done((f32[328,128]{1,0:T(8,128)S(1)}, f32[328,128]{1,0:T(8,128)S(1)}, u32[]{:S(2)}, u32[]{:S(2)}) %collective-permute-start) | collective-permute-done | bytes 167968 | tf_op jit(solution)/shard_map/ppermute | solution.py:781
  7.8 0.0 collective-permute-done.1.got1.goty1.refs_3_
  7.8 0.2 shard_map.56
  8.0 4.2 %collective-permute-start.2 = (f32[312,128]{1,0:T(8,128)S(1)}, f32[312,128]{1,0:T(8,128)S(1)}, u32[]{:S(2)}, u32[]{:S(2)}) collective-permute-start(f32[312,128]{1,0:T(8,128)S(1)} %get-tuple-element.60), channel_id=1, source_target_pairs={{0,8},{8,0},{16,24},{24,16},{1,9},{9,1},{17,25},{25,17},{2,10},{10... | collective-permute-start | bytes 479240 | tf_op jit(solution)/shard_map/ppermute | solution.py:781
  12.2 3.0 %collective-permute-start.3 = (f32[312,128]{1,0:T(8,128)S(1)}, f32[312,128]{1,0:T(8,128)S(1)}, u32[]{:S(2)}, u32[]{:S(2)}) collective-permute-start(f32[312,128]{1,0:T(8,128)S(1)} %get-tuple-element.61), channel_id=1, source_target_pairs={{8,16},{16,8},{9,17},{17,9},{10,18},{18,10},{11,19},{19,11},{12,20... | collective-permute-start | bytes 479240 | tf_op jit(solution)/shard_map/ppermute | solution.py:781
  15.2 0.0 collective-permute-done.2.got0.fx0.refs_4_
  15.3 3.5 %collective-permute-done.3.got1.fx1.refs_5_ = f32[312,128]{1,0:T(8,128)S(1)} collective-permute-done((f32[312,128]{1,0:T(8,128)S(1)}, f32[312,128]{1,0:T(8,128)S(1)}, u32[]{:S(2)}, u32[]{:S(2)}) %collective-permute-start.3) | collective-permute-done | bytes 159776 | tf_op jit(solution)/shard_map/ppermute | solution.py:781
  18.8 3.8 %shard_map.57 = (f32[2,20,24,128]{3,2,1,0:T(8,128)S(1)}, f32[2,20,24,128]{3,2,1,0:T(8,128)S(1)}, f32[20,24,128]{2,1,0:T(8,128)S(1)}, f32[2,20,24,128]{3,2,1,0:T(...) custom-call(f32[512,128]{1,0:T(8,128)S(1)} %get-tuple-element.47.pot, ...), custom_call_target="tpu_custom_call" | custom-call | tf_op jit(solution)/shard_map/pallas_call | solution.py:803
  22.6 0.7 %collective-permute-start.5 = (f32[216,128]{1,0:T(8,128)S(1)}, f32[216,128]{1,0:T(8,128)S(1)}, u32[]{:S(2)}, u32[]{:S(2)}) collective-permute-start(f32[216,128]{1,0:T(8,128)S(1)} %get-tuple-element.63.m1), channel_id=1, source_target_pairs={{1,2},{2,1},{3,4},{4,3},{5,6},{6,5},{9,10},{10,9},{11,12},{12,11},... | collective-permute-start | bytes 331784 | tf_op jit(solution)/shard_map/ppermute | solution.py:781
  23.2 5.1 %collective-permute-start.4 = (f32[216,128]{1,0:T(8,128)S(1)}, f32[216,128]{1,0:T(8,128)S(1)}, u32[]{:S(2)}, u32[]{:S(2)}) collective-permute-start(f32[216,128]{1,0:T(8,128)S(1)} %get-tuple-element.62.m0), channel_id=1, source_target_pairs={{0,1},{1,0},{2,3},{3,2},{4,5},{5,4},{6,7},{7,6},{8,9},{9,8},{10,11... | collective-permute-start | bytes 331784 | tf_op jit(solution)/shard_map/ppermute | solution.py:781
  28.4 0.0 collective-permute-done.5.got1.gy1.refs_27_
  28.4 2.1 %collective-permute-done.4.got0.gy0.refs_26_ = f32[216,128]{1,0:T(8,128)S(1)} collective-permute-done((f32[216,128]{1,0:T(8,128)S(1)}, f32[216,128]{1,0:T(8,128)S(1)}, u32[]{:S(2)}, u32[]{:S(2)}) %collective-permute-start.4) | collective-permute-done | bytes 110624 | tf_op jit(solution)/shard_map/ppermute | solution.py:781
  30.5 0.1 collective-permute-start.6
  30.6 4.2 %collective-permute-start.7 = (f32[344,128]{1,0:T(8,128)S(1)}, f32[344,128]{1,0:T(8,128)S(1)}, u32[]{:S(2)}, u32[]{:S(2)}) collective-permute-start(f32[344,128]{1,0:T(8,128)S(1)} %get-tuple-element.66), channel_id=1, source_target_pairs={{8,16},{16,8},{9,17},{17,9},{10,18},{18,10},{11,19},{19,11},{12,20... | collective-permute-start | bytes 528392 | tf_op jit(solution)/shard_map/ppermute | solution.py:781
  34.8 0.0 collective-permute-done.6.gx0.refs_28_
  34.8 3.1 %collective-permute-done.7.gx1.refs_29_ = f32[344,128]{1,0:T(8,128)S(1)} collective-permute-done((f32[344,128]{1,0:T(8,128)S(1)}, f32[344,128]{1,0:T(8,128)S(1)}, u32[]{:S(2)}, u32[]{:S(2)}) %collective-permute-start.7) | collective-permute-done | bytes 176160 | tf_op jit(solution)/shard_map/ppermute | solution.py:781
  38.0 3.8 %shard_map.59 = (f32[2,18,24,128]{3,2,1,0:T(8,128)S(1)}, f32[2,18,24,128]{3,2,1,0:T(8,128)S(1)}, f32[2,18,24,128]{3,2,1,0:T(8,128)S(1)}, f32[18,24,128]{2,1,0:T(...) custom-call(f32[216,128]{1,0:T(8,128)S(1)} %get-tuple-element.62.m0,, ...), custom_call_target="tpu_custom_call" | custom-call | tf_op jit(solution)/shard_map/pallas_call | solution.py:821
  41.7 16.2 %all_to_all.5 = f32[32,16,128]{2,1,0:T(8,128)S(1)} all-to-all(f32[32,16,128]{2,1,0:T(8,128)S(1)} %get-tuple-element.69), channel_id=1, replica_groups=mesh['gx'=4,'gy'=8] {'gx','gy'}, dimensions={0} | all-to-all | bytes 524288 | tf_op jit(solution)/shard_map/all_to_all | solution.py:834
  57.9 4.6 %finish.1 = f32[512,128]{1,0:T(8,128)} custom-call(f32[4,8,16,128]{3,2,1,0:T(8,128)S(1)} %bitcast.7, f32[8,128]{1,0:T(8,128)S(1)} %get-tuple-element.52.p2.refs_1_, f32[328,128]{1,0:T(8,128)S(1)} %collective-permute-done.got0.goty0.refs_2_, f32[328,128]{1,0:T(8,128)S(1)} %collective-permute-done.1.got1.goty1.refs_3_, ...), custom_call_target="tpu_custom_call" | custom-call | tf_op jit(solution)/shard_map/finish/pallas_call | solution.py:841
  (1 shorter events, 0.0 us)
Async XLA Ops:
  1.7 6.1 %collective-permute-start = (f32[328,128]{1,0:T(8,128)S(1)}, f32[328,128]{1,0:T(8,128)S(1)}, u32[]{:S(2)}, u32[]{:S(2)}) collective-permute-start(f32[328,128]{1,0:T(8,128)S(1)} %get-tuple-element.53), channel_id=1, source_target_pairs={{0,1},{1,0},{2,3},{3,2},{4,5},{5,4},{6,7},{7,6},{8,9},{9,8},{10,11... | collective-permute-start | bytes 503816 | tf_op jit(solution)/shard_map/ppermute | solution.py:781
  3.8 4.0 %collective-permute-start.1 = (f32[328,128]{1,0:T(8,128)S(1)}, f32[328,128]{1,0:T(8,128)S(1)}, u32[]{:S(2)}, u32[]{:S(2)}) collective-permute-start(f32[328,128]{1,0:T(8,128)S(1)} %get-tuple-element.54), channel_id=1, source_target_pairs={{1,2},{2,1},{3,4},{4,3},{5,6},{6,5},{9,10},{10,9},{11,12},{12,11},... | collective-permute-start | bytes 503816 | tf_op jit(solution)/shard_map/ppermute | solution.py:781
  8.0 7.3 %collective-permute-start.2 = (f32[312,128]{1,0:T(8,128)S(1)}, f32[312,128]{1,0:T(8,128)S(1)}, u32[]{:S(2)}, u32[]{:S(2)}) collective-permute-start(f32[312,128]{1,0:T(8,128)S(1)} %get-tuple-element.60), channel_id=1, source_target_pairs={{0,8},{8,0},{16,24},{24,16},{1,9},{9,1},{17,25},{25,17},{2,10},{10... | collective-permute-start | bytes 479240 | tf_op jit(solution)/shard_map/ppermute | solution.py:781
  12.2 6.6 %collective-permute-start.3 = (f32[312,128]{1,0:T(8,128)S(1)}, f32[312,128]{1,0:T(8,128)S(1)}, u32[]{:S(2)}, u32[]{:S(2)}) collective-permute-start(f32[312,128]{1,0:T(8,128)S(1)} %get-tuple-element.61), channel_id=1, source_target_pairs={{8,16},{16,8},{9,17},{17,9},{10,18},{18,10},{11,19},{19,11},{12,20... | collective-permute-start | bytes 479240 | tf_op jit(solution)/shard_map/ppermute | solution.py:781
  22.6 5.8 %collective-permute-start.5 = (f32[216,128]{1,0:T(8,128)S(1)}, f32[216,128]{1,0:T(8,128)S(1)}, u32[]{:S(2)}, u32[]{:S(2)}) collective-permute-start(f32[216,128]{1,0:T(8,128)S(1)} %get-tuple-element.63.m1), channel_id=1, source_target_pairs={{1,2},{2,1},{3,4},{4,3},{5,6},{6,5},{9,10},{10,9},{11,12},{12,11},... | collective-permute-start | bytes 331784 | tf_op jit(solution)/shard_map/ppermute | solution.py:781
  23.2 7.3 %collective-permute-start.4 = (f32[216,128]{1,0:T(8,128)S(1)}, f32[216,128]{1,0:T(8,128)S(1)}, u32[]{:S(2)}, u32[]{:S(2)}) collective-permute-start(f32[216,128]{1,0:T(8,128)S(1)} %get-tuple-element.62.m0), channel_id=1, source_target_pairs={{0,1},{1,0},{2,3},{3,2},{4,5},{5,4},{6,7},{7,6},{8,9},{9,8},{10,11... | collective-permute-start | bytes 331784 | tf_op jit(solution)/shard_map/ppermute | solution.py:781
  30.5 4.3 %collective-permute-start.6 = (f32[344,128]{1,0:T(8,128)S(1)}, f32[344,128]{1,0:T(8,128)S(1)}, u32[]{:S(2)}, u32[]{:S(2)}) collective-permute-start(f32[344,128]{1,0:T(8,128)S(1)} %get-tuple-element.65), channel_id=1, source_target_pairs={{0,8},{8,0},{16,24},{24,16},{1,9},{9,1},{17,25},{25,17},{2,10},{10... | collective-permute-start | bytes 528392 | tf_op jit(solution)/shard_map/ppermute | solution.py:781
  30.6 7.3 %collective-permute-start.7 = (f32[344,128]{1,0:T(8,128)S(1)}, f32[344,128]{1,0:T(8,128)S(1)}, u32[]{:S(2)}, u32[]{:S(2)}) collective-permute-start(f32[344,128]{1,0:T(8,128)S(1)} %get-tuple-element.66), channel_id=1, source_target_pairs={{8,16},{16,8},{9,17},{17,9},{10,18},{18,10},{11,19},{19,11},{12,20... | collective-permute-start | bytes 528392 | tf_op jit(solution)/shard_map/ppermute | solution.py:781

commit v5 on v4

--- a/solution.py
+++ b/solution.py
@@ -54,7 +54,8 @@
 
 
 YROWS = 10 * BX
-XROWS = 12 * YE
+XROWS = 12 * 8
+FIELDS = (3, 3, 2, 2, 2)
 
 
 def split_rows(ref, at):
@@ -64,8 +65,8 @@
     return jnp.concatenate([jnp.where(even, one, two), jnp.where(even, two, one)], axis=0)
 
 
-def pack_y(hpot, hper, hsrc, hscr, hfix, pot, per, src, scr, fix, p2, out0, out1, sems, t, pk):
-    outs = (out0, out1)
+def pack_y(hpot, hper, hsrc, hscr, hfix, pot, per, src, scr, fix, p2, out0, out1, xm0, xm1, sems, t, pk):
+    outs, mains = (out0, out1), (xm0, xm1)
     pairs = ((hpot, pot), (hper, per), (hsrc, src), (hscr, scr), (hfix, fix))
     copies = [pltpu.make_async_copy(a, b, sems.at[k]) for k, (a, b) in enumerate(pairs)]
     for copy in copies:
@@ -117,8 +118,22 @@
 
     by_parity("gy", action)
 
-
-def pack_x(pot, per, src, scr, fix, p2, got0, got1, hpot, hper, hsrc, hscr, hfree, out0, out1):
+    def slab(out, planes):
+        k = 0
+        for ref, depth in zip((pot, per, src, scr, fix), FIELDS, strict=True):
+            for x in planes[:depth]:
+                value = ref[BY * x : BY * (x + 1), :]
+                out[BY * k : BY * (k + 1), :] = free_of(value) if ref is fix else value
+                k += 1
+
+    def action_x(hi, lo):
+        slab(mains[hi], (BX - 1, BX - 2, BX - 3))
+        slab(mains[lo], (0, 1, 2))
+
+    by_parity("gx", action_x)
+
+
+def pack_x(p2, got0, got1, hpot, hper, hsrc, hscr, hfree, out0, out1):
     gots, outs = (got0, got1), (out0, out1)
     halos = (hpot, hper, hsrc, hscr, hfree)
     for h in halos:
@@ -152,13 +167,9 @@
 
     def slab(out, planes):
         k = 0
-        for ref, h, depth in ((pot, hpot, 3), (per, hper, 3), (src, hsrc, 2), (scr, hscr, 2), (fix, hfree, 2)):
+        for h, depth in zip(halos, FIELDS, strict=True):
             for x in planes[:depth]:
-                own = ref[BY * x : BY * (x + 1), :]
-                if ref is fix:
-                    own = jnp.where(own == 0, F32(1.0), F32(0.0))
-                out[YE * k : YE * k + BY, :] = own
-                out[YE * k + BY : YE * (k + 1), :] = h[8 * x : 8 * (x + 1), :]
+                out[8 * k : 8 * (k + 1), :] = h[8 * x : 8 * (x + 1), :]
                 k += 1
 
     def action_p(hi, lo):
@@ -254,10 +265,10 @@
     return value + jnp.where((lane // step) % 2 == 0, rot(value, -step, value.ndim - 1), rot(value, step, value.ndim - 1))
 
 
-def fine_pre(pot, per, src, scr, fix, hpot, hper, hsrc, hscr, hfree, goty0, goty1, got0, got1,
-             u, c, fin, fout, fyp, fym, fzp, fzm, esrc, escr, efree, csum, g1, m0, m1,
+def fine_pre(pot, per, src, scr, fix, hpot, hper, hsrc, hscr, hfree, goty0, goty1, xm0, xm1, got0, got1,
+             u, c, fin, fout, fyp, fym, fzp, fzm, esrc, escr, efree, csum, g1, m0, m1, n0, n1,
              ep, tr, tc, tp, p1):
-    gots, outs = (got0, got1), (m0, m1)
+    gots, mains, outs, nexts = (got0, got1), (xm0, xm1), (m0, m1), (n0, n1)
     first = colour_mask(1, 1)[0]
 
     def own(k, _):
@@ -276,11 +287,14 @@
 
     lax.fori_loop(0, X1, own, 0, unroll=2)
 
-    def place(got, near, far, flip):
+    def place(main, got, near, far, flip):
         k = 0
-        for ext, depth in ((u, 3), (ep, 3), (esrc, 2), (escr, 2), (efree, 2)):
-            planes = [got[YE * (k + j) : YE * (k + j + 1), :] for j in range(depth)]
-            k += depth
+        for ext, depth in zip((u, ep, esrc, escr, efree), FIELDS, strict=True):
+            planes = []
+            for _ in range(depth):
+                rows = main[BY * k : BY * (k + 1), :]
+                planes.append(jnp.concatenate([rows, got[8 * k : 8 * (k + 1), :]], axis=0))
+                k += 1
             one, two = (planes[1], planes[0]) if flip else (planes[0], planes[1])
             ext[0, near] = jnp.where(first, one, two)
             ext[1, near] = jnp.where(first, two, one)
@@ -289,8 +303,8 @@
             ext[1, far] = third
 
     def action_x(hi, lo):
-        place(gots[hi], X1 + 2, X1 + 3, False)
-        place(gots[lo], 1, 0, True)
+        place(mains[hi], gots[hi], X1 + 2, X1 + 3, False)
+        place(mains[lo], gots[lo], 1, 0, True)
 
     by_parity("gx", action_x)
     refs = (c, fin, fout, fyp, fym, fzp, fzm, esrc, escr, efree)
@@ -384,6 +398,18 @@
     def odd_row(out, y):
         out[base : base + X1, :] = u[1, pl.ds(2, X1), y, :]
 
+    def slab(out, at, x):
+        out[0 : H1 * 8, :] = m0[8 * at : 8 * (at + H1), :]
+        row = X1 * 8 + 4 * at
+        out[H1 * 8 : H1 * 12, :] = m0[row : row + H1 * 4, :]
+        out[XOWN:XMAIN, :] = u[1, x, 0:BY, :]
+
+    def action_next(hi, lo):
+        slab(nexts[hi], X1 - H1, X1 + 1)
+        slab(nexts[lo], 0, 2)
+
+    by_parity("gx", action_next)
+
     def action_y(hi, lo):
         odd_row(outs[hi], BY - 2)
         odd_row(outs[lo], 1)
@@ -393,37 +419,47 @@
     by_parity("gy", action_y)
 
 
+def halo_rows(dx):
+    return (16 * (dx - 1), 2) if dx < 5 else (64 + 8 * (dx - 5), 1)
+
+
+def halo_pair(t):
+    return (96 + 16 * t, 2) if t < 2 else (128 + 8 * (t - 2), 1)
+
+
+P2AT = 144
 YMSG = X1 * 8 + X1 * 4 + BX // 2 + 8
-XOWN = H1 * YE + (H1 // 2) * YE
-XMSG = XOWN + BY + 40
-
-
-def pack_x1(m0, m1, got0, got1, fx0, fx1, u, out0, out1):
-    own, gots, outs, fines = m0, (got0, got1), (out0, out1), (fx0, fx1)
+XOWN = H1 * 8 + (H1 // 2) * 8
+XMAIN = XOWN + BY
+XMSG = P2AT + 40
+
+
+def pack_x1(got0, got1, fx0, fx1, _, __, out0, out1):
+    gots, outs, fines = (got0, got1), (out0, out1), (fx0, fx1)
     odd_y = lax.axis_index("gy") % 2
+    upper = iota((8, NL), 0) < 4
 
     def go(hi, lo):
-        def slab(out, first, x, behind):
-            at = 0
-            for a in range(H1):
-                for ref in (own, gots[hi], gots[lo]):
-                    out[at : at + 8, :] = ref[8 * (first + a) : 8 * (first + a) + 8, :]
-                    at += 8
-            for a in range(H1 // 2):
-                row = X1 * 8 + 8 * (first // 2 + a)
-                for ref in (own, gots[hi], gots[lo]):
-                    out[at : at + 8, :] = ref[row : row + 8, :]
-                    at += 8
-            out[at : at + BY, :] = u[1, x, 0:BY, :]
-            at += BY
-            for got in (gots[hi], gots[lo]):
-                out[at : at + 8, :] = got[YMSG - 8 : YMSG, :]
-                at += 8
-            out[at : at + 24, :] = behind[XROWS : XROWS + 24, :]
+        def put(out, at, count, row):
+            above, below = gots[hi][row : row + 8, :], gots[lo][row : row + 8, :]
+            if count == 2:
+                out[at : at + 8, :] = above
+                out[at + 8 : at + 16, :] = below
+            else:
+                out[at : at + 8, :] = jnp.where(upper, above, below)
+
+        def slab(out, near, step, behind):
+            for dx in range(1, H1 + 1):
+                put(out, *halo_rows(dx), 8 * (near + step * (dx - 1)))
+            for t in range(H1 // 2):
+                put(out, *halo_pair(t), X1 * 8 + 8 * (near // 2 + step * t))
+            out[P2AT : P2AT + 8, :] = gots[hi][YMSG - 8 : YMSG, :]
+            out[P2AT + 8 : P2AT + 16, :] = gots[lo][YMSG - 8 : YMSG, :]
+            out[P2AT + 16 : P2AT + 40, :] = behind[XROWS : XROWS + 24, :]
 
         def action(xhi, xlo):
-            slab(outs[xhi], X1 - H1, X1 + 1, fines[xlo])
-            slab(outs[xlo], 0, 2, fines[xhi])
+            slab(outs[xhi], X1 - 1, -1, fines[xlo])
+            slab(outs[xlo], 0, 1, fines[xhi])
 
         by_parity("gx", action)
 
@@ -451,10 +487,10 @@
     return jnp.where(lane % 2 == 1, value, rot(value, -1, value.ndim - 1))
 
 
-def mid_pre(m0, gy0, gy1, gx0, gx1, csum, g1,
+def mid_pre(m0, gy0, gy1, xm0, xm1, gx0, gx1, csum, g1,
             e, r, d, fin, fout, fyp, fym, fzp, fzm, msg,
             p, t, tr, tc, pc, pk):
-    gys, gxs = (gy0, gy1), (gx0, gx1)
+    gys, gxs, mains = (gy0, gy1), (gx0, gx1), (xm0, xm1)
     odd_y = lax.axis_index("gy") % 2
     first = colour_mask(1, 2)[0]
 
@@ -487,19 +523,21 @@
     def _():
         own(1, 0)
 
-    def beyond(ref, at):
-        def pairs(k, _):
-            one = ref[pl.ds(pl.multiple_of(2 * YE * k, 8), YE), :]
-            two = ref[pl.ds(pl.multiple_of(2 * YE * k + YE, 8), YE), :]
-            both = ref[pl.ds(pl.multiple_of(H1 * YE + YE * k, 8), YE), :]
+    def beyond(main, ref, at, far):
+        def whole(row, start, count):
+            own_rows = main[row : row + 8, :]
+            above = ref[start : start + 8, :]
+            below = ref[start + 8 : start + 16, :] if count == 2 else above
+            return jnp.concatenate([own_rows, above, below], axis=0)
+
+        for k in range(H1 // 2):
+            one, two = (whole(8 * a, *halo_rows(H1 - a if far else a + 1)) for a in (2 * k, 2 * k + 1))
+            both = whole(H1 * 8 + 8 * k, *halo_pair(H1 // 2 - 1 - k if far else k))
             put(at + k, slice(0, YE), one, two, both)
-            return 0
-
-        lax.fori_loop(0, H1 // 2, pairs, 0, unroll=2)
 
     def action(hi, lo):
-        beyond(gxs[hi], 1 + H1 // 2 + X1 // 2)
-        beyond(gxs[lo], 1)
+        beyond(mains[hi], gxs[hi], 1 + H1 // 2 + X1 // 2, False)
+        beyond(mains[lo], gxs[lo], 1, True)
 
     by_parity("gx", action)
     for ref in (p, e):
@@ -581,7 +619,7 @@
 
 
 def finish(at, got, p2own, yf0, yf1, xf0, xf1, e, r, d, fin1, fout1, fyp1, fym1, fzp1, fzm1,
-           before, c, fin, fout, fyp, fym, fzp, fzm, src, scr, free, gy0, gy1, gx0, gx1,
+           before, c, fin, fout, fyp, fym, fzp, fzm, src, scr, free, gy0, gy1, xm0, xm1, gx0, gx1,
            result,
            e2, p2, r2, d2, k2, blk, tx, eu, u, hal):
     wx, wy = got.shape[0], got.shape[1]
@@ -607,9 +645,9 @@
             fine, mid = (xf0, xf1)[k], (gx0, gx1)[k]
             for n, db in enumerate((0, 1, -1)):
                 keep(da, db, fine, XROWS + 8 * n)
-                keep(2 * da, db, mid, XOWN + BY + 16 + 8 * n)
-            keep(da, 2, mid, XOWN + BY)
-            keep(da, -2, mid, XOWN + BY + 8)
+                keep(2 * da, db, mid, P2AT + 16 + 8 * n)
+            keep(da, 2, mid, P2AT)
+            keep(da, -2, mid, P2AT + 8)
 
     by_parity("gx", blocks_x)
     l4 = iota((8, NL), 1) % 4
@@ -744,11 +782,11 @@
     lax.fori_loop(0, X1 // 2, add, 0)
 
     def action_x(hi, lo):
-        row = (gx0, gx1)[hi][XOWN : XOWN + BY, :]
+        row = (xm0, xm1)[hi][XOWN:XMAIN, :]
         k = X1 + 2
         now = jnp.where(first[own_rows], row, before[1, k, own_rows, :])
         widen(k, level1_plane(1 + H1 // 2 + X1 // 2, 0), now, before[1, k, BY:YE, :])
-        row = (gx0, gx1)[lo][XOWN : XOWN + BY, :]
+        row = (xm0, xm1)[lo][XOWN:XMAIN, :]
         now = jnp.where(first[own_rows], before[1, 1, own_rows, :], row)
         widen(1, level1_plane(H1 // 2, 1), now, before[1, 1, BY:YE, :])
 
@@ -788,22 +826,23 @@
     args = [pltpu.with_memory_space_constraint(a, pltpu.HBM) for a in args]
 
     whole = (sds(BX * BY, NL),) * 4 + (jax.ShapeDtypeStruct((BX * BY, NL), jnp.int32),)
-    *args, p2, y0, y1 = call(
+    *args, p2, y0, y1, xm0, xm1 = call(
         pack_y,
-        whole + (sds(8, NL),) + (sds(YROWS + 8, NL),) * 2,
+        whole + (sds(8, NL),) + (sds(YROWS + 8, NL),) * 2 + (sds(12 * BY, NL),) * 2,
         [pltpu.SemaphoreType.DMA((5,)), pltpu.VMEM((BX // 4 * BY, NL), F32), pltpu.VMEM((8, NL), F32)],
         hbm=5,
     )(*args)
     y0 = (y0, y1)
     y0 = swap(y0, "gy")
-    *halos, x0, x1 = call(pack_x, (sds(BX * 8, NL),) * 5 + (sds(XROWS + 24, NL),) * 2)(*args, p2, *y0)
+    xm = swap((xm0, xm1), "gx")
+    *halos, x0, x1 = call(pack_x, (sds(BX * 8, NL),) * 5 + (sds(XROWS + 24, NL),) * 2)(p2, *y0)
     gotx = swap((x0, x1), "gx")
 
     ext, one = (2, NF, YE, NL), (NF, YE, NL)
     fine = call(
         fine_pre,
         (sds(*ext),) * 2 + (sds(*one),) + (sds(*ext),) * 8
-        + (sds(X1 // 2, 8, NL), sds(2, X1 // 2, 8, NL)) + (sds(YMSG, NL),) * 2,
+        + (sds(X1 // 2, 8, NL), sds(2, X1 // 2, 8, NL)) + (sds(YMSG, NL),) * 2 + (sds(XMAIN, NL),) * 2,
         [
             pltpu.VMEM(ext, F32),
             pltpu.VMEM((X1 * BY, NL), F32),
@@ -811,10 +850,11 @@
             pltpu.VMEM(((X1 + 2) * YE, NL), F32),
             pltpu.VMEM((X1 + 2, 8, NL), F32),
         ],
-    )(*args, *halos, *y0, *gotx)
-    state, (c1, g1, m0, m1) = fine[:11], fine[11:]
+    )(*args, *halos, *y0, *xm, *gotx)
+    state, (c1, g1, m0, m1, *xm1) = fine[:11], fine[11:]
     goty1 = swap((m0, m1), "gy")
-    x1msg = call(pack_x1, (sds(XMSG, NL),) * 2)(m0, m1, *goty1, *gotx, state[0])
+    xm1 = swap(xm1, "gx")
+    x1msg = call(pack_x1, (sds(XMSG, NL),) * 2)(*goty1, *gotx, *xm1)
     gotx1 = swap(x1msg, "gx")
 
     mid, mid1 = (2, NM, YE, NL), (NM, YE, NL)
@@ -829,7 +869,7 @@
             pltpu.VMEM((3, G1 // 2, NL), F32),
             pltpu.VMEM((24, NL), F32),
         ],
-    )(m0, *goty1, *gotx1, c1, g1)
+    )(m0, *goty1, *xm1, *gotx1, c1, g1)
 
     gathered = lax.all_to_all(message, ("gx", "gy"), 0, 0).reshape(gx, gy, 16, NL)
     wx, wy = min(gx, 6), min(gy, 8)
@@ -837,7 +877,7 @@
         first = (*window(gx, gy, wx, wy)[:2], 0, 0)
         gathered = lax.dynamic_slice(gathered, first, (wx, wy, 16, NL))
 
-    inputs = (gathered, p2, *y0, *gotx, *level1, *state, *goty1, *gotx1)
+    inputs = (gathered, p2, *y0, *gotx, *level1, *state, *goty1, *xm1, *gotx1)
     result = pl.pallas_call(
         finish_kernel(len(inputs), (gx, gy, wx, wy)),
         out_shape=sds(BX * BY, NL),

time: 63.3 us -> 62.3 us (0.984)
  starting transfers between devices: 20.1 us -> 26.4 us
  waiting for transfers between devices: 12.1 us -> 6.57 us
  blocking collectives: 16.2 us -> 14.6 us
    ppermute x8 -> x12, starting transfers between devices: 20.1 us -> 26.4 us  [swap(): got[first] = lax.ppermute(pair[first], axis, route)]
    ppermute x8 -> x12, waiting for transfers between devices: 12.1 us -> 6.57 us  [swap(): got[first] = lax.ppermute(pair[first], axis, route)]
    all_to_all x1, blocking collectives: 16.2 us -> 14.6 us  [body(): lax.all_to_all(message, ('gx', 'gy'), 0, 0).reshape(gx, gy, 16, NL)]
  transfers between devices with their start and end apart: 8 -> 12, of which waited for: 4 -> 3; matrix products, arithmetic and copies ran while one was open for 0% -> 0% of each run, Pallas kernels for 0% -> 0%
where the time goes in v5:
time: 62.3 us; the launch traced here: 61.5 us
  starting transfers between devices  26.4 us (42%)
  blocking collectives  14.6 us (23%)
  Pallas kernels  13.7 us (22%)
  waiting for transfers between devices  6.57 us (11%)
    ppermute x12, starting transfers between devices, swap(): got[first] = lax.ppermute(pair[first], axis, route)  26.4 us
    all_to_all x1, blocking collectives, body(): lax.all_to_all(message, ('gx', 'gy'), 0, 0).reshape(gx, gy, 16, NL)  14.6 us
    ppermute x12, waiting for transfers between devices, swap(): got[first] = lax.ppermute(pair[first], axis, route)  6.57 us
    pallas_call x1, Pallas kernels, body(): pl.pallas_call(finish_kernel(len(inputs), (gx, gy, wx, wy)), out_shape=sd...  4.55 us
    pallas_call x1, Pallas kernels, body(): call(fine_pre, (sds(*ext),) * 2 + (sds(*one),) + (sds(*ext),) * 8 + (sds(...  3.72 us
    pallas_call x1, Pallas kernels, body(): call(mid_pre, (sds(*mid),) * 3 + (sds(*mid1),) + (sds(*mid),) * 5 + (sds(...  3.54 us
    pallas_call x1, Pallas kernels, body(): call(pack_y, whole + (sds(8, NL),) + (sds(YROWS + 8, NL),) * 2 + (sds(12...  1.71 us
  transfers between devices with their start and end apart: 12, of which 3 were waited for; matrix products, arithmetic and copies ran while one was open for 0% of the time, Pallas kernels for 0%

profile of v5, /device:TPU:1, one launch (start us, length us, event | category | flops | bytes accessed | tf_op | source)
XLA Modules:
  0.0 61.5 jit_solution(14635550300183501434)
XLA Ops:
  0.0 1.7 %shard_map.55 = (f32[512,128]{1,0:T(8,128)S(1)}, f32[512,128]{1,0:T(8,128)S(1)}, f32[512,128]{1,0:T(8,128)S(1)}, f32[512,128]{1,0:T(8,128)S(1)}, s32[512,128]{1,...) custom-call(f32[512,128]{1,0:T(8,128)} %bitcast.8, ...), custom_call_target="tpu_custom_call" | custom-call | tf_op jit(solution)/shard_map/pallas_call | solution.py:829
  1.7 2.1 %collective-permute-start = (f32[328,128]{1,0:T(8,128)S(1)}, f32[328,128]{1,0:T(8,128)S(1)}, u32[]{:S(2)}, u32[]{:S(2)}) collective-permute-start(f32[328,128]{1,0:T(8,128)S(1)} %get-tuple-element.57), channel_id=1, source_target_pairs={{0,1},{1,0},{2,3},{3,2},{4,5},{5,4},{6,7},{7,6},{8,9},{9,8},{10,11... | collective-permute-start | bytes 503816 | tf_op jit(solution)/shard_map/ppermute | solution.py:819
  3.8 0.7 %collective-permute-start.1 = (f32[328,128]{1,0:T(8,128)S(1)}, f32[328,128]{1,0:T(8,128)S(1)}, u32[]{:S(2)}, u32[]{:S(2)}) collective-permute-start(f32[328,128]{1,0:T(8,128)S(1)} %get-tuple-element.58), channel_id=1, source_target_pairs={{1,2},{2,1},{3,4},{4,3},{5,6},{6,5},{9,10},{10,9},{11,12},{12,11},... | collective-permute-start | bytes 503816 | tf_op jit(solution)/shard_map/ppermute | solution.py:819
  4.5 1.0 %collective-permute-start.2 = (f32[192,128]{1,0:T(8,128)S(1)}, f32[192,128]{1,0:T(8,128)S(1)}, u32[]{:S(2)}, u32[]{:S(2)}) collective-permute-start(f32[192,128]{1,0:T(8,128)S(1)} %get-tuple-element.64), channel_id=1, source_target_pairs={{0,8},{8,0},{16,24},{24,16},{1,9},{9,1},{17,25},{25,17},{2,10},{10... | collective-permute-start | bytes 294920 | tf_op jit(solution)/shard_map/ppermute | solution.py:819
  5.5 3.0 %collective-permute-start.3 = (f32[192,128]{1,0:T(8,128)S(1)}, f32[192,128]{1,0:T(8,128)S(1)}, u32[]{:S(2)}, u32[]{:S(2)}) collective-permute-start(f32[192,128]{1,0:T(8,128)S(1)} %get-tuple-element.65), channel_id=1, source_target_pairs={{8,16},{16,8},{9,17},{17,9},{10,18},{18,10},{11,19},{19,11},{12,20... | collective-permute-start | bytes 294920 | tf_op jit(solution)/shard_map/ppermute | solution.py:819
  8.6 0.0 collective-permute-done.got0.goty0.refs_2_
  8.6 0.0 collective-permute-done.1.got1.goty1.refs_3_
  8.6 0.2 shard_map.56
  8.8 3.4 %collective-permute-start.4 = (f32[120,128]{1,0:T(8,128)S(1)}, f32[120,128]{1,0:T(8,128)S(1)}, u32[]{:S(2)}, u32[]{:S(2)}) collective-permute-start(f32[120,128]{1,0:T(8,128)S(1)} %get-tuple-element.66), channel_id=1, source_target_pairs={{0,8},{8,0},{16,24},{24,16},{1,9},{9,1},{17,25},{25,17},{2,10},{10... | collective-permute-start | bytes 184328 | tf_op jit(solution)/shard_map/ppermute | solution.py:819
  12.2 3.0 %collective-permute-start.5 = (f32[120,128]{1,0:T(8,128)S(1)}, f32[120,128]{1,0:T(8,128)S(1)}, u32[]{:S(2)}, u32[]{:S(2)}) collective-permute-start(f32[120,128]{1,0:T(8,128)S(1)} %get-tuple-element.67), channel_id=1, source_target_pairs={{8,16},{16,8},{9,17},{17,9},{10,18},{18,10},{11,19},{19,11},{12,20... | collective-permute-start | bytes 184328 | tf_op jit(solution)/shard_map/ppermute | solution.py:819
  15.3 0.0 collective-permute-done.2.xm0
  15.3 0.0 collective-permute-done.3.xm1
  15.3 0.0 collective-permute-done.4.got0.fx0.refs_4_
  15.3 2.4 %collective-permute-done.5.got1.fx1.refs_5_ = f32[120,128]{1,0:T(8,128)S(1)} collective-permute-done((f32[120,128]{1,0:T(8,128)S(1)}, f32[120,128]{1,0:T(8,128)S(1)}, u32[]{:S(2)}, u32[]{:S(2)}) %collective-permute-start.5) | collective-permute-done | bytes 61472 | tf_op jit(solution)/shard_map/ppermute | solution.py:819
  17.7 3.7 %shard_map.57 = (f32[2,20,24,128]{3,2,1,0:T(8,128)S(1)}, f32[2,20,24,128]{3,2,1,0:T(8,128)S(1)}, f32[20,24,128]{2,1,0:T(8,128)S(1)}, f32[2,20,24,128]{3,2,1,0:T(...) custom-call(f32[512,128]{1,0:T(8,128)S(1)} %get-tuple-element.51.pot, ...), custom_call_target="tpu_custom_call" | custom-call | tf_op jit(solution)/shard_map/pallas_call | solution.py:842
  21.5 0.7 %collective-permute-start.7 = (f32[216,128]{1,0:T(8,128)S(1)}, f32[216,128]{1,0:T(8,128)S(1)}, u32[]{:S(2)}, u32[]{:S(2)}) collective-permute-start(f32[216,128]{1,0:T(8,128)S(1)} %get-tuple-element.69), channel_id=1, source_target_pairs={{1,2},{2,1},{3,4},{4,3},{5,6},{6,5},{9,10},{10,9},{11,12},{12,11},... | collective-permute-start | bytes 331784 | tf_op jit(solution)/shard_map/ppermute | solution.py:819
  22.1 5.1 %collective-permute-start.6 = (f32[216,128]{1,0:T(8,128)S(1)}, f32[216,128]{1,0:T(8,128)S(1)}, u32[]{:S(2)}, u32[]{:S(2)}) collective-permute-start(f32[216,128]{1,0:T(8,128)S(1)} %get-tuple-element.68.m0), channel_id=1, source_target_pairs={{0,1},{1,0},{2,3},{3,2},{4,5},{5,4},{6,7},{7,6},{8,9},{9,8},{10,11... | collective-permute-start | bytes 331784 | tf_op jit(solution)/shard_map/ppermute | solution.py:819
  27.3 0.0 collective-permute-start.8
  27.3 3.6 %collective-permute-start.9 = (f32[112,128]{1,0:T(8,128)S(1)}, f32[112,128]{1,0:T(8,128)S(1)}, u32[]{:S(2)}, u32[]{:S(2)}) collective-permute-start(f32[112,128]{1,0:T(8,128)S(1)} %get-tuple-element.71), channel_id=1, source_target_pairs={{8,16},{16,8},{9,17},{17,9},{10,18},{18,10},{11,19},{19,11},{12,20... | collective-permute-start | bytes 172040 | tf_op jit(solution)/shard_map/ppermute | solution.py:819
  30.9 0.0 collective-permute-done.8._.xm0.refs_28_
  30.9 1.9 %collective-permute-done.9.__.xm1.refs_29_ = f32[112,128]{1,0:T(8,128)S(1)} collective-permute-done((f32[112,128]{1,0:T(8,128)S(1)}, f32[112,128]{1,0:T(8,128)S(1)}, u32[]{:S(2)}, u32[]{:S(2)}) %collective-permute-start.9) | collective-permute-done | bytes 57376 | tf_op jit(solution)/shard_map/ppermute | solution.py:819
  32.8 0.0 collective-permute-done.7.got1.gy1.refs_27_
  32.8 0.0 collective-permute-done.6.got0.gy0.refs_26_
  32.8 0.1 collective-permute-start.10
  32.9 3.6 %collective-permute-start.11 = (f32[184,128]{1,0:T(8,128)S(1)}, f32[184,128]{1,0:T(8,128)S(1)}, u32[]{:S(2)}, u32[]{:S(2)}) collective-permute-start(f32[184,128]{1,0:T(8,128)S(1)} %get-tuple-element.73), channel_id=1, source_target_pairs={{8,16},{16,8},{9,17},{17,9},{10,18},{18,10},{11,19},{19,11},{12,20... | collective-permute-start | bytes 282632 | tf_op jit(solution)/shard_map/ppermute | solution.py:819
  36.5 0.0 collective-permute-done.10.gx0.refs_30_
  36.5 2.3 %collective-permute-done.11.gx1.refs_31_ = f32[184,128]{1,0:T(8,128)S(1)} collective-permute-done((f32[184,128]{1,0:T(8,128)S(1)}, f32[184,128]{1,0:T(8,128)S(1)}, u32[]{:S(2)}, u32[]{:S(2)}) %collective-permute-start.11) | collective-permute-done | bytes 94240 | tf_op jit(solution)/shard_map/ppermute | solution.py:819
  38.8 3.5 %shard_map.59 = (f32[2,18,24,128]{3,2,1,0:T(8,128)S(1)}, f32[2,18,24,128]{3,2,1,0:T(8,128)S(1)}, f32[2,18,24,128]{3,2,1,0:T(8,128)S(1)}, f32[18,24,128]{2,1,0:T(...) custom-call(f32[216,128]{1,0:T(8,128)S(1)} %get-tuple-element.68.m0,, ...), custom_call_target="tpu_custom_call" | custom-call | tf_op jit(solution)/shard_map/pallas_call | solution.py:861
  42.3 14.6 %all_to_all.5 = f32[32,16,128]{2,1,0:T(8,128)S(1)} all-to-all(f32[32,16,128]{2,1,0:T(8,128)S(1)} %get-tuple-element.76), channel_id=1, replica_groups=mesh['gx'=4,'gy'=8] {'gx','gy'}, dimensions={0} | all-to-all | bytes 524288 | tf_op jit(solution)/shard_map/all_to_all | solution.py:874
  56.9 4.5 %finish.1 = f32[512,128]{1,0:T(8,128)} custom-call(f32[4,8,16,128]{3,2,1,0:T(8,128)S(1)} %bitcast.7, f32[8,128]{1,0:T(8,128)S(1)} %get-tuple-element.56.p2.refs_1_, f32[328,128]{1,0:T(8,128)S(1)} %collective-permute-done.got0.goty0.refs_2_, f32[328,128]{1,0:T(8,128)S(1)} %collective-permute-done.1.got1.goty1.refs_3_, ...), custom_call_target="tpu_custom_call" | custom-call | tf_op jit(solution)/shard_map/finish/pallas_call | solution.py:881
  (1 shorter events, 0.0 us)
Async XLA Ops:
  1.7 6.8 %collective-permute-start = (f32[328,128]{1,0:T(8,128)S(1)}, f32[328,128]{1,0:T(8,128)S(1)}, u32[]{:S(2)}, u32[]{:S(2)}) collective-permute-start(f32[328,128]{1,0:T(8,128)S(1)} %get-tuple-element.57), channel_id=1, source_target_pairs={{0,1},{1,0},{2,3},{3,2},{4,5},{5,4},{6,7},{7,6},{8,9},{9,8},{10,11... | collective-permute-start | bytes 503816 | tf_op jit(solution)/shard_map/ppermute | solution.py:819
  3.8 4.8 %collective-permute-start.1 = (f32[328,128]{1,0:T(8,128)S(1)}, f32[328,128]{1,0:T(8,128)S(1)}, u32[]{:S(2)}, u32[]{:S(2)}) collective-permute-start(f32[328,128]{1,0:T(8,128)S(1)} %get-tuple-element.58), channel_id=1, source_target_pairs={{1,2},{2,1},{3,4},{4,3},{5,6},{6,5},{9,10},{10,9},{11,12},{12,11},... | collective-permute-start | bytes 503816 | tf_op jit(solution)/shard_map/ppermute | solution.py:819
  4.5 10.8 %collective-permute-start.2 = (f32[192,128]{1,0:T(8,128)S(1)}, f32[192,128]{1,0:T(8,128)S(1)}, u32[]{:S(2)}, u32[]{:S(2)}) collective-permute-start(f32[192,128]{1,0:T(8,128)S(1)} %get-tuple-element.64), channel_id=1, source_target_pairs={{0,8},{8,0},{16,24},{24,16},{1,9},{9,1},{17,25},{25,17},{2,10},{10... | collective-permute-start | bytes 294920 | tf_op jit(solution)/shard_map/ppermute | solution.py:819
  5.5 9.8 %collective-permute-start.3 = (f32[192,128]{1,0:T(8,128)S(1)}, f32[192,128]{1,0:T(8,128)S(1)}, u32[]{:S(2)}, u32[]{:S(2)}) collective-permute-start(f32[192,128]{1,0:T(8,128)S(1)} %get-tuple-element.65), channel_id=1, source_target_pairs={{8,16},{16,8},{9,17},{17,9},{10,18},{18,10},{11,19},{19,11},{12,20... | collective-permute-start | bytes 294920 | tf_op jit(solution)/shard_map/ppermute | solution.py:819
  8.8 6.5 %collective-permute-start.4 = (f32[120,128]{1,0:T(8,128)S(1)}, f32[120,128]{1,0:T(8,128)S(1)}, u32[]{:S(2)}, u32[]{:S(2)}) collective-permute-start(f32[120,128]{1,0:T(8,128)S(1)} %get-tuple-element.66), channel_id=1, source_target_pairs={{0,8},{8,0},{16,24},{24,16},{1,9},{9,1},{17,25},{25,17},{2,10},{10... | collective-permute-start | bytes 184328 | tf_op jit(solution)/shard_map/ppermute | solution.py:819
  12.2 5.5 %collective-permute-start.5 = (f32[120,128]{1,0:T(8,128)S(1)}, f32[120,128]{1,0:T(8,128)S(1)}, u32[]{:S(2)}, u32[]{:S(2)}) collective-permute-start(f32[120,128]{1,0:T(8,128)S(1)} %get-tuple-element.67), channel_id=1, source_target_pairs={{8,16},{16,8},{9,17},{17,9},{10,18},{18,10},{11,19},{19,11},{12,20... | collective-permute-start | bytes 184328 | tf_op jit(solution)/shard_map/ppermute | solution.py:819
  21.5 11.3 %collective-permute-start.7 = (f32[216,128]{1,0:T(8,128)S(1)}, f32[216,128]{1,0:T(8,128)S(1)}, u32[]{:S(2)}, u32[]{:S(2)}) collective-permute-start(f32[216,128]{1,0:T(8,128)S(1)} %get-tuple-element.69), channel_id=1, source_target_pairs={{1,2},{2,1},{3,4},{4,3},{5,6},{6,5},{9,10},{10,9},{11,12},{12,11},... | collective-permute-start | bytes 331784 | tf_op jit(solution)/shard_map/ppermute | solution.py:819
  22.1 10.6 %collective-permute-start.6 = (f32[216,128]{1,0:T(8,128)S(1)}, f32[216,128]{1,0:T(8,128)S(1)}, u32[]{:S(2)}, u32[]{:S(2)}) collective-permute-start(f32[216,128]{1,0:T(8,128)S(1)} %get-tuple-element.68.m0), channel_id=1, source_target_pairs={{0,1},{1,0},{2,3},{3,2},{4,5},{5,4},{6,7},{7,6},{8,9},{9,8},{10,11... | collective-permute-start | bytes 331784 | tf_op jit(solution)/shard_map/ppermute | solution.py:819
  27.3 3.6 %collective-permute-start.8 = (f32[112,128]{1,0:T(8,128)S(1)}, f32[112,128]{1,0:T(8,128)S(1)}, u32[]{:S(2)}, u32[]{:S(2)}) collective-permute-start(f32[112,128]{1,0:T(8,128)S(1)} %get-tuple-element.70), channel_id=1, source_target_pairs={{0,8},{8,0},{16,24},{24,16},{1,9},{9,1},{17,25},{25,17},{2,10},{10... | collective-permute-start | bytes 172040 | tf_op jit(solution)/shard_map/ppermute | solution.py:819
  27.3 5.5 %collective-permute-start.9 = (f32[112,128]{1,0:T(8,128)S(1)}, f32[112,128]{1,0:T(8,128)S(1)}, u32[]{:S(2)}, u32[]{:S(2)}) collective-permute-start(f32[112,128]{1,0:T(8,128)S(1)} %get-tuple-element.71), channel_id=1, source_target_pairs={{8,16},{16,8},{9,17},{17,9},{10,18},{18,10},{11,19},{19,11},{12,20... | collective-permute-start | bytes 172040 | tf_op jit(solution)/shard_map/ppermute | solution.py:819
  32.8 3.7 %collective-permute-start.10 = (f32[184,128]{1,0:T(8,128)S(1)}, f32[184,128]{1,0:T(8,128)S(1)}, u32[]{:S(2)}, u32[]{:S(2)}) collective-permute-start(f32[184,128]{1,0:T(8,128)S(1)} %get-tuple-element.72), channel_id=1, source_target_pairs={{0,8},{8,0},{16,24},{24,16},{1,9},{9,1},{17,25},{25,17},{2,10},{10... | collective-permute-start | bytes 282632 | tf_op jit(solution)/shard_map/ppermute | solution.py:819
  32.9 5.9 %collective-permute-start.11 = (f32[184,128]{1,0:T(8,128)S(1)}, f32[184,128]{1,0:T(8,128)S(1)}, u32[]{:S(2)}, u32[]{:S(2)}) collective-permute-start(f32[184,128]{1,0:T(8,128)S(1)} %get-tuple-element.73), channel_id=1, source_target_pairs={{8,16},{16,8},{9,17},{17,9},{10,18},{18,10},{11,19},{19,11},{12,20... | collective-permute-start | bytes 282632 | tf_op jit(solution)/shard_map/ppermute | solution.py:819

commit v6 on v5

--- a/solution.py
+++ b/solution.py
@@ -13,7 +13,7 @@
 G1 = X1 + 2 * H1
 NF = X1 + 4
 NM = G1 // 2 + 2
-GF = 6
+GF = 3
 GM = 8
 LN2 = 0.6931471805599453
 
@@ -69,10 +69,9 @@
     outs, mains = (out0, out1), (xm0, xm1)
     pairs = ((hpot, pot), (hper, per), (hsrc, src), (hscr, scr), (hfix, fix))
     copies = [pltpu.make_async_copy(a, b, sems.at[k]) for k, (a, b) in enumerate(pairs)]
-    for copy in copies:
-        copy.start()
-    for copy in copies:
-        copy.wait()
+    for k in (1, 0, 2, 3, 4):
+        copies[k].start()
+    copies[1].wait()
     zlane = iota((BX // 2, NL), 1)
 
     def free_of(value):
@@ -109,6 +108,8 @@
         total = value if total is None else jnp.where(lane % 4 == j, value, total)
     pk[...] = F32(1.0 / 64) * total
     p2[...] = split_rows(pk, 0)
+    for k in (0, 2, 3, 4):
+        copies[k].wait()
 
     def action(hi, lo):
         side(outs[hi], BY - 1, BY - 2, BY - 3)
@@ -238,7 +239,7 @@
         step(first + g * n)
         return 0
 
-    lax.fori_loop(0, count // n, one, 0)
+    lax.fori_loop(0, count // n, one, 0, unroll=True)
 
 
 def faces_of(p, at, n, scale, zstep, fin, fout, fyp, fym, fzp, fzm):
@@ -285,7 +286,7 @@
                 ext[1, k + 2, rows, :] = jnp.where(first[rows], two, one)
         return 0
 
-    lax.fori_loop(0, X1, own, 0, unroll=2)
+    lax.fori_loop(0, X1, own, 0, unroll=4)
 
     def place(main, got, near, far, flip):
         k = 0
@@ -343,7 +344,7 @@
         tp[pl.ds(at, YE), :] = lane_pairs(ep[0, k + 1] + ep[1, k + 1], 1)
         return 0
 
-    lax.fori_loop(0, X1 + 2, coarse_p, 0, unroll=2)
+    lax.fori_loop(0, X1 + 2, coarse_p, 0, unroll=6)
 
     eighth = F32(0.125)
     sub = iota((8, NL), 0)
@@ -353,7 +354,7 @@
         p1[k] = eighth * (tp[pl.ds(k * YE, 8, stride=2), :] + tp[pl.ds(k * YE + 1, 8, stride=2), :])
         return 0
 
-    lax.fori_loop(0, X1 + 2, gather_p, 0, unroll=2)
+    lax.fori_loop(0, X1 + 2, gather_p, 0, unroll=6)
 
     first8 = (sub + lane // 2) % 2 == 0
 
@@ -386,7 +387,7 @@
         g1[1, k] = jnp.where(first8, diag1, diag0)
         return 0
 
-    lax.fori_loop(0, X1 // 2, make, 0)
+    lax.fori_loop(0, X1 // 2, make, 0, unroll=4)
 
     for a in range(X1 // 2):
         message = jnp.where(lane % 2 == 0, p1[1 + 2 * a], p1[2 + 2 * a])
@@ -513,7 +514,7 @@
                 put(1 + H1 // 2 + k, slice(8 * j, 8 * j + 8), two[:8], two[8:], both)
             return 0
 
-        lax.fori_loop(0, X1 // 2, pairs, 0, unroll=2)
+        lax.fori_loop(0, X1 // 2, pairs, 0, unroll=4)
 
     @pl.when(odd_y == 0)
     def _():
@@ -573,7 +574,7 @@
         t[pl.ds(pl.multiple_of(x2 * YE, 8), YE), :] = lane_pairs(p[0, x2 + 1] + p[1, x2 + 1], 2)
         return 0
 
-    lax.fori_loop(0, G1 // 2, coarse_p, 0, unroll=2)
+    lax.fori_loop(0, G1 // 2, coarse_p, 0, unroll=4)
 
     eighth = F32(0.125)
     n2, m2 = X1 // 2, G1 // 2
@@ -615,18 +616,20 @@
         msg[k, 8:16, :] = inverse2
         return 0
 
-    lax.fori_loop(0, msg.shape[0], every, 0, unroll=2)
+    lax.fori_loop(0, msg.shape[0], every, 0, unroll=8)
 
 
 def finish(at, got, p2own, yf0, yf1, xf0, xf1, e, r, d, fin1, fout1, fyp1, fym1, fzp1, fzm1,
            before, c, fin, fout, fyp, fym, fzp, fzm, src, scr, free, gy0, gy1, xm0, xm1, gx0, gx1,
            result,
-           e2, p2, r2, d2, k2, blk, tx, eu, u, hal):
+           e2, p2, r2, d2, k2, blk, tx, eu, u, hal, res, sems):
     wx, wy = got.shape[0], got.shape[1]
     rows = wx * 4
     ox, oy = at
     blk[...] = jnp.zeros_like(blk)
-    e2[...] = jnp.zeros_like(e2)
+    for b in (0, wy + 1):
+        for colour in (0, 1):
+            e2[colour, b] = jnp.zeros((rows, NL), F32)
 
     def keep(da, db, ref, first):
         blk[oy + db + 3, ox + da + 2] = ref[first : first + 8, :]
@@ -669,7 +672,7 @@
                 p2[colour, b + 1, to, :] = blk[b + 3, a + 2, own, :]
         return 0
 
-    lax.fori_loop(0, wy, spread, 0, unroll=2)
+    lax.fori_loop(0, wy, spread, 0, unroll=4)
     for b in (0, wy + 1):
         for colour in (0, 1):
             p2[colour, b] = jnp.zeros((rows, NL), F32)
@@ -713,7 +716,7 @@
         half2(1)
         return carry
 
-    lax.fori_loop(0, 3, sweep2, 0)
+    lax.fori_loop(0, 3, sweep2, 0, unroll=True)
 
     s8, l8 = iota((8, NL), 0), iota((8, NL), 1)
     even8 = (l8 % 4 + l8 // 4) % 2 == 0
@@ -739,7 +742,7 @@
             eu[colour, x2 + 1] = e[colour, x2 + 1] + value
         return 0
 
-    lax.fori_loop(0, G1 // 2, correct, 0, unroll=2)
+    lax.fori_loop(0, G1 // 2, correct, 0, unroll=4)
     faces1 = (fin1, fout1, fyp1, fym1, fzp1, fzm1)
     for at1, count, n, colour in ((3, 12, 4, 0), (3, 12, 4, 1), (4, 10, 5, 0), (4, 10, 5, 1)):
         groups(at1, count, n, lambda at, n=n, colour=colour: coarse_half(eu, r, d, at, n, colour, faces1, 2))
@@ -779,7 +782,7 @@
             widen(k, level1_plane(m + 1 + H1 // 2, second), before[1, k, own_rows, :], halo)
         return 0
 
-    lax.fori_loop(0, X1 // 2, add, 0)
+    lax.fori_loop(0, X1 // 2, add, 0, unroll=4)
 
     def action_x(hi, lo):
         row = (xm0, xm1)[hi][XOWN:XMAIN, :]
@@ -803,10 +806,17 @@
         mask = first[own_rows]
         for k in range(n):
             to = pl.multiple_of((at - 2 + k) * 2 * BY, 8)
-            result[pl.ds(to, BY), :] = jnp.where(mask, even[k], new[k])
-            result[pl.ds(to + BY, BY), :] = jnp.where(mask, new[k], even[k])
-
-    groups(2, X1, 4, last)
+            res[pl.ds(to, BY), :] = jnp.where(mask, even[k], new[k])
+            res[pl.ds(to + BY, BY), :] = jnp.where(mask, new[k], even[k])
+
+    copies = []
+    for g in range(X1 // 4):
+        last(2 + 4 * g)
+        part = pl.ds(g * 8 * BY, 8 * BY)
+        copies.append(pltpu.make_async_copy(res.at[part], result.at[part], sems.at[g]))
+        copies[-1].start()
+    for copy in copies:
+        copy.wait()
 
 
 def swap(pair, axis):
@@ -892,7 +902,10 @@
             pltpu.VMEM(mid, F32),
             pltpu.VMEM(ext, F32),
             pltpu.VMEM((BX // 2 * 8, NL), F32),
+            pltpu.VMEM((BX * BY, NL), F32),
+            pltpu.SemaphoreType.DMA((X1 // 4,)),
         ],
+        out_specs=pl.BlockSpec(memory_space=pltpu.HBM),
         compiler_params=pltpu.CompilerParams(vmem_limit_bytes=24 << 20),
         name="finish",
     )(*inputs)

time: 62.3 us -> 58.4 us (0.937)
  Pallas kernels: 13.7 us -> 9.83 us
    pallas_call x1, Pallas kernels: 3.54 us -> 2.05 us  [body(): call(mid_pre, (sds(*mid),) * 3 + (sds(*mid1),) + (sds(*mid),) * 5 + (sds(...]
    pallas_call x1, Pallas kernels: 3.72 us -> 2.45 us  [body(): call(fine_pre, (sds(*ext),) * 2 + (sds(*one),) + (sds(*ext),) * 8 + (sds(...]
    pallas_call x1, Pallas kernels: 4.55 us -> 3.6 us  [body(): pl.pallas_call(finish_kernel(len(inputs), (gx, gy, wx, wy)), out_shape=sd...]
where the time goes in v6:
time: 58.4 us; the launch traced here: 57.5 us
  starting transfers between devices  26.4 us (45%)
  blocking collectives  14.6 us (25%)
  Pallas kernels  9.83 us (17%)
  waiting for transfers between devices  6.58 us (11%)
    ppermute x12, starting transfers between devices, swap(): got[first] = lax.ppermute(pair[first], axis, route)  26.4 us
    all_to_all x1, blocking collectives, body(): lax.all_to_all(message, ('gx', 'gy'), 0, 0).reshape(gx, gy, 16, NL)  14.6 us
    ppermute x12, waiting for transfers between devices, swap(): got[first] = lax.ppermute(pair[first], axis, route)  6.58 us
    pallas_call x1, Pallas kernels, body(): pl.pallas_call(finish_kernel(len(inputs), (gx, gy, wx, wy)), out_shape=sd...  3.6 us
    pallas_call x1, Pallas kernels, body(): call(fine_pre, (sds(*ext),) * 2 + (sds(*one),) + (sds(*ext),) * 8 + (sds(...  2.45 us
    pallas_call x1, Pallas kernels, body(): call(mid_pre, (sds(*mid),) * 3 + (sds(*mid1),) + (sds(*mid),) * 5 + (sds(...  2.05 us
    pallas_call x1, Pallas kernels, body(): call(pack_y, whole + (sds(8, NL),) + (sds(YROWS + 8, NL),) * 2 + (sds(12...  1.52 us
  transfers between devices with their start and end apart: 12, of which 3 were waited for; matrix products, arithmetic and copies ran while one was open for 0% of the time, Pallas kernels for 0%

profile of v6, /device:TPU:1, one launch (start us, length us, event | category | flops | bytes accessed | tf_op | source)
XLA Modules:
  0.0 57.5 jit_solution(9133895929361341993)
XLA Ops:
  0.0 1.5 %shard_map.55 = (f32[512,128]{1,0:T(8,128)S(1)}, f32[512,128]{1,0:T(8,128)S(1)}, f32[512,128]{1,0:T(8,128)S(1)}, f32[512,128]{1,0:T(8,128)S(1)}, s32[512,128]{1,...) custom-call(f32[512,128]{1,0:T(8,128)} %bitcast.8, ...), custom_call_target="tpu_custom_call" | custom-call | tf_op jit(solution)/shard_map/pallas_call | solution.py:839
  1.5 2.1 %collective-permute-start = (f32[328,128]{1,0:T(8,128)S(1)}, f32[328,128]{1,0:T(8,128)S(1)}, u32[]{:S(2)}, u32[]{:S(2)}) collective-permute-start(f32[328,128]{1,0:T(8,128)S(1)} %get-tuple-element.57), channel_id=1, source_target_pairs={{0,1},{1,0},{2,3},{3,2},{4,5},{5,4},{6,7},{7,6},{8,9},{9,8},{10,11... | collective-permute-start | bytes 503816 | tf_op jit(solution)/shard_map/ppermute | solution.py:829
  3.6 0.7 %collective-permute-start.1 = (f32[328,128]{1,0:T(8,128)S(1)}, f32[328,128]{1,0:T(8,128)S(1)}, u32[]{:S(2)}, u32[]{:S(2)}) collective-permute-start(f32[328,128]{1,0:T(8,128)S(1)} %get-tuple-element.58), channel_id=1, source_target_pairs={{1,2},{2,1},{3,4},{4,3},{5,6},{6,5},{9,10},{10,9},{11,12},{12,11},... | collective-permute-start | bytes 503816 | tf_op jit(solution)/shard_map/ppermute | solution.py:829
  4.3 1.0 %collective-permute-start.2 = (f32[192,128]{1,0:T(8,128)S(1)}, f32[192,128]{1,0:T(8,128)S(1)}, u32[]{:S(2)}, u32[]{:S(2)}) collective-permute-start(f32[192,128]{1,0:T(8,128)S(1)} %get-tuple-element.64), channel_id=1, source_target_pairs={{0,8},{8,0},{16,24},{24,16},{1,9},{9,1},{17,25},{25,17},{2,10},{10... | collective-permute-start | bytes 294920 | tf_op jit(solution)/shard_map/ppermute | solution.py:829
  5.3 3.0 %collective-permute-start.3 = (f32[192,128]{1,0:T(8,128)S(1)}, f32[192,128]{1,0:T(8,128)S(1)}, u32[]{:S(2)}, u32[]{:S(2)}) collective-permute-start(f32[192,128]{1,0:T(8,128)S(1)} %get-tuple-element.65), channel_id=1, source_target_pairs={{8,16},{16,8},{9,17},{17,9},{10,18},{18,10},{11,19},{19,11},{12,20... | collective-permute-start | bytes 294920 | tf_op jit(solution)/shard_map/ppermute | solution.py:829
  8.4 0.0 collective-permute-done.got0.goty0.refs_2_
  8.4 0.0 collective-permute-done.1.got1.goty1.refs_3_
  8.4 0.2 shard_map.56
  8.6 3.4 %collective-permute-start.4 = (f32[120,128]{1,0:T(8,128)S(1)}, f32[120,128]{1,0:T(8,128)S(1)}, u32[]{:S(2)}, u32[]{:S(2)}) collective-permute-start(f32[120,128]{1,0:T(8,128)S(1)} %get-tuple-element.66), channel_id=1, source_target_pairs={{0,8},{8,0},{16,24},{24,16},{1,9},{9,1},{17,25},{25,17},{2,10},{10... | collective-permute-start | bytes 184328 | tf_op jit(solution)/shard_map/ppermute | solution.py:829
  12.0 3.0 %collective-permute-start.5 = (f32[120,128]{1,0:T(8,128)S(1)}, f32[120,128]{1,0:T(8,128)S(1)}, u32[]{:S(2)}, u32[]{:S(2)}) collective-permute-start(f32[120,128]{1,0:T(8,128)S(1)} %get-tuple-element.67), channel_id=1, source_target_pairs={{8,16},{16,8},{9,17},{17,9},{10,18},{18,10},{11,19},{19,11},{12,20... | collective-permute-start | bytes 184328 | tf_op jit(solution)/shard_map/ppermute | solution.py:829
  15.1 0.0 collective-permute-done.2.xm0
  15.1 0.0 collective-permute-done.3.xm1
  15.1 0.0 collective-permute-done.4.got0.fx0.refs_4_
  15.1 2.4 %collective-permute-done.5.got1.fx1.refs_5_ = f32[120,128]{1,0:T(8,128)S(1)} collective-permute-done((f32[120,128]{1,0:T(8,128)S(1)}, f32[120,128]{1,0:T(8,128)S(1)}, u32[]{:S(2)}, u32[]{:S(2)}) %collective-permute-start.5) | collective-permute-done | bytes 61472 | tf_op jit(solution)/shard_map/ppermute | solution.py:829
  17.5 2.4 %shard_map.57 = (f32[2,20,24,128]{3,2,1,0:T(8,128)S(1)}, f32[2,20,24,128]{3,2,1,0:T(8,128)S(1)}, f32[20,24,128]{2,1,0:T(8,128)S(1)}, f32[2,20,24,128]{3,2,1,0:T(...) custom-call(f32[512,128]{1,0:T(8,128)S(1)} %get-tuple-element.51.pot, ...), custom_call_target="tpu_custom_call" | custom-call | tf_op jit(solution)/shard_map/pallas_call | solution.py:852
  20.0 0.7 %collective-permute-start.7 = (f32[216,128]{1,0:T(8,128)S(1)}, f32[216,128]{1,0:T(8,128)S(1)}, u32[]{:S(2)}, u32[]{:S(2)}) collective-permute-start(f32[216,128]{1,0:T(8,128)S(1)} %get-tuple-element.69), channel_id=1, source_target_pairs={{1,2},{2,1},{3,4},{4,3},{5,6},{6,5},{9,10},{10,9},{11,12},{12,11},... | collective-permute-start | bytes 331784 | tf_op jit(solution)/shard_map/ppermute | solution.py:829
  20.7 5.1 %collective-permute-start.6 = (f32[216,128]{1,0:T(8,128)S(1)}, f32[216,128]{1,0:T(8,128)S(1)}, u32[]{:S(2)}, u32[]{:S(2)}) collective-permute-start(f32[216,128]{1,0:T(8,128)S(1)} %get-tuple-element.68.m0), channel_id=1, source_target_pairs={{0,1},{1,0},{2,3},{3,2},{4,5},{5,4},{6,7},{7,6},{8,9},{9,8},{10,11... | collective-permute-start | bytes 331784 | tf_op jit(solution)/shard_map/ppermute | solution.py:829
  25.8 0.0 collective-permute-start.8
  25.8 3.6 %collective-permute-start.9 = (f32[112,128]{1,0:T(8,128)S(1)}, f32[112,128]{1,0:T(8,128)S(1)}, u32[]{:S(2)}, u32[]{:S(2)}) collective-permute-start(f32[112,128]{1,0:T(8,128)S(1)} %get-tuple-element.71), channel_id=1, source_target_pairs={{8,16},{16,8},{9,17},{17,9},{10,18},{18,10},{11,19},{19,11},{12,20... | collective-permute-start | bytes 172040 | tf_op jit(solution)/shard_map/ppermute | solution.py:829
  29.4 0.0 collective-permute-done.8._.xm0.refs_28_
  29.4 1.9 %collective-permute-done.9.__.xm1.refs_29_ = f32[112,128]{1,0:T(8,128)S(1)} collective-permute-done((f32[112,128]{1,0:T(8,128)S(1)}, f32[112,128]{1,0:T(8,128)S(1)}, u32[]{:S(2)}, u32[]{:S(2)}) %collective-permute-start.9) | collective-permute-done | bytes 57376 | tf_op jit(solution)/shard_map/ppermute | solution.py:829
  31.3 0.0 collective-permute-done.7.got1.gy1.refs_27_
  31.3 0.0 collective-permute-done.6.got0.gy0.refs_26_
  31.3 0.1 collective-permute-start.10
  31.4 3.6 %collective-permute-start.11 = (f32[184,128]{1,0:T(8,128)S(1)}, f32[184,128]{1,0:T(8,128)S(1)}, u32[]{:S(2)}, u32[]{:S(2)}) collective-permute-start(f32[184,128]{1,0:T(8,128)S(1)} %get-tuple-element.73), channel_id=1, source_target_pairs={{8,16},{16,8},{9,17},{17,9},{10,18},{18,10},{11,19},{19,11},{12,20... | collective-permute-start | bytes 282632 | tf_op jit(solution)/shard_map/ppermute | solution.py:829
  35.0 0.0 collective-permute-done.10.gx0.refs_30_
  35.1 2.3 %collective-permute-done.11.gx1.refs_31_ = f32[184,128]{1,0:T(8,128)S(1)} collective-permute-done((f32[184,128]{1,0:T(8,128)S(1)}, f32[184,128]{1,0:T(8,128)S(1)}, u32[]{:S(2)}, u32[]{:S(2)}) %collective-permute-start.11) | collective-permute-done | bytes 94240 | tf_op jit(solution)/shard_map/ppermute | solution.py:829
  37.3 2.0 %shard_map.59 = (f32[2,18,24,128]{3,2,1,0:T(8,128)S(1)}, f32[2,18,24,128]{3,2,1,0:T(8,128)S(1)}, f32[2,18,24,128]{3,2,1,0:T(8,128)S(1)}, f32[18,24,128]{2,1,0:T(...) custom-call(f32[216,128]{1,0:T(8,128)S(1)} %get-tuple-element.68.m0,, ...), custom_call_target="tpu_custom_call" | custom-call | tf_op jit(solution)/shard_map/pallas_call | solution.py:871
  39.4 14.6 %all_to_all.5 = f32[32,16,128]{2,1,0:T(8,128)S(1)} all-to-all(f32[32,16,128]{2,1,0:T(8,128)S(1)} %get-tuple-element.76), channel_id=1, replica_groups=mesh['gx'=4,'gy'=8] {'gx','gy'}, dimensions={0} | all-to-all | bytes 524288 | tf_op jit(solution)/shard_map/all_to_all | solution.py:884
  53.9 3.6 %finish.1 = f32[512,128]{1,0:T(8,128)} custom-call(f32[4,8,16,128]{3,2,1,0:T(8,128)S(1)} %bitcast.7, f32[8,128]{1,0:T(8,128)S(1)} %get-tuple-element.56.p2.refs_1_, f32[328,128]{1,0:T(8,128)S(1)} %collective-permute-done.got0.goty0.refs_2_, f32[328,128]{1,0:T(8,128)S(1)} %collective-permute-done.1.got1.goty1.refs_3_, ...), custom_call_target="tpu_custom_call" | custom-call | tf_op jit(solution)/shard_map/finish/pallas_call | solution.py:891
  (1 shorter events, 0.0 us)
Async XLA Ops:
  1.5 6.8 %collective-permute-start = (f32[328,128]{1,0:T(8,128)S(1)}, f32[328,128]{1,0:T(8,128)S(1)}, u32[]{:S(2)}, u32[]{:S(2)}) collective-permute-start(f32[328,128]{1,0:T(8,128)S(1)} %get-tuple-element.57), channel_id=1, source_target_pairs={{0,1},{1,0},{2,3},{3,2},{4,5},{5,4},{6,7},{7,6},{8,9},{9,8},{10,11... | collective-permute-start | bytes 503816 | tf_op jit(solution)/shard_map/ppermute | solution.py:829
  3.6 4.8 %collective-permute-start.1 = (f32[328,128]{1,0:T(8,128)S(1)}, f32[328,128]{1,0:T(8,128)S(1)}, u32[]{:S(2)}, u32[]{:S(2)}) collective-permute-start(f32[328,128]{1,0:T(8,128)S(1)} %get-tuple-element.58), channel_id=1, source_target_pairs={{1,2},{2,1},{3,4},{4,3},{5,6},{6,5},{9,10},{10,9},{11,12},{12,11},... | collective-permute-start | bytes 503816 | tf_op jit(solution)/shard_map/ppermute | solution.py:829
  4.3 10.8 %collective-permute-start.2 = (f32[192,128]{1,0:T(8,128)S(1)}, f32[192,128]{1,0:T(8,128)S(1)}, u32[]{:S(2)}, u32[]{:S(2)}) collective-permute-start(f32[192,128]{1,0:T(8,128)S(1)} %get-tuple-element.64), channel_id=1, source_target_pairs={{0,8},{8,0},{16,24},{24,16},{1,9},{9,1},{17,25},{25,17},{2,10},{10... | collective-permute-start | bytes 294920 | tf_op jit(solution)/shard_map/ppermute | solution.py:829
  5.3 9.8 %collective-permute-start.3 = (f32[192,128]{1,0:T(8,128)S(1)}, f32[192,128]{1,0:T(8,128)S(1)}, u32[]{:S(2)}, u32[]{:S(2)}) collective-permute-start(f32[192,128]{1,0:T(8,128)S(1)} %get-tuple-element.65), channel_id=1, source_target_pairs={{8,16},{16,8},{9,17},{17,9},{10,18},{18,10},{11,19},{19,11},{12,20... | collective-permute-start | bytes 294920 | tf_op jit(solution)/shard_map/ppermute | solution.py:829
  8.6 6.5 %collective-permute-start.4 = (f32[120,128]{1,0:T(8,128)S(1)}, f32[120,128]{1,0:T(8,128)S(1)}, u32[]{:S(2)}, u32[]{:S(2)}) collective-permute-start(f32[120,128]{1,0:T(8,128)S(1)} %get-tuple-element.66), channel_id=1, source_target_pairs={{0,8},{8,0},{16,24},{24,16},{1,9},{9,1},{17,25},{25,17},{2,10},{10... | collective-permute-start | bytes 184328 | tf_op jit(solution)/shard_map/ppermute | solution.py:829
  12.0 5.5 %collective-permute-start.5 = (f32[120,128]{1,0:T(8,128)S(1)}, f32[120,128]{1,0:T(8,128)S(1)}, u32[]{:S(2)}, u32[]{:S(2)}) collective-permute-start(f32[120,128]{1,0:T(8,128)S(1)} %get-tuple-element.67), channel_id=1, source_target_pairs={{8,16},{16,8},{9,17},{17,9},{10,18},{18,10},{11,19},{19,11},{12,20... | collective-permute-start | bytes 184328 | tf_op jit(solution)/shard_map/ppermute | solution.py:829
  20.0 11.3 %collective-permute-start.7 = (f32[216,128]{1,0:T(8,128)S(1)}, f32[216,128]{1,0:T(8,128)S(1)}, u32[]{:S(2)}, u32[]{:S(2)}) collective-permute-start(f32[216,128]{1,0:T(8,128)S(1)} %get-tuple-element.69), channel_id=1, source_target_pairs={{1,2},{2,1},{3,4},{4,3},{5,6},{6,5},{9,10},{10,9},{11,12},{12,11},... | collective-permute-start | bytes 331784 | tf_op jit(solution)/shard_map/ppermute | solution.py:829
  20.7 10.6 %collective-permute-start.6 = (f32[216,128]{1,0:T(8,128)S(1)}, f32[216,128]{1,0:T(8,128)S(1)}, u32[]{:S(2)}, u32[]{:S(2)}) collective-permute-start(f32[216,128]{1,0:T(8,128)S(1)} %get-tuple-element.68.m0), channel_id=1, source_target_pairs={{0,1},{1,0},{2,3},{3,2},{4,5},{5,4},{6,7},{7,6},{8,9},{9,8},{10,11... | collective-permute-start | bytes 331784 | tf_op jit(solution)/shard_map/ppermute | solution.py:829
  25.8 3.6 %collective-permute-start.8 = (f32[112,128]{1,0:T(8,128)S(1)}, f32[112,128]{1,0:T(8,128)S(1)}, u32[]{:S(2)}, u32[]{:S(2)}) collective-permute-start(f32[112,128]{1,0:T(8,128)S(1)} %get-tuple-element.70), channel_id=1, source_target_pairs={{0,8},{8,0},{16,24},{24,16},{1,9},{9,1},{17,25},{25,17},{2,10},{10... | collective-permute-start | bytes 172040 | tf_op jit(solution)/shard_map/ppermute | solution.py:829
  25.8 5.5 %collective-permute-start.9 = (f32[112,128]{1,0:T(8,128)S(1)}, f32[112,128]{1,0:T(8,128)S(1)}, u32[]{:S(2)}, u32[]{:S(2)}) collective-permute-start(f32[112,128]{1,0:T(8,128)S(1)} %get-tuple-element.71), channel_id=1, source_target_pairs={{8,16},{16,8},{9,17},{17,9},{10,18},{18,10},{11,19},{19,11},{12,20... | collective-permute-start | bytes 172040 | tf_op jit(solution)/shard_map/ppermute | solution.py:829
  31.3 3.7 %collective-permute-start.10 = (f32[184,128]{1,0:T(8,128)S(1)}, f32[184,128]{1,0:T(8,128)S(1)}, u32[]{:S(2)}, u32[]{:S(2)}) collective-permute-start(f32[184,128]{1,0:T(8,128)S(1)} %get-tuple-element.72), channel_id=1, source_target_pairs={{0,8},{8,0},{16,24},{24,16},{1,9},{9,1},{17,25},{25,17},{2,10},{10... | collective-permute-start | bytes 282632 | tf_op jit(solution)/shard_map/ppermute | solution.py:829
  31.4 5.9 %collective-permute-start.11 = (f32[184,128]{1,0:T(8,128)S(1)}, f32[184,128]{1,0:T(8,128)S(1)}, u32[]{:S(2)}, u32[]{:S(2)}) collective-permute-start(f32[184,128]{1,0:T(8,128)S(1)} %get-tuple-element.73), channel_id=1, source_target_pairs={{8,16},{16,8},{9,17},{17,9},{10,18},{18,10},{11,19},{19,11},{12,20... | collective-permute-start | bytes 282632 | tf_op jit(solution)/shard_map/ppermute | solution.py:829
